TPU v7x, 32 devices: a whole 2x2x4 slice. The times are simulated.
32 devices in a mesh: rep: 8 (over z, x), grp: 4 (over y, core).
Axes of the slice: x: 2, y: 2, z: 4, core: 2. Of those that a mesh axis runs over, the one named last changes fastest.
Arguments:
- images: bfloat16 [32, 14, 14, 512], P(('rep', 'grp')), may hold values from -45 to 45
- cotangent: bfloat16 [32, 14, 14, 512], P(('rep', 'grp')), may hold values from -6 to 6
- region_ids: int32 [14, 14], replicated, may hold values from 0 to 8, as said below
- rel_index: int32 [169], replicated, may hold values from 0 to 168, each once
- matrices: float32 [3145728], P(('rep', 'grp')), may hold values from -0.8838835 to 0.8838835
- matrix_m: float32 [3145728], P(('rep', 'grp')), may hold values from -0.75 to 0.75
- matrix_v: float32 [3145728], P(('rep', 'grp')), may hold values from 2e-05 to 0.0005
- small: float32 [8848], replicated, may hold values from -4 to 301.5
- small_m: float32 [8848], replicated, may hold values from -0.75 to 0.75
- small_v: float32 [8848], replicated, may hold values from 2e-05 to 0.0005
Outputs:
- output: bfloat16 [32, 14, 14, 512], P(('rep', 'grp'))
- input_grad: bfloat16 [32, 14, 14, 512], P(('rep', 'grp'))
- matrix_grad: float32 [3145728], P(('rep', 'grp'))
- small_grad: float32 [8848], replicated
- new_matrices: float32 [3145728], P(('rep', 'grp'))
- new_matrix_m: float32 [3145728], P(('rep', 'grp'))
- new_matrix_v: float32 [3145728], P(('rep', 'grp'))
- new_small: float32 [8848], replicated
- new_small_m: float32 [8848], replicated
- new_small_v: float32 [8848], replicated
Inputs may be any that keep to these rules, and one draw needn't show every extreme that they name: `region_ids`: 3 times a row band plus a column band; each dimension is cut into three nonempty bands. `rel_index`: a permutation of the table's rows.
All inputs are finite; a program needn't handle non-finite values.
Results may differ from a plain program's by a relative error of at most 0.01.
The roundings to bfloat16 on the way count: a program that leaves them out, or rounds other values in their place, can miss the bound.
Values may be sent and summed in bfloat16 or wider, within the bound.
No kernel may reach another device: no remote copies, remote signals or barrier semaphores. Data moves between devices by JAX's collectives and lax.ppermute only.
A program may use at most 128 MiB of HBM per device.

v0:
```python
import math

import jax
import jax.numpy as jnp
import numpy as np
from jax import lax
from jax.experimental import pallas as pl
from jax.experimental.pallas import tpu as pltpu
from jax.sharding import PartitionSpec as P


D = 512
HEADS = 16
FF = 2048
WIN = 7
SIDE = 14
SHIFT = 3
STEP = 5
HEAD_DIM = 32
REL = 169

norm_eps = 1e-05
beta_one = 0.9
beta_two = 0.999
adam_eps = 1e-08
rate_matrix = 0.01
rate_small = 0.2
decay_rate = 0.05
masked_score = -1e30
root_half = 0.7071067811865476
inv_root_twopi = 0.3989422804014327
highest = lax.Precision.HIGHEST
score_scale = HEAD_DIM ** (-0.5)

PLACES = WIN * WIN
PAD = 64
WINDOWS = (SIDE // WIN) ** 2
ROWS = WINDOWS * PAD
STRIP = 16
FLAT = SIDE * STRIP
GROUP = 4
GROUPS = HEADS // GROUP
LANES = GROUP * HEAD_DIM
WIDE = GROUP * PAD

PIECE = 64
UP_ROWS = PIECE // (FF // D)
BLOCKS = (3 * D * D + D * D + 2 * D * FF) // (PIECE * D)
QKV_END = 3 * D // PIECE
PROJ_END = QKV_END + D // PIECE
UP_END = PROJ_END + FF // PIECE
KINDS = 4 + 2 * (FF // D)
SMALL_ROWS = 8 + FF // D
f32 = jnp.float32
bf16 = jnp.bfloat16


def window_source():
    source = np.full((ROWS,), -1, np.int64)
    blocks = SIDE // WIN
    for window in range(WINDOWS):
        for place in range(PLACES):
            row = (window // blocks * WIN + place // WIN + SHIFT) % SIDE
            col = (window % blocks * WIN + place % WIN + SHIFT) % SIDE
            source[window * PAD + place] = row * STRIP + col
    return source


def permutation():
    return (window_source()[:, None] == np.arange(FLAT)[None, :]).astype(np.float32)


def dot(a, b):
    return lax.dot_general(a, b, (((1,), (0,)), ((), ())), preferred_element_type=f32)


def dot_t(a, b):
    return lax.dot_general(a, b, (((1,), (1,)), ((), ())), preferred_element_type=f32)


def t_dot(a, b):
    return lax.dot_general(a, b, (((0,), (0,)), ((), ())), preferred_element_type=f32)


def norm_stats(values):
    center = values - jnp.mean(values, axis=-1, keepdims=True)
    spread = jnp.mean(center * center, axis=-1, keepdims=True)
    scaling = lax.rsqrt(spread + norm_eps)
    return center * scaling, scaling


def norm_back(incoming, normed, scaling, gain_vector):
    scaled = incoming * gain_vector
    return scaling * (
        scaled
        - jnp.mean(scaled, axis=-1, keepdims=True)
        - normed * jnp.mean(scaled * normed, axis=-1, keepdims=True)
    )


def col_sum(values):
    return jnp.sum(values, axis=0, keepdims=True)


def layer_kernel(counts, out_counts):
    n_in = len(counts)
    n_out = len(out_counts)

    def body(*refs):
        slots, out_slots = refs[0], refs[1]
        img, cot, perm, small, bias, mask = refs[2:8]
        pieces = refs[8 : 8 + n_in]
        refs = refs[8 + n_in :]
        out, in_grad, sums, rel_sum = refs[:4]
        grads = refs[4 : 4 + n_out]
        (
            weights,
            wgrad,
            flat,
            xw,
            cw,
            in_one,
            qkv,
            att,
            att_low,
            mixed,
            resid,
            in_two,
            act,
            acc,
            acc_two,
            pre,
            gres,
            grow,
            mgrad,
            dqkv,
            ext,
            sem,
            sem_out,
        ) = refs[4 + n_out :]

        def place(third, make, make_up):
            @pl.when(third < QKV_END)
            def _():
                make(lax.rem(third, 3), lax.div(third, 3) * PIECE)

            @pl.when((third >= QKV_END) & (third < PROJ_END))
            def _():
                make(3, (third - QKV_END) * PIECE)

            @pl.when((third >= PROJ_END) & (third < UP_END))
            def _():
                make_up((third - PROJ_END) * UP_ROWS)

            @pl.when(third >= UP_END)
            def _():
                at = third - UP_END
                make(4 + FF // D + lax.div(at, D // PIECE), lax.rem(at, D // PIECE) * PIECE)

        base = 0
        for number, count in enumerate(counts):

            def fetch(slot, carry, number=number, base=base):
                source = pieces[number].at[slot]

                def make(block, row):
                    row = pl.multiple_of(row, PIECE)
                    pltpu.make_async_copy(source, weights.at[block, pl.ds(row, PIECE)], sem).start()

                def make_up(row):
                    row = pl.multiple_of(row, UP_ROWS)
                    for j in range(FF // D):
                        pltpu.make_async_copy(
                            source.at[pl.ds(j * UP_ROWS, UP_ROWS)],
                            weights.at[4 + j, pl.ds(row, UP_ROWS)],
                            sem,
                        ).start()

                place(slots[base + slot], make, make_up)
                return carry

            lax.fori_loop(0, count, fetch, 0)
            base += count

        gain_one, gain_two, shift_one, bias_query, bias_value, bias_proj, shift_two, bias_down = (
            small[number : number + 1, :] for number in range(8)
        )

        flat[...] = jnp.zeros_like(flat)
        for row in range(SIDE):
            flat[row * STRIP : row * STRIP + SIDE, :] = img[0, row]
        xw[...] = dot(perm[...], flat[...])
        for row in range(SIDE):
            flat[row * STRIP : row * STRIP + SIDE, :] = cot[0, row]
        cw[...] = dot(perm[...], flat[...]).astype(bf16)

        def rows_of(number, size):
            return pl.ds(pl.multiple_of(number * size, size), size)

        def norm_one(number, carry):
            at = rows_of(number, PAD)
            normed, _ = norm_stats(xw[at, :])
            in_one[at, :] = (normed * gain_one + shift_one).astype(bf16)
            return carry

        lax.fori_loop(0, WINDOWS, norm_one, 0)

        for window in range(WINDOWS):
            allowed = mask[window] != 0
            for group in range(GROUPS):
                ext[window, group] = jnp.where(
                    allowed, bias[:, group * WIDE : (group + 1) * WIDE], masked_score
                )
        head_mask = (
            lax.broadcasted_iota(jnp.int32, (WIDE, LANES), 0) // PAD
            == lax.broadcasted_iota(jnp.int32, (WIDE, LANES), 1) // HEAD_DIM
        )

        def spread_heads(values):
            return jnp.where(head_mask, jnp.concatenate([values] * GROUP, axis=0), 0)

        def join_heads(values):
            kept = jnp.where(head_mask, values, 0.0)
            total = kept[:PAD]
            for head in range(1, GROUP):
                total = total + kept[head * PAD : (head + 1) * PAD]
            return total

        pltpu.make_async_copy(weights, weights, sem).wait()

        for part, vector in enumerate((bias_query, None, bias_value)):
            product = dot(in_one[...], weights[part])
            if vector is not None:
                product = product + vector
            qkv[part] = product.astype(bf16)

        def attend(window, carry):
            at = rows_of(window, PAD)
            for group in range(GROUPS):
                lanes = slice(group * LANES, (group + 1) * LANES)
                scores = dot_t(qkv[1, at, lanes], spread_heads(qkv[0, at, lanes]))
                masked = score_scale * scores + ext[window, group]
                top = jnp.max(masked, axis=0, keepdims=True)
                raised = jnp.exp(masked - top)
                attention = raised * (1.0 / col_sum(raised))
                low = attention.astype(bf16)
                att[window, group] = attention
                att_low[window, group] = low
                mixed[at, lanes] = join_heads(t_dot(low, qkv[2, at, lanes])).astype(bf16)
            return carry

        lax.fori_loop(0, WINDOWS, attend, 0)

        resid[...] = xw[...] + (dot(mixed[...], weights[3]) + bias_proj)

        def norm_two(number, carry):
            at = rows_of(number, PAD)
            normed, _ = norm_stats(resid[at, :])
            in_two[at, :] = (normed * gain_two + shift_two).astype(bf16)
            return carry

        lax.fori_loop(0, WINDOWS, norm_two, 0)

        def feed(j, carry):
            up = weights.at[4 + j]
            down = weights.at[4 + FF // D + j]
            acc_two[...] = dot(in_two[...], up[...]) + small[pl.ds(8 + j, 1), :]
            pre[...] = dot_t(cw[...], down[...])

            def gelu_part(number, total):
                at = rows_of(number, 32)
                value = acc_two[at, :]
                phi = 0.5 * (1.0 + lax.erf(value * root_half))
                act[at, :] = (value * phi).astype(bf16)
                slope = phi + value * jnp.exp(-0.5 * value * value) * inv_root_twopi
                back = pre[at, :] * slope
                grow[at, :] = back.astype(bf16)
                return total + col_sum(back)

            sums[pl.ds(8 + j, 1), :] = lax.fori_loop(
                0, ROWS // 32, gelu_part, jnp.zeros((1, D), f32)
            )
            forward = dot(act[...], down[...])
            backward = dot_t(grow[...], up[...])

            @pl.when(j == 0)
            def _():
                acc[...] = forward
                gres[...] = backward

            @pl.when(j > 0)
            def _():
                acc[...] += forward
                gres[...] += backward

            wgrad[4 + j] = t_dot(in_two[...], grow[...]).astype(bf16)
            wgrad[4 + FF // D + j] = t_dot(act[...], cw[...]).astype(bf16)
            return carry

        lax.fori_loop(0, FF // D, feed, 0)

        def second_back(number, carry):
            gain_sum, shift_sum, resid_sum, cot_sum = carry
            at = rows_of(number, 32)
            value = resid[at, :]
            normed, scaling = norm_stats(value)
            act[at, :] = (value + (acc[at, :] + bias_down)).astype(bf16)
            incoming = gres[at, :]
            back = norm_back(incoming, normed, scaling, gain_two)
            cotangent = cw[at, :].astype(f32)
            total = cotangent + back
            gres[at, :] = total
            grow[at, :] = total.astype(bf16)
            return (
                gain_sum + col_sum(incoming * normed),
                shift_sum + col_sum(incoming),
                resid_sum + col_sum(total),
                cot_sum + col_sum(cotangent),
            )

        zero_row = jnp.zeros((1, D), f32)
        sums[1:2, :], sums[6:7, :], sums[5:6, :], sums[7:8, :] = lax.fori_loop(
            0, ROWS // 32, second_back, (zero_row,) * 4
        )
        result = t_dot(perm[...], act[...]).astype(bf16)
        for row in range(SIDE):
            out[0, row] = result[row * STRIP : row * STRIP + SIDE, :]

        wgrad[3] = t_dot(mixed[...], grow[...]).astype(bf16)
        mgrad[...] = dot_t(grow[...], weights[3]).astype(bf16)
        sums[3:4, :] = zero_row
        sums[4:5, :] = zero_row
        rel_sum[...] = jnp.zeros_like(rel_sum)

        def attend_back(window, carry):
            at = rows_of(window, PAD)
            for group in range(GROUPS):
                lanes = slice(group * LANES, (group + 1) * LANES)
                wide = slice(group * WIDE, (group + 1) * WIDE)
                mixed_blk = spread_heads(mgrad[at, lanes])
                query_blk = spread_heads(qkv[0, at, lanes])
                prob = dot_t(qkv[2, at, lanes], mixed_blk)
                attention = att[window, group]
                score = attention * (prob - col_sum(attention * prob))
                rel_sum[:, wide] += score
                low = score.astype(bf16)
                value_grad = dot(att_low[window, group], mixed_blk)
                key_grad = score_scale * dot(low, query_blk)
                query_grad = score_scale * join_heads(t_dot(low, qkv[1, at, lanes]))
                sums[3:4, lanes] += col_sum(query_grad)
                sums[4:5, lanes] += col_sum(value_grad)
                dqkv[0, at, lanes] = query_grad.astype(bf16)
                dqkv[1, at, lanes] = key_grad.astype(bf16)
                dqkv[2, at, lanes] = value_grad.astype(bf16)
            return carry

        lax.fori_loop(0, WINDOWS, attend_back, 0)

        for part in range(3):
            wgrad[part] = t_dot(in_one[...], dqkv[part]).astype(bf16)

        base = 0
        for number, count in enumerate(out_counts):

            def store(slot, carry, number=number, base=base):
                target = grads[number].at[slot]

                def make(block, row):
                    row = pl.multiple_of(row, PIECE)
                    pltpu.make_async_copy(
                        wgrad.at[block, pl.ds(row, PIECE)], target, sem_out
                    ).start()

                def make_up(row):
                    row = pl.multiple_of(row, UP_ROWS)
                    for j in range(FF // D):
                        pltpu.make_async_copy(
                            wgrad.at[4 + j, pl.ds(row, UP_ROWS)],
                            target.at[pl.ds(j * UP_ROWS, UP_ROWS)],
                            sem_out,
                        ).start()

                place(out_slots[base + slot], make, make_up)
                return carry

            lax.fori_loop(0, count, store, 0)
            base += count

        acc[...] = dot_t(dqkv[0], weights[0])
        acc[...] += dot_t(dqkv[1], weights[1])
        acc[...] += dot_t(dqkv[2], weights[2])

        def first_back(number, carry):
            gain_sum, shift_sum = carry
            at = rows_of(number, 32)
            normed, scaling = norm_stats(xw[at, :])
            incoming = acc[at, :]
            back = norm_back(incoming, normed, scaling, gain_one)
            act[at, :] = (gres[at, :] + back).astype(bf16)
            return gain_sum + col_sum(incoming * normed), shift_sum + col_sum(incoming)

        sums[0:1, :], sums[2:3, :] = lax.fori_loop(0, ROWS // 32, first_back, (zero_row,) * 2)
        result = t_dot(perm[...], act[...]).astype(bf16)
        for row in range(SIDE):
            in_grad[0, row] = result[row * STRIP : row * STRIP + SIDE, :]
        pltpu.make_async_copy(wgrad, wgrad, sem_out).wait()

    return body


def run_layer(images, cotangent, small, bias, mask, slots, out_slots, pieces, outs):
    perm = jnp.asarray(permutation(), bf16)
    vmem = pl.BlockSpec(memory_space=pltpu.VMEM)
    smem = pl.BlockSpec(memory_space=pltpu.SMEM)
    hbm = pl.BlockSpec(memory_space=pl.ANY)
    counts = [piece.shape[0] for piece in pieces]
    image_shape = (1, SIDE, SIDE, D)
    return pl.pallas_call(
        layer_kernel(counts, outs),
        in_specs=[smem, smem] + [vmem] * 6 + [hbm] * len(counts),
        out_specs=[vmem] * 4 + [hbm] * len(outs),
        out_shape=[
            jax.ShapeDtypeStruct(image_shape, bf16),
            jax.ShapeDtypeStruct(image_shape, bf16),
            jax.ShapeDtypeStruct((SMALL_ROWS, D), f32),
            jax.ShapeDtypeStruct((PAD, HEADS * PAD), f32),
        ]
        + [jax.ShapeDtypeStruct((count, PIECE, D), bf16) for count in outs],
        scratch_shapes=[
            pltpu.VMEM((KINDS, D, D), bf16),
            pltpu.VMEM((KINDS, D, D), bf16),
            pltpu.VMEM((FLAT, D), bf16),
            pltpu.VMEM((ROWS, D), f32),
            pltpu.VMEM((ROWS, D), bf16),
            pltpu.VMEM((ROWS, D), bf16),
            pltpu.VMEM((3, ROWS, D), bf16),
            pltpu.VMEM((WINDOWS, GROUPS, PAD, WIDE), f32),
            pltpu.VMEM((WINDOWS, GROUPS, PAD, WIDE), bf16),
            pltpu.VMEM((ROWS, D), bf16),
            pltpu.VMEM((ROWS, D), f32),
            pltpu.VMEM((ROWS, D), bf16),
            pltpu.VMEM((ROWS, D), bf16),
            pltpu.VMEM((ROWS, D), f32),
            pltpu.VMEM((ROWS, D), f32),
            pltpu.VMEM((ROWS, D), f32),
            pltpu.VMEM((ROWS, D), f32),
            pltpu.VMEM((ROWS, D), bf16),
            pltpu.VMEM((ROWS, D), bf16),
            pltpu.VMEM((3, ROWS, D), bf16),
            pltpu.VMEM((WINDOWS, GROUPS, PAD, WIDE), f32),
            pltpu.SemaphoreType.DMA,
            pltpu.SemaphoreType.DMA,
        ],
        name="layer",
    )(slots, out_slots, images, cotangent, perm, small, bias, mask, *pieces)


VIEW = PIECE * D * 3 // 128


def shard_kinds(device):
    third = 3 * device + jnp.arange(3, dtype=jnp.int32)
    is_up = (third >= PROJ_END) & (third < UP_END)
    return jnp.where(third < QKV_END, 0, jnp.where(is_up, 2, 1)).astype(jnp.int32)


def piece_rows(kind, part):
    per_row = D // 128
    if kind == 0:
        return [(slice(0, PIECE), per_row * part, 3 * per_row)]
    if kind == 1:
        return [(slice(0, PIECE), per_row * PIECE * part, per_row)]
    return [
        (slice(j * UP_ROWS, (j + 1) * UP_ROWS), per_row * (PIECE * part + j), per_row * (FF // D))
        for j in range(FF // D)
    ]


def pack_kernel(kinds, shard, out):
    for part in range(3):
        for kind in range(3):

            @pl.when(kinds[part] == kind)
            def _(part=part, kind=kind):
                for rows, start, stride in piece_rows(kind, part):
                    size = rows.stop - rows.start
                    for lane in range(D // 128):
                        lanes = slice(lane * 128, (lane + 1) * 128)
                        value = shard[pl.ds(start + lane, size, stride=stride), :].astype(bf16)
                        out[part, rows, lanes] = value


def pack_shard(shard, kinds):
    vmem = pl.BlockSpec(memory_space=pltpu.VMEM)
    return pl.pallas_call(
        pack_kernel,
        in_specs=[pl.BlockSpec(memory_space=pltpu.SMEM), vmem],
        out_specs=vmem,
        out_shape=jax.ShapeDtypeStruct((3, PIECE, D), bf16),
        name="pack",
    )(kinds, shard.reshape(VIEW, 128))


def adam_step(weights, first_moment, second_moment, gradient, rate, decay):
    new_first = beta_one * first_moment + (1.0 - beta_one) * gradient
    new_second = beta_two * second_moment + (1.0 - beta_two) * gradient * gradient
    first_hat = new_first / (1.0 - beta_one**STEP)
    second_hat = new_second / (1.0 - beta_two**STEP)
    update = first_hat / (jnp.sqrt(second_hat) + adam_eps) + decay * weights
    return (weights - rate * update, new_first, new_second)


def adam_kernel(grad_scale):
    def body(kinds, *refs):
        mine, theirs, weights, first, second = refs[:5]
        grad, new_weights, new_first, new_second = refs[5:9]
        for part in range(3):
            for kind in range(3):

                @pl.when(kinds[part] == kind)
                def _(part=part, kind=kind):
                    for rows, start, stride in piece_rows(kind, part):
                        size = rows.stop - rows.start
                        for lane in range(D // 128):
                            lanes = slice(lane * 128, (lane + 1) * 128)
                            total = mine[part, rows, lanes].astype(f32) + theirs[
                                part, rows, lanes
                            ].astype(f32)
                            grad[pl.ds(start + lane, size, stride=stride), :] = total * grad_scale

        def step(number, carry):
            at = pl.ds(pl.multiple_of(number * 64, 64), 64)
            new_weights[at, :], new_first[at, :], new_second[at, :] = adam_step(
                weights[at, :], first[at, :], second[at, :], grad[at, :], rate_matrix, decay_rate
            )
            return carry

        lax.fori_loop(0, VIEW // 64, step, 0)

    return body


def adam_shard(kinds, parts, weights, first, second, grad_scale):
    vmem = pl.BlockSpec(memory_space=pltpu.VMEM)
    size = weights.shape[0]
    results = pl.pallas_call(
        adam_kernel(grad_scale),
        in_specs=[pl.BlockSpec(memory_space=pltpu.SMEM)] + [vmem] * 5,
        out_specs=[vmem] * 4,
        out_shape=[jax.ShapeDtypeStruct((VIEW, 128), f32)] * 4,
        name="adam",
    )(kinds, *parts, *(array.reshape(VIEW, 128) for array in (weights, first, second)))
    return [result.reshape(size) for result in results]


def to_pieces(flat):
    q_end, p_end, u_end = QKV_END * PIECE * D, PROJ_END * PIECE * D, UP_END * PIECE * D
    qkv = flat[:q_end].reshape(-1, PIECE, 3, D).transpose(0, 2, 1, 3).reshape(-1, PIECE, D)
    proj = flat[q_end:p_end].reshape(-1, PIECE, D)
    up = flat[p_end:u_end].reshape(-1, UP_ROWS, FF // D, D).transpose(0, 2, 1, 3)
    down = flat[u_end:].reshape(-1, PIECE, D)
    return jnp.concatenate([qkv, proj, up.reshape(-1, PIECE, D), down])


def from_pieces(pieces):
    qkv = pieces[:QKV_END].reshape(-1, 3, PIECE, D).transpose(0, 2, 1, 3)
    up = pieces[PROJ_END:UP_END].reshape(-1, FF // D, UP_ROWS, D).transpose(0, 2, 1, 3)
    return jnp.concatenate(
        [
            qkv.reshape(-1),
            pieces[QKV_END:PROJ_END].reshape(-1),
            up.reshape(-1),
            pieces[UP_END:].reshape(-1),
        ]
    )


def offset_grid():
    spots = np.arange(PAD)
    rows_at = spots // WIN
    cols_at = spots % WIN
    grid = (rows_at[None, :] - rows_at[:, None] + WIN - 1) * (2 * WIN - 1) + (
        cols_at[None, :] - cols_at[:, None] + WIN - 1
    )
    real = (spots[:, None] < PLACES) & (spots[None, :] < PLACES)
    return np.where(real, grid, -1)


AXES = ("rep", "grp")


def on_device(
    images, cotangent, region_ids, rel_index, matrices, matrix_m, matrix_v, small, small_m, small_v
):
    devices = lax.axis_size("rep") * lax.axis_size("grp")
    me = lax.axis_index(AXES)
    bits = [1 << number for number in range(devices.bit_length() - 1)]
    exact = devices == sum(bits) + 1 and matrices.shape[0] == 3 * PIECE * D

    def swap(value, bit):
        return lax.ppermute(value, AXES, [(i, i ^ bit) for i in range(devices)])

    labels = jnp.arange(REL, dtype=jnp.int32)
    grid = jnp.asarray(offset_grid(), jnp.int32)

    def split(values):
        high = lax.reduce_precision(values, 8, 7)
        middle = lax.reduce_precision(values - high, 8, 7)
        low = values - high - middle
        return [part.astype(bf16) for part in (high, middle, low)]

    def tables(rel_index):
        select_offset = (grid[None] == labels[:, None, None]).astype(f32)
        select_row = (rel_index[:, None] == labels[None, :]).astype(f32)
        return select_offset, select_row

    def prepare(small, region_ids, rel_index):
        small_rows = small[: SMALL_ROWS * D].reshape(SMALL_ROWS, D)
        rel_table = small[SMALL_ROWS * D :].reshape(REL, HEADS)
        select_offset, select_row = tables(rel_index)
        table_rows = jnp.dot(select_row, rel_table, precision=highest)
        table_parts = jnp.concatenate(split(table_rows), axis=1)
        bias = jnp.einsum(
            "okq,oh->khq", select_offset.astype(bf16), table_parts, preferred_element_type=f32
        )
        bias = bias.reshape(PAD, 3, HEADS, PAD).sum(axis=1)
        blocks = SIDE // WIN
        regions = region_ids.reshape(blocks, WIN, blocks, WIN).transpose(0, 2, 1, 3)
        regions = regions.reshape(WINDOWS, PLACES)
        padded = ((0, 0), (0, PAD - PLACES))
        keys = jnp.pad(regions, padded, constant_values=-1)[:, :, None]
        queries = jnp.tile(jnp.pad(regions, padded, constant_values=-2), (1, GROUP))[:, None, :]
        mask = (keys == queries).astype(jnp.int32)
        return small_rows, bias.reshape(PAD, HEADS * PAD), mask

    if exact:
        core, inner, top = bits[0], bits[1:-1], bits[-1]
        orders = [inner[color:] + inner[:color] for color in range(3)]
        kinds = shard_kinds(me)
        packed = pack_shard(matrices, kinds)
        received = swap(packed, top)
        masks = [[0]] * 3 + [[top]] * 3
        for color in range(3):
            for step in range(1, len(inner)):
                for at in (color, 3 + color):
                    bit = orders[color][-step]
                    masks[at] = masks[at] + [mask ^ bit for mask in masks[at]]

        def slot_table(entries):
            table = jnp.asarray(entries, jnp.int32)
            return 3 * (me ^ table[:, 0]) + table[:, 1]

        out_entries = []
        for color in range(3):
            order = orders[color] + [top]
            half = [0]
            for bit in reversed(order[1:]):
                half = half + [mask ^ bit for mask in half]
            for extra in (order[0] ^ core, core, order[0], 0):
                out_entries += [(mask ^ extra, color) for mask in half]
        piece_entries = []
        for tree in range(2):
            for color in range(3):
                last = orders[color][0]
                for extra in (0, last, core, last ^ core):
                    piece_entries += [(mask ^ extra, color) for mask in masks[3 * tree + color]]
        operands = prepare(small, region_ids, rel_index)
        operands = (*operands, slot_table(piece_entries), slot_table(out_entries))
        received, operands = lax.optimization_barrier((received, operands))
        buffers = [tree[color : color + 1] for tree in (packed, received) for color in range(3)]
        for step, tree in ((1, 0), (1, 1), (2, 0), (2, 1)):
            for color in range(3):
                at = 3 * tree + color
                bit = orders[color][-step]
                own = buffers[at]
                other = swap(own, bit)
                buffers[at] = jnp.concatenate([own, other])

        pieces = []
        for tree in range(2):
            for color in range(3):
                buffer = buffers[3 * tree + color]
                far = swap(buffer, orders[color][0])
                pieces += [buffer, far, swap(buffer, core), swap(far, core)]
        outs = [devices // 4] * 12
    else:
        gathered = lax.all_gather(matrices.astype(bf16), AXES, axis=0, tiled=True)
        pieces = [to_pieces(gathered)]
        slots = jnp.arange(BLOCKS, dtype=jnp.int32)
        operands = (*prepare(small, region_ids, rel_index), slots, slots)
        outs = [BLOCKS]

    output, input_grad, sums, rel_sum, *grads = run_layer(
        images, cotangent, *operands, pieces, outs
    )

    tokens_all = images.shape[0] * devices * SIDE * SIDE
    grad_scale = 1.0 / math.sqrt(tokens_all)

    def small_sums(sums, rel_sum, rel_index):
        select_offset, select_row = tables(rel_index)
        rel_parts = jnp.concatenate(split(rel_sum.reshape(PAD, HEADS, PAD)), axis=1)
        rel_grad = jnp.einsum(
            "okq,khq->oh", select_offset.astype(bf16), rel_parts, preferred_element_type=f32
        )
        rel_grad = rel_grad.reshape(REL, 3, HEADS).sum(axis=1)
        table_grad = jnp.dot(select_row.T, rel_grad, precision=highest)
        return jnp.concatenate([sums.reshape(-1), table_grad.reshape(-1)]) * grad_scale

    if exact:

        def add(a, b):
            return (a.astype(f32) + b.astype(f32)).astype(bf16)

        from_far = [swap(grads[4 * color], core) for color in range(3)]
        from_near = [swap(grads[4 * color + 1], core) for color in range(3)]
        far = [add(grads[4 * color + 2], from_far[color]) for color in range(3)]
        small_grad = small_sums(sums, rel_sum, rel_index)
        near = [add(grads[4 * color + 3], from_near[color]) for color in range(3)]
        for stage in range(3):
            for color in range(3):
                received = swap(far[color], orders[color][stage])
                size = received.shape[0] // 2
                far[color] = add(near[color][size:], received[size:])
                near[color] = add(near[color][:size], received[:size])
        parts = [jnp.concatenate(near), swap(jnp.concatenate(far), top)]
        for bit in bits:
            small_grad = small_grad + swap(small_grad, bit)
        owned_grad, new_matrices, new_matrix_m, new_matrix_v = adam_shard(
            kinds, parts, matrices, matrix_m, matrix_v, grad_scale
        )
    else:
        flat_grad = from_pieces(grads[0].astype(f32)) * grad_scale
        owned_grad = lax.psum_scatter(flat_grad, AXES, scatter_dimension=0, tiled=True)
        new_matrices, new_matrix_m, new_matrix_v = adam_step(
            matrices, matrix_m, matrix_v, owned_grad, rate_matrix, decay_rate
        )
        small_grad = lax.psum(small_sums(sums, rel_sum, rel_index), AXES)
    new_small, new_small_m, new_small_v = adam_step(
        small, small_m, small_v, small_grad, rate_small, 0.0
    )
    return (
        output,
        input_grad,
        owned_grad,
        small_grad,
        new_matrices,
        new_matrix_m,
        new_matrix_v,
        new_small,
        new_small_m,
        new_small_v,
    )


def solution(mesh):
    tokens = P(AXES, None, None, None)
    shard = P(AXES)
    whole = P()

    return jax.shard_map(
        on_device,
        mesh=mesh,
        in_specs=(tokens, tokens, whole, whole, shard, shard, shard, whole, whole, whole),
        out_specs=(tokens, tokens, shard, whole, shard, shard, shard, whole, whole, whole),
        check_vma=False,
    )
```

profile of v0, /device:TPU:0, one launch (start us, length us, event | category | flops | bytes accessed | tf_op | source)
XLA Modules:
  0.0 155.6 jit_solution(8836231682161508716)
XLA Ops:
  1.3 1.8 %pack.1 = bf16[3,64,512]{2,1,0:T(8,128)(2,1)} custom-call(s32[3]{0:T(128)} %compare_select_fusion.kinds, f32[768,128]{1,0:T(8,128)} %bitcast.26), custom_call_target="tpu_custom_call" | custom-call | tf_op jit(solution)/shard_map/pack/pallas_call | solution.py:495
  3.1 4.2 %collective-permute-start = (bf16[3,64,512]{2,1,0:T(8,128)(2,1)}, bf16[3,64,512]{2,1,0:T(8,128)(2,1)S(1)}, u32[]{:S(2)}, u32[]{:S(2)}) collective-permute-start(bf16[3,64,512]{2,1,0:T(8,128)(2,1)} %pack.1), channel_id=1, source_target_pairs={{0,16},{1,17},{2,18},{3,19},{4,20},{5,21},{6,22},{7,23},{8,24},{9,... | collective-permute-start | bytes 589832 | tf_op jit(solution)/shard_map/ppermute | solution.py:601
  7.3 0.9 fusion.27
  8.2 1.6 %collective-permute-start.11 = (bf16[1,64,512]{2,1,0:T(8,128)(2,1)S(1)}, bf16[1,64,512]{2,1,0:T(8,128)(2,1)S(1)}, u32[]{:S(2)}, u32[]{:S(2)}) collective-permute-start(bf16[1,64,512]{2,1,0:T(8,128)(2,1)S(1)} %get-tuple-element.90), channel_id=1, source_target_pairs={{0,4},{1,5},{2,6},{3,7},{4,0},{5,1},{6,2},{7,3},{8,12},{9,13},{10,... | collective-permute-start | bytes 196616 | tf_op jit(solution)/shard_map/ppermute | solution.py:601
  9.7 1.4 collective-permute-start.6
  11.2 1.6 %collective-permute-start.1 = (bf16[1,64,512]{2,1,0:T(8,128)(2,1)S(1)}, bf16[1,64,512]{2,1,0:T(8,128)(2,1)S(1)}, u32[]{:S(2)}, u32[]{:S(2)}) collective-permute-start(bf16[1,64,512]{2,1,0:T(8,128)(2,1)S(1)} %get-tuple-element.92), channel_id=1, source_target_pairs={{0,8},{1,9},{2,10},{3,11},{4,12},{5,13},{6,14},{7,15},{8,0},{9,1},... | collective-permute-start | bytes 196616 | tf_op jit(solution)/shard_map/ppermute | solution.py:601
  12.7 0.7 slice.153
  13.5 0.8 reshape.104
  14.5 1.0 reduce-precision_convert_fusion.3
  15.5 0.8 compare_convert_fusion.refs_7_
  16.3 1.2 fusion.1
  18.8 0.9 reshape.103.refs_6_
  21.6 3.2 %collective-permute-done.2 = bf16[2,64,512]{2,1,0:T(8,128)(2,1)S(1)} collective-permute-done((bf16[2,64,512]{2,1,0:T(8,128)(2,1)S(1)}, bf16[2,64,512]{2,1,0:T(8,128)(2,1)S(1)}, u32[]{:S(2)}, u32[]{:S(2)}) %collective-permute-start.2) | collective-permute-done | bytes 131104 | tf_op jit(solution)/shard_map/ppermute | solution.py:601
  26.2 1.4 collective-permute-start.26
  27.6 2.2 %collective-permute-done.16 = bf16[1,64,512]{2,1,0:T(8,128)(2,1)S(1)} collective-permute-done((bf16[1,64,512]{2,1,0:T(8,128)(2,1)S(1)}, bf16[1,64,512]{2,1,0:T(8,128)(2,1)S(1)}, u32[]{:S(2)}, u32[]{:S(2)}) %collective-permute-start.16) | collective-permute-done | bytes 65568 | tf_op jit(solution)/shard_map/ppermute | solution.py:601
  29.8 1.5 collective-permute-start.21
  31.4 3.7 %collective-permute-done.21 = bf16[1,64,512]{2,1,0:T(8,128)(2,1)S(1)} collective-permute-done((bf16[1,64,512]{2,1,0:T(8,128)(2,1)S(1)}, bf16[1,64,512]{2,1,0:T(8,128)(2,1)S(1)}, u32[]{:S(2)}, u32[]{:S(2)}) %collective-permute-start.21) | collective-permute-done | bytes 65568 | tf_op jit(solution)/shard_map/ppermute | solution.py:601
  36.4 3.6 %collective-permute-done.17 = bf16[2,64,512]{2,1,0:T(8,128)(2,1)S(1)} collective-permute-done((bf16[2,64,512]{2,1,0:T(8,128)(2,1)S(1)}, bf16[2,64,512]{2,1,0:T(8,128)(2,1)S(1)}, u32[]{:S(2)}, u32[]{:S(2)}) %collective-permute-start.17) | collective-permute-done | bytes 131104 | tf_op jit(solution)/shard_map/ppermute | solution.py:601
  40.5 1.1 collective-permute-done.27
  41.7 1.5 collective-permute-start.8
  43.1 1.8 %collective-permute-done.22 = bf16[2,64,512]{2,1,0:T(8,128)(2,1)S(1)} collective-permute-done((bf16[2,64,512]{2,1,0:T(8,128)(2,1)S(1)}, bf16[2,64,512]{2,1,0:T(8,128)(2,1)S(1)}, u32[]{:S(2)}, u32[]{:S(2)}) %collective-permute-start.22) | collective-permute-done | bytes 131104 | tf_op jit(solution)/shard_map/ppermute | solution.py:601
  46.4 3.1 %collective-permute-done.8.refs_13_ = bf16[4,64,512]{2,1,0:T(8,128)(2,1)S(1)} collective-permute-done((bf16[4,64,512]{2,1,0:T(8,128)(2,1)S(1)}, bf16[4,64,512]{2,1,0:T(8,128)(2,1)S(1)}, u32[]{:S(2)}, u32[]{:S(2)}) %collective-permute-start.8) | collective-permute-done | bytes 262176 | tf_op jit(solution)/shard_map/ppermute | solution.py:601
  49.5 1.6 collective-permute-start.23
  51.1 2.6 %collective-permute-done.13.refs_17_ = bf16[4,64,512]{2,1,0:T(8,128)(2,1)S(1)} collective-permute-done((bf16[4,64,512]{2,1,0:T(8,128)(2,1)S(1)}, bf16[4,64,512]{2,1,0:T(8,128)(2,1)S(1)}, u32[]{:S(2)}, u32[]{:S(2)}) %collective-permute-start.13) | collective-permute-done | bytes 262176 | tf_op jit(solution)/shard_map/ppermute | solution.py:601
  54.7 3.5 %collective-permute-done.23.refs_25_ = bf16[4,64,512]{2,1,0:T(8,128)(2,1)S(1)} collective-permute-done((bf16[4,64,512]{2,1,0:T(8,128)(2,1)S(1)}, bf16[4,64,512]{2,1,0:T(8,128)(2,1)S(1)}, u32[]{:S(2)}, u32[]{:S(2)}) %collective-permute-start.23) | collective-permute-done | bytes 262176 | tf_op jit(solution)/shard_map/ppermute | solution.py:601
  58.7 3.7 %collective-permute-done.28.refs_29_ = bf16[4,64,512]{2,1,0:T(8,128)(2,1)S(1)} collective-permute-done((bf16[4,64,512]{2,1,0:T(8,128)(2,1)S(1)}, bf16[4,64,512]{2,1,0:T(8,128)(2,1)S(1)}, u32[]{:S(2)}, u32[]{:S(2)}) %collective-permute-start.28) | collective-permute-done | bytes 262176 | tf_op jit(solution)/shard_map/ppermute | solution.py:601
  63.0 1.0 collective-permute-done.25.refs_27_
  64.0 0.7 copy-done.28
  64.8 30.7 %layer.1 = (bf16[1,14,14,512]{3,2,1,0:T(8,128)(2,1)}, bf16[1,14,14,512]{3,2,1,0:T(8,128)(2,1)}, f32[12,512]{1,0:T(8,128)}, f32[64,1024]{1,0:T(8,128)}, bf16[8,64...) custom-call(s32[96]{0:T(128)} %get-tuple-element.36.refs_0_, ...), custom_call_target="tpu_custom_call" | custom-call | tf_op jit(solution)/shard_map/layer/pallas_call | solution.py:418
  95.5 0.8 reshape.109
  96.3 1.1 reshape.110
  97.6 0.8 fusion
  100.9 3.4 %collective-permute-done.48 = f32[8848]{0:T(1024)S(1)} collective-permute-done((f32[8848]{0:T(1024)S(1)}, f32[8848]{0:T(1024)S(1)}, u32[]{:S(2)}, u32[]{:S(2)}) %collective-permute-start.48) | collective-permute-done | bytes 35424 | tf_op jit(solution)/shard_map/ppermute | solution.py:601
  104.8 3.4 %collective-permute-done.49 = f32[8848]{0:T(1024)S(1)} collective-permute-done((f32[8848]{0:T(1024)S(1)}, f32[8848]{0:T(1024)S(1)}, u32[]{:S(2)}, u32[]{:S(2)}) %collective-permute-start.49) | collective-permute-done | bytes 35424 | tf_op jit(solution)/shard_map/ppermute | solution.py:601
  109.2 3.0 %collective-permute-done.50 = f32[8848]{0:T(1024)S(1)} collective-permute-done((f32[8848]{0:T(1024)S(1)}, f32[8848]{0:T(1024)S(1)}, u32[]{:S(2)}, u32[]{:S(2)}) %collective-permute-start.50) | collective-permute-done | bytes 35424 | tf_op jit(solution)/shard_map/ppermute | solution.py:601
  116.6 10.7 %collective-permute-done.33 = bf16[8,64,512]{2,1,0:T(8,128)(2,1)S(1)} collective-permute-done((bf16[8,64,512]{2,1,0:T(8,128)(2,1)S(1)}, bf16[8,64,512]{2,1,0:T(8,128)(2,1)S(1)}, u32[]{:S(2)}, u32[]{:S(2)}) %collective-permute-start.33) | collective-permute-done | bytes 524320 | tf_op jit(solution)/shard_map/ppermute | solution.py:601
  128.0 0.9 collective-permute-done.38
  129.7 1.2 collective-permute-start.44
  130.9 3.7 %collective-permute-done.34 = bf16[4,64,512]{2,1,0:T(8,128)(2,1)S(1)} collective-permute-done((bf16[4,64,512]{2,1,0:T(8,128)(2,1)S(1)}, bf16[4,64,512]{2,1,0:T(8,128)(2,1)S(1)}, u32[]{:S(2)}, u32[]{:S(2)}) %collective-permute-start.34) | collective-permute-done | bytes 262176 | tf_op jit(solution)/shard_map/ppermute | solution.py:601
  134.7 1.3 collective-permute-start.35
  136.0 1.8 %collective-permute-done.39 = bf16[4,64,512]{2,1,0:T(8,128)(2,1)S(1)} collective-permute-done((bf16[4,64,512]{2,1,0:T(8,128)(2,1)S(1)}, bf16[4,64,512]{2,1,0:T(8,128)(2,1)S(1)}, u32[]{:S(2)}, u32[]{:S(2)}) %collective-permute-start.39) | collective-permute-done | bytes 262176 | tf_op jit(solution)/shard_map/ppermute | solution.py:601
  138.0 0.7 collective-permute-start.45
  138.7 1.1 collective-permute-done.35
  139.8 3.1 %collective-permute-done.40 = bf16[2,64,512]{2,1,0:T(8,128)(2,1)S(1)} collective-permute-done((bf16[2,64,512]{2,1,0:T(8,128)(2,1)S(1)}, bf16[2,64,512]{2,1,0:T(8,128)(2,1)S(1)}, u32[]{:S(2)}, u32[]{:S(2)}) %collective-permute-start.40) | collective-permute-done | bytes 131104 | tf_op jit(solution)/shard_map/ppermute | solution.py:601
  143.1 1.4 collective-permute-start.46
  145.2 0.7 pad_maximum_fusion.6.refs_0_
  145.9 5.9 %collective-permute-done.46.refs_1_ = bf16[3,64,512]{2,1,0:T(8,128)(2,1)S(1)} collective-permute-done((bf16[3,64,512]{2,1,0:T(8,128)(2,1)S(1)}, bf16[3,64,512]{2,1,0:T(8,128)(2,1)S(1)}, u32[]{:S(2)}, u32[]{:S(2)}) %collective-permute-start.46) | collective-permute-done | bytes 196640 | tf_op jit(solution)/shard_map/ppermute | solution.py:601
  152.5 3.1 %adam.1 = (f32[768,128]{1,0:T(8,128)}, f32[768,128]{1,0:T(8,128)}, f32[768,128]{1,0:T(8,128)}, f32[768,128]{1,0:T(8,128)}) custom-call(s32[3]{0:T(128)} %compare_select_fusion.kinds, bf16[3,64,512]{2,1,0:T(8,128)(2,1)} %pad_maximum_fusion.6.refs_0_, bf16[3,64,512]{2,1,0:T(8,128)(2,1)} %copy-done.29, f32[768,128]{1,0:T(8,128)} %bitcast.27, ...), custom_call_target="tpu_custom_call" | custom-call | tf_op jit(solution)/shard_map/adam/pallas_call | solution.py:546
  (207 shorter events, 22.4 us)
Async XLA Ops:
  3.1 22.4 %collective-permute-start = (bf16[3,64,512]{2,1,0:T(8,128)(2,1)}, bf16[3,64,512]{2,1,0:T(8,128)(2,1)S(1)}, u32[]{:S(2)}, u32[]{:S(2)}) collective-permute-start(bf16[3,64,512]{2,1,0:T(8,128)(2,1)} %pack.1), channel_id=1, source_target_pairs={{0,16},{1,17},{2,18},{3,19},{4,20},{5,21},{6,22},{7,23},{8,24},{9,... | collective-permute-start | bytes 589832 | tf_op jit(solution)/shard_map/ppermute | solution.py:601
  8.2 12.2 %collective-permute-start.11 = (bf16[1,64,512]{2,1,0:T(8,128)(2,1)S(1)}, bf16[1,64,512]{2,1,0:T(8,128)(2,1)S(1)}, u32[]{:S(2)}, u32[]{:S(2)}) collective-permute-start(bf16[1,64,512]{2,1,0:T(8,128)(2,1)S(1)} %get-tuple-element.90), channel_id=1, source_target_pairs={{0,4},{1,5},{2,6},{3,7},{4,0},{5,1},{6,2},{7,3},{8,12},{9,13},{10,... | collective-permute-start | bytes 196616 | tf_op jit(solution)/shard_map/ppermute | solution.py:601
  9.7 11.2 %collective-permute-start.6 = (bf16[1,64,512]{2,1,0:T(8,128)(2,1)S(1)}, bf16[1,64,512]{2,1,0:T(8,128)(2,1)S(1)}, u32[]{:S(2)}, u32[]{:S(2)}) collective-permute-start(bf16[1,64,512]{2,1,0:T(8,128)(2,1)S(1)} %get-tuple-element.91), channel_id=1, source_target_pairs={{0,2},{1,3},{2,0},{3,1},{4,6},{5,7},{6,4},{7,5},{8,10},{9,11},{10,... | collective-permute-start | bytes 196616 | tf_op jit(solution)/shard_map/ppermute | solution.py:601
  11.2 8.6 %collective-permute-start.1 = (bf16[1,64,512]{2,1,0:T(8,128)(2,1)S(1)}, bf16[1,64,512]{2,1,0:T(8,128)(2,1)S(1)}, u32[]{:S(2)}, u32[]{:S(2)}) collective-permute-start(bf16[1,64,512]{2,1,0:T(8,128)(2,1)S(1)} %get-tuple-element.92), channel_id=1, source_target_pairs={{0,8},{1,9},{2,10},{3,11},{4,12},{5,13},{6,14},{7,15},{8,0},{9,1},... | collective-permute-start | bytes 196616 | tf_op jit(solution)/shard_map/ppermute | solution.py:601
  19.8 5.0 %collective-permute-start.2 = (bf16[2,64,512]{2,1,0:T(8,128)(2,1)S(1)}, bf16[2,64,512]{2,1,0:T(8,128)(2,1)S(1)}, u32[]{:S(2)}, u32[]{:S(2)}) collective-permute-start(bf16[2,64,512]{2,1,0:T(8,128)(2,1)S(1)} %pad_maximum_fusion.8), channel_id=1, source_target_pairs={{0,4},{1,5},{2,6},{3,7},{4,0},{5,1},{6,2},{7,3},{8,12},{9,13},{10,... | collective-permute-start | bytes 393224 | tf_op jit(solution)/shard_map/ppermute | solution.py:601
  20.4 15.3 %collective-permute-start.12 = (bf16[2,64,512]{2,1,0:T(8,128)(2,1)S(1)}, bf16[2,64,512]{2,1,0:T(8,128)(2,1)S(1)}, u32[]{:S(2)}, u32[]{:S(2)}) collective-permute-start(bf16[2,64,512]{2,1,0:T(8,128)(2,1)S(1)} %pad_maximum_fusion.10), channel_id=1, source_target_pairs={{0,2},{1,3},{2,0},{3,1},{4,6},{5,7},{6,4},{7,5},{8,10},{9,11},{10,... | collective-permute-start | bytes 393224 | tf_op jit(solution)/shard_map/ppermute | solution.py:601
  21.0 5.1 %collective-permute-start.7 = (bf16[2,64,512]{2,1,0:T(8,128)(2,1)S(1)}, bf16[2,64,512]{2,1,0:T(8,128)(2,1)S(1)}, u32[]{:S(2)}, u32[]{:S(2)}) collective-permute-start(bf16[2,64,512]{2,1,0:T(8,128)(2,1)S(1)} %pad_maximum_fusion.9), channel_id=1, source_target_pairs={{0,8},{1,9},{2,10},{3,11},{4,12},{5,13},{6,14},{7,15},{8,0},{9,1},... | collective-permute-start | bytes 393224 | tf_op jit(solution)/shard_map/ppermute | solution.py:601
  24.8 20.1 %collective-permute-start.4 = (bf16[4,64,512]{2,1,0:T(8,128)(2,1)S(1)}, bf16[4,64,512]{2,1,0:T(8,128)(2,1)S(1)}, u32[]{:S(2)}, u32[]{:S(2)}) collective-permute-start(bf16[4,64,512]{2,1,0:T(8,128)(2,1)S(1)} %pad_maximum_fusion.refs_8_), channel_id=1, source_target_pairs={{0,1},{1,0},{2,3},{3,2},{4,5},{5,4},{6,7},{7,6},{8,9},{9,8},{10,11... | collective-permute-start | bytes 786440 | tf_op jit(solution)/shard_map/ppermute | solution.py:601
  24.9 20.6 %collective-permute-start.3 = (bf16[4,64,512]{2,1,0:T(8,128)(2,1)S(1)}, bf16[4,64,512]{2,1,0:T(8,128)(2,1)S(1)}, u32[]{:S(2)}, u32[]{:S(2)}) collective-permute-start(bf16[4,64,512]{2,1,0:T(8,128)(2,1)S(1)} %pad_maximum_fusion.refs_8_), channel_id=1, source_target_pairs={{0,2},{1,3},{2,0},{3,1},{4,6},{5,7},{6,4},{7,5},{8,10},{9,11},{10,... | collective-permute-start | bytes 786440 | tf_op jit(solution)/shard_map/ppermute | solution.py:601
  25.5 4.3 %collective-permute-start.16 = (bf16[1,64,512]{2,1,0:T(8,128)(2,1)S(1)}, bf16[1,64,512]{2,1,0:T(8,128)(2,1)S(1)}, u32[]{:S(2)}, u32[]{:S(2)}) collective-permute-start(bf16[1,64,512]{2,1,0:T(8,128)(2,1)S(1)} %get-tuple-element.89), channel_id=1, source_target_pairs={{0,8},{1,9},{2,10},{3,11},{4,12},{5,13},{6,14},{7,15},{8,0},{9,1},... | collective-permute-start | bytes 196616 | tf_op jit(solution)/shard_map/ppermute | solution.py:601
  26.2 9.4 %collective-permute-start.26 = (bf16[1,64,512]{2,1,0:T(8,128)(2,1)S(1)}, bf16[1,64,512]{2,1,0:T(8,128)(2,1)S(1)}, u32[]{:S(2)}, u32[]{:S(2)}) collective-permute-start(bf16[1,64,512]{2,1,0:T(8,128)(2,1)S(1)} %get-tuple-element.87), channel_id=1, source_target_pairs={{0,4},{1,5},{2,6},{3,7},{4,0},{5,1},{6,2},{7,3},{8,12},{9,13},{10,... | collective-permute-start | bytes 196616 | tf_op jit(solution)/shard_map/ppermute | solution.py:601
  29.8 5.2 %collective-permute-start.21 = (bf16[1,64,512]{2,1,0:T(8,128)(2,1)S(1)}, bf16[1,64,512]{2,1,0:T(8,128)(2,1)S(1)}, u32[]{:S(2)}, u32[]{:S(2)}) collective-permute-start(bf16[1,64,512]{2,1,0:T(8,128)(2,1)S(1)} %get-tuple-element.88), channel_id=1, source_target_pairs={{0,2},{1,3},{2,0},{3,1},{4,6},{5,7},{6,4},{7,5},{8,10},{9,11},{10,... | collective-permute-start | bytes 196616 | tf_op jit(solution)/shard_map/ppermute | solution.py:601
  35.0 5.0 %collective-permute-start.17 = (bf16[2,64,512]{2,1,0:T(8,128)(2,1)S(1)}, bf16[2,64,512]{2,1,0:T(8,128)(2,1)S(1)}, u32[]{:S(2)}, u32[]{:S(2)}) collective-permute-start(bf16[2,64,512]{2,1,0:T(8,128)(2,1)S(1)} %pad_maximum_fusion.11), channel_id=1, source_target_pairs={{0,4},{1,5},{2,6},{3,7},{4,0},{5,1},{6,2},{7,3},{8,12},{9,13},{10,... | collective-permute-start | bytes 393224 | tf_op jit(solution)/shard_map/ppermute | solution.py:601
  35.6 10.1 %collective-permute-start.9 = (bf16[4,64,512]{2,1,0:T(8,128)(2,1)S(1)}, bf16[4,64,512]{2,1,0:T(8,128)(2,1)S(1)}, u32[]{:S(2)}, u32[]{:S(2)}) collective-permute-start(bf16[4,64,512]{2,1,0:T(8,128)(2,1)S(1)} %pad_maximum_fusion.1.refs_12_), channel_id=1, source_target_pairs={{0,1},{1,0},{2,3},{3,2},{4,5},{5,4},{6,7},{7,6},{8,9},{9,8},{10,11... | collective-permute-start | bytes 786440 | tf_op jit(solution)/shard_map/ppermute | solution.py:601
  35.7 6.0 %collective-permute-start.27 = (bf16[2,64,512]{2,1,0:T(8,128)(2,1)S(1)}, bf16[2,64,512]{2,1,0:T(8,128)(2,1)S(1)}, u32[]{:S(2)}, u32[]{:S(2)}) collective-permute-start(bf16[2,64,512]{2,1,0:T(8,128)(2,1)S(1)} %pad_maximum_fusion.13), channel_id=1, source_target_pairs={{0,2},{1,3},{2,0},{3,1},{4,6},{5,7},{6,4},{7,5},{8,10},{9,11},{10,... | collective-permute-start | bytes 393224 | tf_op jit(solution)/shard_map/ppermute | solution.py:601
  40.0 5.0 %collective-permute-start.22 = (bf16[2,64,512]{2,1,0:T(8,128)(2,1)S(1)}, bf16[2,64,512]{2,1,0:T(8,128)(2,1)S(1)}, u32[]{:S(2)}, u32[]{:S(2)}) collective-permute-start(bf16[2,64,512]{2,1,0:T(8,128)(2,1)S(1)} %pad_maximum_fusion.12), channel_id=1, source_target_pairs={{0,8},{1,9},{2,10},{3,11},{4,12},{5,13},{6,14},{7,15},{8,0},{9,1},... | collective-permute-start | bytes 393224 | tf_op jit(solution)/shard_map/ppermute | solution.py:601
  41.7 7.8 %collective-permute-start.8 = (bf16[4,64,512]{2,1,0:T(8,128)(2,1)S(1)}, bf16[4,64,512]{2,1,0:T(8,128)(2,1)S(1)}, u32[]{:S(2)}, u32[]{:S(2)}) collective-permute-start(bf16[4,64,512]{2,1,0:T(8,128)(2,1)S(1)} %pad_maximum_fusion.1.refs_12_), channel_id=1, source_target_pairs={{0,4},{1,5},{2,6},{3,7},{4,0},{5,1},{6,2},{7,3},{8,12},{9,13},{10,... | collective-permute-start | bytes 786440 | tf_op jit(solution)/shard_map/ppermute | solution.py:601
  45.0 4.5 %collective-permute-start.14 = (bf16[4,64,512]{2,1,0:T(8,128)(2,1)S(1)}, bf16[4,64,512]{2,1,0:T(8,128)(2,1)S(1)}, u32[]{:S(2)}, u32[]{:S(2)}) collective-permute-start(bf16[4,64,512]{2,1,0:T(8,128)(2,1)S(1)} %pad_maximum_fusion.2.refs_16_), channel_id=1, source_target_pairs={{0,1},{1,0},{2,3},{3,2},{4,5},{5,4},{6,7},{7,6},{8,9},{9,8},{10,11... | collective-permute-start | bytes 786440 | tf_op jit(solution)/shard_map/ppermute | solution.py:601
  45.0 8.7 %collective-permute-start.13 = (bf16[4,64,512]{2,1,0:T(8,128)(2,1)S(1)}, bf16[4,64,512]{2,1,0:T(8,128)(2,1)S(1)}, u32[]{:S(2)}, u32[]{:S(2)}) collective-permute-start(bf16[4,64,512]{2,1,0:T(8,128)(2,1)S(1)} %pad_maximum_fusion.2.refs_16_), channel_id=1, source_target_pairs={{0,8},{1,9},{2,10},{3,11},{4,12},{5,13},{6,14},{7,15},{8,0},{9,1},... | collective-permute-start | bytes 786440 | tf_op jit(solution)/shard_map/ppermute | solution.py:601
  45.5 8.2 %collective-permute-start.19 = (bf16[4,64,512]{2,1,0:T(8,128)(2,1)S(1)}, bf16[4,64,512]{2,1,0:T(8,128)(2,1)S(1)}, u32[]{:S(2)}, u32[]{:S(2)}) collective-permute-start(bf16[4,64,512]{2,1,0:T(8,128)(2,1)S(1)} %pad_maximum_fusion.3.refs_20_), channel_id=1, source_target_pairs={{0,1},{1,0},{2,3},{3,2},{4,5},{5,4},{6,7},{7,6},{8,9},{9,8},{10,11... | collective-permute-start | bytes 786440 | tf_op jit(solution)/shard_map/ppermute | solution.py:601
  45.7 8.6 %collective-permute-start.18 = (bf16[4,64,512]{2,1,0:T(8,128)(2,1)S(1)}, bf16[4,64,512]{2,1,0:T(8,128)(2,1)S(1)}, u32[]{:S(2)}, u32[]{:S(2)}) collective-permute-start(bf16[4,64,512]{2,1,0:T(8,128)(2,1)S(1)} %pad_maximum_fusion.3.refs_20_), channel_id=1, source_target_pairs={{0,2},{1,3},{2,0},{3,1},{4,6},{5,7},{6,4},{7,5},{8,10},{9,11},{10,... | collective-permute-start | bytes 786440 | tf_op jit(solution)/shard_map/ppermute | solution.py:601
  49.5 4.9 %collective-permute-start.24 = (bf16[4,64,512]{2,1,0:T(8,128)(2,1)S(1)}, bf16[4,64,512]{2,1,0:T(8,128)(2,1)S(1)}, u32[]{:S(2)}, u32[]{:S(2)}) collective-permute-start(bf16[4,64,512]{2,1,0:T(8,128)(2,1)S(1)} %pad_maximum_fusion.4.refs_24_), channel_id=1, source_target_pairs={{0,1},{1,0},{2,3},{3,2},{4,5},{5,4},{6,7},{7,6},{8,9},{9,8},{10,11... | collective-permute-start | bytes 786440 | tf_op jit(solution)/shard_map/ppermute | solution.py:601
  49.5 8.7 %collective-permute-start.23 = (bf16[4,64,512]{2,1,0:T(8,128)(2,1)S(1)}, bf16[4,64,512]{2,1,0:T(8,128)(2,1)S(1)}, u32[]{:S(2)}, u32[]{:S(2)}) collective-permute-start(bf16[4,64,512]{2,1,0:T(8,128)(2,1)S(1)} %pad_maximum_fusion.4.refs_24_), channel_id=1, source_target_pairs={{0,4},{1,5},{2,6},{3,7},{4,0},{5,1},{6,2},{7,3},{8,12},{9,13},{10,... | collective-permute-start | bytes 786440 | tf_op jit(solution)/shard_map/ppermute | solution.py:601
  53.7 4.5 %collective-permute-start.29 = (bf16[4,64,512]{2,1,0:T(8,128)(2,1)S(1)}, bf16[4,64,512]{2,1,0:T(8,128)(2,1)S(1)}, u32[]{:S(2)}, u32[]{:S(2)}) collective-permute-start(bf16[4,64,512]{2,1,0:T(8,128)(2,1)S(1)} %pad_maximum_fusion.5.refs_28_), channel_id=1, source_target_pairs={{0,1},{1,0},{2,3},{3,2},{4,5},{5,4},{6,7},{7,6},{8,9},{9,8},{10,11... | collective-permute-start | bytes 786440 | tf_op jit(solution)/shard_map/ppermute | solution.py:601
  53.7 8.7 %collective-permute-start.28 = (bf16[4,64,512]{2,1,0:T(8,128)(2,1)S(1)}, bf16[4,64,512]{2,1,0:T(8,128)(2,1)S(1)}, u32[]{:S(2)}, u32[]{:S(2)}) collective-permute-start(bf16[4,64,512]{2,1,0:T(8,128)(2,1)S(1)} %pad_maximum_fusion.5.refs_28_), channel_id=1, source_target_pairs={{0,8},{1,9},{2,10},{3,11},{4,12},{5,13},{6,14},{7,15},{8,0},{9,1},... | collective-permute-start | bytes 786440 | tf_op jit(solution)/shard_map/ppermute | solution.py:601
  54.2 8.2 %collective-permute-start.5 = (bf16[4,64,512]{2,1,0:T(8,128)(2,1)S(1)}, bf16[4,64,512]{2,1,0:T(8,128)(2,1)S(1)}, u32[]{:S(2)}, u32[]{:S(2)}) collective-permute-start(bf16[4,64,512]{2,1,0:T(8,128)(2,1)S(1)} %collective-permute-done.3.refs_9_), channel_id=1, source_target_pairs={{0,1},{1,0},{2,3},{3,2},{4,5},{5,4},{6,7},{7,6},{8,9},{9,8},{10,11... | collective-permute-start | bytes 786440 | tf_op jit(solution)/shard_map/ppermute | solution.py:601
  54.4 8.6 %collective-permute-start.10 = (bf16[4,64,512]{2,1,0:T(8,128)(2,1)S(1)}, bf16[4,64,512]{2,1,0:T(8,128)(2,1)S(1)}, u32[]{:S(2)}, u32[]{:S(2)}) collective-permute-start(bf16[4,64,512]{2,1,0:T(8,128)(2,1)S(1)} %collective-permute-done.8.refs_13_), channel_id=1, source_target_pairs={{0,1},{1,0},{2,3},{3,2},{4,5},{5,4},{6,7},{7,6},{8,9},{9,8},{10,11... | collective-permute-start | bytes 786440 | tf_op jit(solution)/shard_map/ppermute | solution.py:601
  58.2 4.7 %collective-permute-start.15 = (bf16[4,64,512]{2,1,0:T(8,128)(2,1)S(1)}, bf16[4,64,512]{2,1,0:T(8,128)(2,1)S(1)}, u32[]{:S(2)}, u32[]{:S(2)}) collective-permute-start(bf16[4,64,512]{2,1,0:T(8,128)(2,1)S(1)} %collective-permute-done.13.refs_17_), channel_id=1, source_target_pairs={{0,1},{1,0},{2,3},{3,2},{4,5},{5,4},{6,7},{7,6},{8,9},{9,8},{10,11... | collective-permute-start | bytes 786440 | tf_op jit(solution)/shard_map/ppermute | solution.py:601
  58.2 4.7 %collective-permute-start.20 = (bf16[4,64,512]{2,1,0:T(8,128)(2,1)S(1)}, bf16[4,64,512]{2,1,0:T(8,128)(2,1)S(1)}, u32[]{:S(2)}, u32[]{:S(2)}) collective-permute-start(bf16[4,64,512]{2,1,0:T(8,128)(2,1)S(1)} %collective-permute-done.18.refs_21_), channel_id=1, source_target_pairs={{0,1},{1,0},{2,3},{3,2},{4,5},{5,4},{6,7},{7,6},{8,9},{9,8},{10,11... | collective-permute-start | bytes 786440 | tf_op jit(solution)/shard_map/ppermute | solution.py:601
  99.2 13.1 %collective-permute-start.31 = (bf16[8,64,512]{2,1,0:T(8,128)(2,1)}, bf16[8,64,512]{2,1,0:T(8,128)(2,1)S(1)}, u32[]{:S(2)}, u32[]{:S(2)}) collective-permute-start(bf16[8,64,512]{2,1,0:T(8,128)(2,1)} %get-tuple-element.45), channel_id=1, source_target_pairs={{0,1},{1,0},{2,3},{3,2},{4,5},{5,4},{6,7},{7,6},{8,9},{9,8},{10,11... | collective-permute-start | bytes 1572872 | tf_op jit(solution)/shard_map/ppermute | solution.py:601
  99.6 13.4 %collective-permute-start.32 = (bf16[8,64,512]{2,1,0:T(8,128)(2,1)}, bf16[8,64,512]{2,1,0:T(8,128)(2,1)S(1)}, u32[]{:S(2)}, u32[]{:S(2)}) collective-permute-start(bf16[8,64,512]{2,1,0:T(8,128)(2,1)} %get-tuple-element.47), channel_id=1, source_target_pairs={{0,1},{1,0},{2,3},{3,2},{4,5},{5,4},{6,7},{7,6},{8,9},{9,8},{10,11... | collective-permute-start | bytes 1572872 | tf_op jit(solution)/shard_map/ppermute | solution.py:601
  100.3 4.0 %collective-permute-start.48 = (f32[8848]{0:T(1024)S(1)}, f32[8848]{0:T(1024)S(1)}, u32[]{:S(2)}, u32[]{:S(2)}) collective-permute-start(f32[8848]{0:T(1024)S(1)} %fusion.24), channel_id=1, source_target_pairs={{0,2},{1,3},{2,0},{3,1},{4,6},{5,7},{6,4},{7,5},{8,10},{9,11},{10,... | collective-permute-start | bytes 106184 | tf_op jit(solution)/shard_map/ppermute | solution.py:601
  104.3 4.0 %collective-permute-start.49 = (f32[8848]{0:T(1024)S(1)}, f32[8848]{0:T(1024)S(1)}, u32[]{:S(2)}, u32[]{:S(2)}) collective-permute-start(f32[8848]{0:T(1024)S(1)} %add.159), channel_id=1, source_target_pairs={{0,4},{1,5},{2,6},{3,7},{4,0},{5,1},{6,2},{7,3},{8,12},{9,13},{10,... | collective-permute-start | bytes 106184 | tf_op jit(solution)/shard_map/ppermute | solution.py:601
  108.3 4.0 %collective-permute-start.50 = (f32[8848]{0:T(1024)S(1)}, f32[8848]{0:T(1024)S(1)}, u32[]{:S(2)}, u32[]{:S(2)}) collective-permute-start(f32[8848]{0:T(1024)S(1)} %add.160), channel_id=1, source_target_pairs={{0,8},{1,9},{2,10},{3,11},{4,12},{5,13},{6,14},{7,15},{8,0},{9,1},... | collective-permute-start | bytes 106184 | tf_op jit(solution)/shard_map/ppermute | solution.py:601
  108.7 6.9 %collective-permute-start.36 = (bf16[8,64,512]{2,1,0:T(8,128)(2,1)S(1)}, bf16[8,64,512]{2,1,0:T(8,128)(2,1)S(1)}, u32[]{:S(2)}, u32[]{:S(2)}) collective-permute-start(bf16[8,64,512]{2,1,0:T(8,128)(2,1)S(1)} %copy-done.40), channel_id=1, source_target_pairs={{0,1},{1,0},{2,3},{3,2},{4,5},{5,4},{6,7},{7,6},{8,9},{9,8},{10,11... | collective-permute-start | bytes 1572872 | tf_op jit(solution)/shard_map/ppermute | solution.py:601
  108.7 4.9 %collective-permute-start.37 = (bf16[8,64,512]{2,1,0:T(8,128)(2,1)S(1)}, bf16[8,64,512]{2,1,0:T(8,128)(2,1)S(1)}, u32[]{:S(2)}, u32[]{:S(2)}) collective-permute-start(bf16[8,64,512]{2,1,0:T(8,128)(2,1)S(1)} %copy-done.42), channel_id=1, source_target_pairs={{0,1},{1,0},{2,3},{3,2},{4,5},{5,4},{6,7},{7,6},{8,9},{9,8},{10,11... | collective-permute-start | bytes 1572872 | tf_op jit(solution)/shard_map/ppermute | solution.py:601
  112.2 4.1 %collective-permute-start.41 = (bf16[8,64,512]{2,1,0:T(8,128)(2,1)S(1)}, bf16[8,64,512]{2,1,0:T(8,128)(2,1)S(1)}, u32[]{:S(2)}, u32[]{:S(2)}) collective-permute-start(bf16[8,64,512]{2,1,0:T(8,128)(2,1)S(1)} %copy-done.39), channel_id=1, source_target_pairs={{0,1},{1,0},{2,3},{3,2},{4,5},{5,4},{6,7},{7,6},{8,9},{9,8},{10,11... | collective-permute-start | bytes 1572872 | tf_op jit(solution)/shard_map/ppermute | solution.py:601
  113.0 31.5 %collective-permute-start.51 = (f32[8848]{0:T(1024)S(1)}, f32[8848]{0:T(1024)S(1)}, u32[]{:S(2)}, u32[]{:S(2)}) collective-permute-start(f32[8848]{0:T(1024)S(1)} %add.161), channel_id=1, source_target_pairs={{0,16},{1,17},{2,18},{3,19},{4,20},{5,21},{6,22},{7,23},{8,24},{9,... | collective-permute-start | bytes 106184 | tf_op jit(solution)/shard_map/ppermute | solution.py:601
  113.6 13.6 %collective-permute-start.33 = (bf16[8,64,512]{2,1,0:T(8,128)(2,1)S(1)}, bf16[8,64,512]{2,1,0:T(8,128)(2,1)S(1)}, u32[]{:S(2)}, u32[]{:S(2)}) collective-permute-start(bf16[8,64,512]{2,1,0:T(8,128)(2,1)S(1)} %add_convert_fusion.4), channel_id=1, source_target_pairs={{0,2},{1,3},{2,0},{3,1},{4,6},{5,7},{6,4},{7,5},{8,10},{9,11},{10,... | collective-permute-start | bytes 1572872 | tf_op jit(solution)/shard_map/ppermute | solution.py:601
  114.9 14.0 %collective-permute-start.38 = (bf16[8,64,512]{2,1,0:T(8,128)(2,1)S(1)}, bf16[8,64,512]{2,1,0:T(8,128)(2,1)S(1)}, u32[]{:S(2)}, u32[]{:S(2)}) collective-permute-start(bf16[8,64,512]{2,1,0:T(8,128)(2,1)S(1)} %add_convert_fusion.2), channel_id=1, source_target_pairs={{0,4},{1,5},{2,6},{3,7},{4,0},{5,1},{6,2},{7,3},{8,12},{9,13},{10,... | collective-permute-start | bytes 1572872 | tf_op jit(solution)/shard_map/ppermute | solution.py:601
  115.6 13.9 %collective-permute-start.43 = (bf16[8,64,512]{2,1,0:T(8,128)(2,1)S(1)}, bf16[8,64,512]{2,1,0:T(8,128)(2,1)S(1)}, u32[]{:S(2)}, u32[]{:S(2)}) collective-permute-start(bf16[8,64,512]{2,1,0:T(8,128)(2,1)S(1)} %add_convert_fusion), channel_id=1, source_target_pairs={{0,8},{1,9},{2,10},{3,11},{4,12},{5,13},{6,14},{7,15},{8,0},{9,1},... | collective-permute-start | bytes 1572872 | tf_op jit(solution)/shard_map/ppermute | solution.py:601
  127.4 7.2 %collective-permute-start.34 = (bf16[4,64,512]{2,1,0:T(8,128)(2,1)S(1)}, bf16[4,64,512]{2,1,0:T(8,128)(2,1)S(1)}, u32[]{:S(2)}, u32[]{:S(2)}) collective-permute-start(bf16[4,64,512]{2,1,0:T(8,128)(2,1)S(1)} %get-tuple-element.67), channel_id=1, source_target_pairs={{0,4},{1,5},{2,6},{3,7},{4,0},{5,1},{6,2},{7,3},{8,12},{9,13},{10,... | collective-permute-start | bytes 786440 | tf_op jit(solution)/shard_map/ppermute | solution.py:601
  129.0 8.7 %collective-permute-start.39 = (bf16[4,64,512]{2,1,0:T(8,128)(2,1)S(1)}, bf16[4,64,512]{2,1,0:T(8,128)(2,1)S(1)}, u32[]{:S(2)}, u32[]{:S(2)}) collective-permute-start(bf16[4,64,512]{2,1,0:T(8,128)(2,1)S(1)} %get-tuple-element.69), channel_id=1, source_target_pairs={{0,8},{1,9},{2,10},{3,11},{4,12},{5,13},{6,14},{7,15},{8,0},{9,1},... | collective-permute-start | bytes 786440 | tf_op jit(solution)/shard_map/ppermute | solution.py:601
  129.7 8.2 %collective-permute-start.44 = (bf16[4,64,512]{2,1,0:T(8,128)(2,1)S(1)}, bf16[4,64,512]{2,1,0:T(8,128)(2,1)S(1)}, u32[]{:S(2)}, u32[]{:S(2)}) collective-permute-start(bf16[4,64,512]{2,1,0:T(8,128)(2,1)S(1)} %get-tuple-element.71), channel_id=1, source_target_pairs={{0,2},{1,3},{2,0},{3,1},{4,6},{5,7},{6,4},{7,5},{8,10},{9,11},{10,... | collective-permute-start | bytes 786440 | tf_op jit(solution)/shard_map/ppermute | solution.py:601
  134.7 5.0 %collective-permute-start.35 = (bf16[2,64,512]{2,1,0:T(8,128)(2,1)S(1)}, bf16[2,64,512]{2,1,0:T(8,128)(2,1)S(1)}, u32[]{:S(2)}, u32[]{:S(2)}) collective-permute-start(bf16[2,64,512]{2,1,0:T(8,128)(2,1)S(1)} %get-tuple-element.76), channel_id=1, source_target_pairs={{0,8},{1,9},{2,10},{3,11},{4,12},{5,13},{6,14},{7,15},{8,0},{9,1},... | collective-permute-start | bytes 393224 | tf_op jit(solution)/shard_map/ppermute | solution.py:601
  137.8 5.0 %collective-permute-start.40 = (bf16[2,64,512]{2,1,0:T(8,128)(2,1)S(1)}, bf16[2,64,512]{2,1,0:T(8,128)(2,1)S(1)}, u32[]{:S(2)}, u32[]{:S(2)}) collective-permute-start(bf16[2,64,512]{2,1,0:T(8,128)(2,1)S(1)} %get-tuple-element.78), channel_id=1, source_target_pairs={{0,2},{1,3},{2,0},{3,1},{4,6},{5,7},{6,4},{7,5},{8,10},{9,11},{10,... | collective-permute-start | bytes 393224 | tf_op jit(solution)/shard_map/ppermute | solution.py:601
  138.0 5.0 %collective-permute-start.45 = (bf16[2,64,512]{2,1,0:T(8,128)(2,1)S(1)}, bf16[2,64,512]{2,1,0:T(8,128)(2,1)S(1)}, u32[]{:S(2)}, u32[]{:S(2)}) collective-permute-start(bf16[2,64,512]{2,1,0:T(8,128)(2,1)S(1)} %get-tuple-element.80), channel_id=1, source_target_pairs={{0,4},{1,5},{2,6},{3,7},{4,0},{5,1},{6,2},{7,3},{8,12},{9,13},{10,... | collective-permute-start | bytes 393224 | tf_op jit(solution)/shard_map/ppermute | solution.py:601
  143.1 8.7 %collective-permute-start.46 = (bf16[3,64,512]{2,1,0:T(8,128)(2,1)S(1)}, bf16[3,64,512]{2,1,0:T(8,128)(2,1)S(1)}, u32[]{:S(2)}, u32[]{:S(2)}) collective-permute-start(bf16[3,64,512]{2,1,0:T(8,128)(2,1)S(1)} %pad_maximum_fusion.7), channel_id=1, source_target_pairs={{0,16},{1,17},{2,18},{3,19},{4,20},{5,21},{6,22},{7,23},{8,24},{9,... | collective-permute-start | bytes 589832 | tf_op jit(solution)/shard_map/ppermute | solution.py:601
  (48 other events, 509.3 us)
where the time goes:
time: 156 us
  waiting for transfers between devices  67.6 us (43%)
  Pallas kernels  35.6 us (23%)
  starting transfers between devices  34.3 us (22%)
  local copies, waits for them, and re-layouts  7.79 us (5%)
  other arithmetic  5.45 us (3%)
  matrix products  3.36 us (2%)
    ppermute x52, waiting for transfers between devices, swap(): return lax.ppermute(value, AXES, [(i, i ^ bit) for i in range(devices)])  67.6 us
    ppermute x52, starting transfers between devices, swap(): return lax.ppermute(value, AXES, [(i, i ^ bit) for i in range(devices)])  34.3 us
    pallas_call x1, Pallas kernels, run_layer(): pl.pallas_call(layer_kernel(counts, outs), in_specs=[smem, smem] + [vmem]...  30.7 us
  transfers between devices with their start and end apart: 52, of which 24 were waited for; matrix products, arithmetic and copies ran while one was open for 7% of the time, Pallas kernels for 0%

commit v1 on v0

--- a/solution.py
+++ b/solution.py
@@ -49,7 +49,6 @@
 QKV_END = 3 * D // PIECE
 PROJ_END = QKV_END + D // PIECE
 UP_END = PROJ_END + FF // PIECE
-KINDS = 4 + 2 * (FF // D)
 SMALL_ROWS = 8 + FF // D
 f32 = jnp.float32
 bf16 = jnp.bfloat16
@@ -116,6 +115,10 @@
         (
             weights,
             wgrad,
+            n_one,
+            n_two,
+            s_one,
+            s_two,
             flat,
             xw,
             cw,
@@ -139,48 +142,34 @@
             sem_out,
         ) = refs[4 + n_out :]
 
-        def place(third, make, make_up):
-            @pl.when(third < QKV_END)
-            def _():
-                make(lax.rem(third, 3), lax.div(third, 3) * PIECE)
-
-            @pl.when((third >= QKV_END) & (third < PROJ_END))
-            def _():
-                make(3, (third - QKV_END) * PIECE)
-
-            @pl.when((third >= PROJ_END) & (third < UP_END))
-            def _():
-                make_up((third - PROJ_END) * UP_ROWS)
-
-            @pl.when(third >= UP_END)
-            def _():
-                at = third - UP_END
-                make(4 + FF // D + lax.div(at, D // PIECE), lax.rem(at, D // PIECE) * PIECE)
-
         base = 0
         for number, count in enumerate(counts):
 
             def fetch(slot, carry, number=number, base=base):
-                source = pieces[number].at[slot]
-
-                def make(block, row):
-                    row = pl.multiple_of(row, PIECE)
-                    pltpu.make_async_copy(source, weights.at[block, pl.ds(row, PIECE)], sem).start()
-
-                def make_up(row):
-                    row = pl.multiple_of(row, UP_ROWS)
-                    for j in range(FF // D):
-                        pltpu.make_async_copy(
-                            source.at[pl.ds(j * UP_ROWS, UP_ROWS)],
-                            weights.at[4 + j, pl.ds(row, UP_ROWS)],
-                            sem,
-                        ).start()
-
-                place(slots[base + slot], make, make_up)
+                pltpu.make_async_copy(
+                    pieces[number].at[slot], weights.at[slots[base + slot]], sem
+                ).start()
                 return carry
 
-            lax.fori_loop(0, count, fetch, 0)
+            lax.fori_loop(0, count, fetch, 0, unroll=min(count, 8))
             base += count
+
+        def third_rows(first, count, stride=1):
+            parts = [weights[first + stride * number] for number in range(count)]
+            return jnp.concatenate(parts, axis=0)
+
+        def qkv_block(part):
+            return third_rows(part, D // PIECE, 3)
+
+        def proj_block():
+            return weights[QKV_END:PROJ_END].reshape(D, D)
+
+        def up_block(j):
+            at = pl.ds(pl.multiple_of(j * UP_ROWS, UP_ROWS), UP_ROWS)
+            return weights[PROJ_END:UP_END, at, :].reshape(D, D)
+
+        def down_block(j):
+            return weights[pl.ds(UP_END + j * (D // PIECE), D // PIECE)].reshape(D, D)
 
         gain_one, gain_two, shift_one, bias_query, bias_value, bias_proj, shift_two, bias_down = (
             small[number : number + 1, :] for number in range(8)
@@ -199,11 +188,13 @@
 
         def norm_one(number, carry):
             at = rows_of(number, PAD)
-            normed, _ = norm_stats(xw[at, :])
+            normed, scaling = norm_stats(xw[at, :])
+            n_one[at, :] = normed
+            s_one[at, :] = jnp.broadcast_to(scaling, (PAD, 128))
             in_one[at, :] = (normed * gain_one + shift_one).astype(bf16)
             return carry
 
-        lax.fori_loop(0, WINDOWS, norm_one, 0)
+        lax.fori_loop(0, WINDOWS, norm_one, 0, unroll=True)
 
         for window in range(WINDOWS):
             allowed = mask[window] != 0
@@ -229,7 +220,7 @@
         pltpu.make_async_copy(weights, weights, sem).wait()
 
         for part, vector in enumerate((bias_query, None, bias_value)):
-            product = dot(in_one[...], weights[part])
+            product = dot(in_one[...], qkv_block(part))
             if vector is not None:
                 product = product + vector
             qkv[part] = product.astype(bf16)
@@ -251,21 +242,21 @@
 
         lax.fori_loop(0, WINDOWS, attend, 0)
 
-        resid[...] = xw[...] + (dot(mixed[...], weights[3]) + bias_proj)
+        resid[...] = xw[...] + (dot(mixed[...], proj_block()) + bias_proj)
 
         def norm_two(number, carry):
             at = rows_of(number, PAD)
-            normed, _ = norm_stats(resid[at, :])
+            normed, scaling = norm_stats(resid[at, :])
+            n_two[at, :] = normed
+            s_two[at, :] = jnp.broadcast_to(scaling, (PAD, 128))
             in_two[at, :] = (normed * gain_two + shift_two).astype(bf16)
             return carry
 
-        lax.fori_loop(0, WINDOWS, norm_two, 0)
+        lax.fori_loop(0, WINDOWS, norm_two, 0, unroll=True)
 
         def feed(j, carry):
-            up = weights.at[4 + j]
-            down = weights.at[4 + FF // D + j]
-            acc_two[...] = dot(in_two[...], up[...]) + small[pl.ds(8 + j, 1), :]
-            pre[...] = dot_t(cw[...], down[...])
+            acc_two[...] = dot(in_two[...], up_block(j)) + small[pl.ds(8 + j, 1), :]
+            pre[...] = dot_t(cw[...], down_block(j))
 
             def gelu_part(number, total):
                 at = rows_of(number, 32)
@@ -278,10 +269,10 @@
                 return total + col_sum(back)
 
             sums[pl.ds(8 + j, 1), :] = lax.fori_loop(
-                0, ROWS // 32, gelu_part, jnp.zeros((1, D), f32)
+                0, ROWS // 32, gelu_part, jnp.zeros((1, D), f32), unroll=2
             )
-            forward = dot(act[...], down[...])
-            backward = dot_t(grow[...], up[...])
+            forward = dot(act[...], down_block(j))
+            backward = dot_t(grow[...], up_block(j))
 
             @pl.when(j == 0)
             def _():
@@ -293,8 +284,13 @@
                 acc[...] += forward
                 gres[...] += backward
 
-            wgrad[4 + j] = t_dot(in_two[...], grow[...]).astype(bf16)
-            wgrad[4 + FF // D + j] = t_dot(act[...], cw[...]).astype(bf16)
+            up_grad = t_dot(in_two[...], grow[...]).astype(bf16)
+            at = pl.ds(pl.multiple_of(j * UP_ROWS, UP_ROWS), UP_ROWS)
+            wgrad[PROJ_END:UP_END, at, :] = up_grad.reshape(FF // PIECE, UP_ROWS, D)
+            down_grad = t_dot(act[...], cw[...]).astype(bf16)
+            wgrad[pl.ds(UP_END + j * (D // PIECE), D // PIECE)] = down_grad.reshape(
+                D // PIECE, PIECE, D
+            )
             return carry
 
         lax.fori_loop(0, FF // D, feed, 0)
@@ -303,7 +299,7 @@
             gain_sum, shift_sum, resid_sum, cot_sum = carry
             at = rows_of(number, 32)
             value = resid[at, :]
-            normed, scaling = norm_stats(value)
+            normed, scaling = n_two[at, :], s_two[at, 0:1]
             act[at, :] = (value + (acc[at, :] + bias_down)).astype(bf16)
             incoming = gres[at, :]
             back = norm_back(incoming, normed, scaling, gain_two)
@@ -320,14 +316,15 @@
 
         zero_row = jnp.zeros((1, D), f32)
         sums[1:2, :], sums[6:7, :], sums[5:6, :], sums[7:8, :] = lax.fori_loop(
-            0, ROWS // 32, second_back, (zero_row,) * 4
+            0, ROWS // 32, second_back, (zero_row,) * 4, unroll=4
         )
         result = t_dot(perm[...], act[...]).astype(bf16)
         for row in range(SIDE):
             out[0, row] = result[row * STRIP : row * STRIP + SIDE, :]
 
-        wgrad[3] = t_dot(mixed[...], grow[...]).astype(bf16)
-        mgrad[...] = dot_t(grow[...], weights[3]).astype(bf16)
+        proj_grad = t_dot(mixed[...], grow[...]).astype(bf16)
+        wgrad[QKV_END:PROJ_END] = proj_grad.reshape(D // PIECE, PIECE, D)
+        mgrad[...] = dot_t(grow[...], proj_block()).astype(bf16)
         sums[3:4, :] = zero_row
         sums[4:5, :] = zero_row
         rel_sum[...] = jnp.zeros_like(rel_sum)
@@ -357,49 +354,38 @@
         lax.fori_loop(0, WINDOWS, attend_back, 0)
 
         for part in range(3):
-            wgrad[part] = t_dot(in_one[...], dqkv[part]).astype(bf16)
+            part_grad = t_dot(in_one[...], dqkv[part]).astype(bf16)
+            for number in range(D // PIECE):
+                wgrad[3 * number + part] = part_grad[number * PIECE : (number + 1) * PIECE]
 
         base = 0
         for number, count in enumerate(out_counts):
 
             def store(slot, carry, number=number, base=base):
-                target = grads[number].at[slot]
-
-                def make(block, row):
-                    row = pl.multiple_of(row, PIECE)
-                    pltpu.make_async_copy(
-                        wgrad.at[block, pl.ds(row, PIECE)], target, sem_out
-                    ).start()
-
-                def make_up(row):
-                    row = pl.multiple_of(row, UP_ROWS)
-                    for j in range(FF // D):
-                        pltpu.make_async_copy(
-                            wgrad.at[4 + j, pl.ds(row, UP_ROWS)],
-                            target.at[pl.ds(j * UP_ROWS, UP_ROWS)],
-                            sem_out,
-                        ).start()
-
-                place(out_slots[base + slot], make, make_up)
+                pltpu.make_async_copy(
+                    wgrad.at[out_slots[base + slot]], grads[number].at[slot], sem_out
+                ).start()
                 return carry
 
-            lax.fori_loop(0, count, store, 0)
+            lax.fori_loop(0, count, store, 0, unroll=min(count, 8))
             base += count
 
-        acc[...] = dot_t(dqkv[0], weights[0])
-        acc[...] += dot_t(dqkv[1], weights[1])
-        acc[...] += dot_t(dqkv[2], weights[2])
+        acc[...] = (
+            dot_t(dqkv[0], qkv_block(0)) + dot_t(dqkv[1], qkv_block(1))
+        ) + dot_t(dqkv[2], qkv_block(2))
 
         def first_back(number, carry):
             gain_sum, shift_sum = carry
             at = rows_of(number, 32)
-            normed, scaling = norm_stats(xw[at, :])
+            normed, scaling = n_one[at, :], s_one[at, 0:1]
             incoming = acc[at, :]
             back = norm_back(incoming, normed, scaling, gain_one)
             act[at, :] = (gres[at, :] + back).astype(bf16)
             return gain_sum + col_sum(incoming * normed), shift_sum + col_sum(incoming)
 
-        sums[0:1, :], sums[2:3, :] = lax.fori_loop(0, ROWS // 32, first_back, (zero_row,) * 2)
+        sums[0:1, :], sums[2:3, :] = lax.fori_loop(
+            0, ROWS // 32, first_back, (zero_row,) * 2, unroll=4
+        )
         result = t_dot(perm[...], act[...]).astype(bf16)
         for row in range(SIDE):
             in_grad[0, row] = result[row * STRIP : row * STRIP + SIDE, :]
@@ -427,8 +413,12 @@
         ]
         + [jax.ShapeDtypeStruct((count, PIECE, D), bf16) for count in outs],
         scratch_shapes=[
-            pltpu.VMEM((KINDS, D, D), bf16),
-            pltpu.VMEM((KINDS, D, D), bf16),
+            pltpu.VMEM((BLOCKS, PIECE, D), bf16),
+            pltpu.VMEM((BLOCKS, PIECE, D), bf16),
+            pltpu.VMEM((ROWS, D), f32),
+            pltpu.VMEM((ROWS, D), f32),
+            pltpu.VMEM((ROWS, 128), f32),
+            pltpu.VMEM((ROWS, 128), f32),
             pltpu.VMEM((FLAT, D), bf16),
             pltpu.VMEM((ROWS, D), f32),
             pltpu.VMEM((ROWS, D), bf16),

time: 156 us -> 150 us (0.962)
  Pallas kernels: 35.6 us -> 29.8 us
    pallas_call x1, Pallas kernels: 30.7 us -> 24.9 us  [run_layer(): pl.pallas_call(layer_kernel(counts, outs), in_specs=[smem, smem] + [vmem]...]
where the time goes in v1:
time: 150 us
  waiting for transfers between devices  67.7 us (45%)
  starting transfers between devices  34.2 us (23%)
  Pallas kernels  29.8 us (20%)
  local copies, waits for them, and re-layouts  7.79 us (5%)
  other arithmetic  5.45 us (4%)
  matrix products  3.36 us (2%)
    ppermute x52, waiting for transfers between devices, swap(): return lax.ppermute(value, AXES, [(i, i ^ bit) for i in range(devices)])  67.7 us
    ppermute x52, starting transfers between devices, swap(): return lax.ppermute(value, AXES, [(i, i ^ bit) for i in range(devices)])  34.2 us
    pallas_call x1, Pallas kernels, run_layer(): pl.pallas_call(layer_kernel(counts, outs), in_specs=[smem, smem] + [vmem]...  24.9 us
    pallas_call x1, Pallas kernels, adam_shard(): pl.pallas_call(adam_kernel(grad_scale), in_specs=[pl.BlockSpec(memory_spa...  3.1 us
  transfers between devices with their start and end apart: 52, of which 24 were waited for; matrix products, arithmetic and copies ran while one was open for 7% of the time, Pallas kernels for 0%

profile of v1, /device:TPU:0, one launch (start us, length us, event | category | flops | bytes accessed | tf_op | source)
XLA Modules:
  0.0 149.8 jit_solution(8462065093216023696)
XLA Ops:
  1.3 1.8 %pack.1 = bf16[3,64,512]{2,1,0:T(8,128)(2,1)} custom-call(s32[3]{0:T(128)} %compare_select_fusion.kinds, f32[768,128]{1,0:T(8,128)} %bitcast.26), custom_call_target="tpu_custom_call" | custom-call | tf_op jit(solution)/shard_map/pack/pallas_call | solution.py:485
  3.1 4.2 %collective-permute-start = (bf16[3,64,512]{2,1,0:T(8,128)(2,1)}, bf16[3,64,512]{2,1,0:T(8,128)(2,1)S(1)}, u32[]{:S(2)}, u32[]{:S(2)}) collective-permute-start(bf16[3,64,512]{2,1,0:T(8,128)(2,1)} %pack.1), channel_id=1, source_target_pairs={{0,16},{1,17},{2,18},{3,19},{4,20},{5,21},{6,22},{7,23},{8,24},{9,... | collective-permute-start | bytes 589832 | tf_op jit(solution)/shard_map/ppermute | solution.py:591
  7.3 0.9 fusion.27
  8.2 1.6 %collective-permute-start.11 = (bf16[1,64,512]{2,1,0:T(8,128)(2,1)S(1)}, bf16[1,64,512]{2,1,0:T(8,128)(2,1)S(1)}, u32[]{:S(2)}, u32[]{:S(2)}) collective-permute-start(bf16[1,64,512]{2,1,0:T(8,128)(2,1)S(1)} %get-tuple-element.90), channel_id=1, source_target_pairs={{0,4},{1,5},{2,6},{3,7},{4,0},{5,1},{6,2},{7,3},{8,12},{9,13},{10,... | collective-permute-start | bytes 196616 | tf_op jit(solution)/shard_map/ppermute | solution.py:591
  9.7 1.4 collective-permute-start.6
  11.2 1.6 %collective-permute-start.1 = (bf16[1,64,512]{2,1,0:T(8,128)(2,1)S(1)}, bf16[1,64,512]{2,1,0:T(8,128)(2,1)S(1)}, u32[]{:S(2)}, u32[]{:S(2)}) collective-permute-start(bf16[1,64,512]{2,1,0:T(8,128)(2,1)S(1)} %get-tuple-element.92), channel_id=1, source_target_pairs={{0,8},{1,9},{2,10},{3,11},{4,12},{5,13},{6,14},{7,15},{8,0},{9,1},... | collective-permute-start | bytes 196616 | tf_op jit(solution)/shard_map/ppermute | solution.py:591
  12.7 0.7 slice.153
  13.5 0.8 reshape.104
  14.5 1.0 reduce-precision_convert_fusion.3
  15.5 0.8 compare_convert_fusion.refs_7_
  16.3 1.2 fusion.1
  18.8 0.9 reshape.103.refs_6_
  21.6 3.2 %collective-permute-done.2 = bf16[2,64,512]{2,1,0:T(8,128)(2,1)S(1)} collective-permute-done((bf16[2,64,512]{2,1,0:T(8,128)(2,1)S(1)}, bf16[2,64,512]{2,1,0:T(8,128)(2,1)S(1)}, u32[]{:S(2)}, u32[]{:S(2)}) %collective-permute-start.2) | collective-permute-done | bytes 131104 | tf_op jit(solution)/shard_map/ppermute | solution.py:591
  26.2 1.4 collective-permute-start.26
  27.6 2.2 %collective-permute-done.16 = bf16[1,64,512]{2,1,0:T(8,128)(2,1)S(1)} collective-permute-done((bf16[1,64,512]{2,1,0:T(8,128)(2,1)S(1)}, bf16[1,64,512]{2,1,0:T(8,128)(2,1)S(1)}, u32[]{:S(2)}, u32[]{:S(2)}) %collective-permute-start.16) | collective-permute-done | bytes 65568 | tf_op jit(solution)/shard_map/ppermute | solution.py:591
  29.8 1.5 %collective-permute-start.21 = (bf16[1,64,512]{2,1,0:T(8,128)(2,1)S(1)}, bf16[1,64,512]{2,1,0:T(8,128)(2,1)S(1)}, u32[]{:S(2)}, u32[]{:S(2)}) collective-permute-start(bf16[1,64,512]{2,1,0:T(8,128)(2,1)S(1)} %get-tuple-element.88), channel_id=1, source_target_pairs={{0,2},{1,3},{2,0},{3,1},{4,6},{5,7},{6,4},{7,5},{8,10},{9,11},{10,... | collective-permute-start | bytes 196616 | tf_op jit(solution)/shard_map/ppermute | solution.py:591
  31.4 3.7 %collective-permute-done.21 = bf16[1,64,512]{2,1,0:T(8,128)(2,1)S(1)} collective-permute-done((bf16[1,64,512]{2,1,0:T(8,128)(2,1)S(1)}, bf16[1,64,512]{2,1,0:T(8,128)(2,1)S(1)}, u32[]{:S(2)}, u32[]{:S(2)}) %collective-permute-start.21) | collective-permute-done | bytes 65568 | tf_op jit(solution)/shard_map/ppermute | solution.py:591
  36.4 3.6 %collective-permute-done.17 = bf16[2,64,512]{2,1,0:T(8,128)(2,1)S(1)} collective-permute-done((bf16[2,64,512]{2,1,0:T(8,128)(2,1)S(1)}, bf16[2,64,512]{2,1,0:T(8,128)(2,1)S(1)}, u32[]{:S(2)}, u32[]{:S(2)}) %collective-permute-start.17) | collective-permute-done | bytes 131104 | tf_op jit(solution)/shard_map/ppermute | solution.py:591
  40.5 1.1 collective-permute-done.27
  41.7 1.5 collective-permute-start.8
  43.1 1.8 %collective-permute-done.22 = bf16[2,64,512]{2,1,0:T(8,128)(2,1)S(1)} collective-permute-done((bf16[2,64,512]{2,1,0:T(8,128)(2,1)S(1)}, bf16[2,64,512]{2,1,0:T(8,128)(2,1)S(1)}, u32[]{:S(2)}, u32[]{:S(2)}) %collective-permute-start.22) | collective-permute-done | bytes 131104 | tf_op jit(solution)/shard_map/ppermute | solution.py:591
  46.4 3.1 %collective-permute-done.8.refs_13_ = bf16[4,64,512]{2,1,0:T(8,128)(2,1)S(1)} collective-permute-done((bf16[4,64,512]{2,1,0:T(8,128)(2,1)S(1)}, bf16[4,64,512]{2,1,0:T(8,128)(2,1)S(1)}, u32[]{:S(2)}, u32[]{:S(2)}) %collective-permute-start.8) | collective-permute-done | bytes 262176 | tf_op jit(solution)/shard_map/ppermute | solution.py:591
  49.5 1.6 %collective-permute-start.23 = (bf16[4,64,512]{2,1,0:T(8,128)(2,1)S(1)}, bf16[4,64,512]{2,1,0:T(8,128)(2,1)S(1)}, u32[]{:S(2)}, u32[]{:S(2)}) collective-permute-start(bf16[4,64,512]{2,1,0:T(8,128)(2,1)S(1)} %pad_maximum_fusion.4.refs_24_), channel_id=1, source_target_pairs={{0,4},{1,5},{2,6},{3,7},{4,0},{5,1},{6,2},{7,3},{8,12},{9,13},{10,... | collective-permute-start | bytes 786440 | tf_op jit(solution)/shard_map/ppermute | solution.py:591
  51.1 2.6 %collective-permute-done.13.refs_17_ = bf16[4,64,512]{2,1,0:T(8,128)(2,1)S(1)} collective-permute-done((bf16[4,64,512]{2,1,0:T(8,128)(2,1)S(1)}, bf16[4,64,512]{2,1,0:T(8,128)(2,1)S(1)}, u32[]{:S(2)}, u32[]{:S(2)}) %collective-permute-start.13) | collective-permute-done | bytes 262176 | tf_op jit(solution)/shard_map/ppermute | solution.py:591
  54.7 3.5 %collective-permute-done.23.refs_25_ = bf16[4,64,512]{2,1,0:T(8,128)(2,1)S(1)} collective-permute-done((bf16[4,64,512]{2,1,0:T(8,128)(2,1)S(1)}, bf16[4,64,512]{2,1,0:T(8,128)(2,1)S(1)}, u32[]{:S(2)}, u32[]{:S(2)}) %collective-permute-start.23) | collective-permute-done | bytes 262176 | tf_op jit(solution)/shard_map/ppermute | solution.py:591
  58.7 3.7 %collective-permute-done.28.refs_29_ = bf16[4,64,512]{2,1,0:T(8,128)(2,1)S(1)} collective-permute-done((bf16[4,64,512]{2,1,0:T(8,128)(2,1)S(1)}, bf16[4,64,512]{2,1,0:T(8,128)(2,1)S(1)}, u32[]{:S(2)}, u32[]{:S(2)}) %collective-permute-start.28) | collective-permute-done | bytes 262176 | tf_op jit(solution)/shard_map/ppermute | solution.py:591
  63.0 1.0 collective-permute-done.25.refs_27_
  64.0 0.7 copy-done.28
  64.8 24.9 %layer.1 = (bf16[1,14,14,512]{3,2,1,0:T(8,128)(2,1)}, bf16[1,14,14,512]{3,2,1,0:T(8,128)(2,1)}, f32[12,512]{1,0:T(8,128)}, f32[64,1024]{1,0:T(8,128)}, bf16[8,64...) custom-call(s32[96]{0:T(128)} %get-tuple-element.36.refs_0_, ...), custom_call_target="tpu_custom_call" | custom-call | tf_op jit(solution)/shard_map/layer/pallas_call | solution.py:404
  89.7 0.8 reshape.109
  90.5 1.1 reshape.110
  91.8 0.8 fusion
  95.1 3.4 %collective-permute-done.48 = f32[8848]{0:T(1024)S(1)} collective-permute-done((f32[8848]{0:T(1024)S(1)}, f32[8848]{0:T(1024)S(1)}, u32[]{:S(2)}, u32[]{:S(2)}) %collective-permute-start.48) | collective-permute-done | bytes 35424 | tf_op jit(solution)/shard_map/ppermute | solution.py:591
  99.0 3.4 %collective-permute-done.49 = f32[8848]{0:T(1024)S(1)} collective-permute-done((f32[8848]{0:T(1024)S(1)}, f32[8848]{0:T(1024)S(1)}, u32[]{:S(2)}, u32[]{:S(2)}) %collective-permute-start.49) | collective-permute-done | bytes 35424 | tf_op jit(solution)/shard_map/ppermute | solution.py:591
  103.4 3.0 %collective-permute-done.50 = f32[8848]{0:T(1024)S(1)} collective-permute-done((f32[8848]{0:T(1024)S(1)}, f32[8848]{0:T(1024)S(1)}, u32[]{:S(2)}, u32[]{:S(2)}) %collective-permute-start.50) | collective-permute-done | bytes 35424 | tf_op jit(solution)/shard_map/ppermute | solution.py:591
  110.8 10.7 %collective-permute-done.33 = bf16[8,64,512]{2,1,0:T(8,128)(2,1)S(1)} collective-permute-done((bf16[8,64,512]{2,1,0:T(8,128)(2,1)S(1)}, bf16[8,64,512]{2,1,0:T(8,128)(2,1)S(1)}, u32[]{:S(2)}, u32[]{:S(2)}) %collective-permute-start.33) | collective-permute-done | bytes 524320 | tf_op jit(solution)/shard_map/ppermute | solution.py:591
  122.1 0.9 collective-permute-done.38
  123.8 1.2 collective-permute-start.44
  125.1 3.7 %collective-permute-done.34 = bf16[4,64,512]{2,1,0:T(8,128)(2,1)S(1)} collective-permute-done((bf16[4,64,512]{2,1,0:T(8,128)(2,1)S(1)}, bf16[4,64,512]{2,1,0:T(8,128)(2,1)S(1)}, u32[]{:S(2)}, u32[]{:S(2)}) %collective-permute-start.34) | collective-permute-done | bytes 262176 | tf_op jit(solution)/shard_map/ppermute | solution.py:591
  128.8 1.3 collective-permute-start.35
  130.1 1.8 %collective-permute-done.39 = bf16[4,64,512]{2,1,0:T(8,128)(2,1)S(1)} collective-permute-done((bf16[4,64,512]{2,1,0:T(8,128)(2,1)S(1)}, bf16[4,64,512]{2,1,0:T(8,128)(2,1)S(1)}, u32[]{:S(2)}, u32[]{:S(2)}) %collective-permute-start.39) | collective-permute-done | bytes 262176 | tf_op jit(solution)/shard_map/ppermute | solution.py:591
  132.2 0.7 collective-permute-start.45
  132.8 1.1 collective-permute-done.35
  133.9 3.1 %collective-permute-done.40 = bf16[2,64,512]{2,1,0:T(8,128)(2,1)S(1)} collective-permute-done((bf16[2,64,512]{2,1,0:T(8,128)(2,1)S(1)}, bf16[2,64,512]{2,1,0:T(8,128)(2,1)S(1)}, u32[]{:S(2)}, u32[]{:S(2)}) %collective-permute-start.40) | collective-permute-done | bytes 131104 | tf_op jit(solution)/shard_map/ppermute | solution.py:591
  137.3 1.4 collective-permute-start.46
  139.4 0.7 pad_maximum_fusion.6.refs_0_
  140.1 5.9 %collective-permute-done.46.refs_1_ = bf16[3,64,512]{2,1,0:T(8,128)(2,1)S(1)} collective-permute-done((bf16[3,64,512]{2,1,0:T(8,128)(2,1)S(1)}, bf16[3,64,512]{2,1,0:T(8,128)(2,1)S(1)}, u32[]{:S(2)}, u32[]{:S(2)}) %collective-permute-start.46) | collective-permute-done | bytes 196640 | tf_op jit(solution)/shard_map/ppermute | solution.py:591
  146.7 3.1 %adam.1 = (f32[768,128]{1,0:T(8,128)}, f32[768,128]{1,0:T(8,128)}, f32[768,128]{1,0:T(8,128)}, f32[768,128]{1,0:T(8,128)}) custom-call(s32[3]{0:T(128)} %compare_select_fusion.kinds, bf16[3,64,512]{2,1,0:T(8,128)(2,1)} %pad_maximum_fusion.6.refs_0_, bf16[3,64,512]{2,1,0:T(8,128)(2,1)} %copy-done.29, f32[768,128]{1,0:T(8,128)} %bitcast.27, ...), custom_call_target="tpu_custom_call" | custom-call | tf_op jit(solution)/shard_map/adam/pallas_call | solution.py:536
  (207 shorter events, 22.4 us)
Async XLA Ops:
  3.1 22.4 %collective-permute-start = (bf16[3,64,512]{2,1,0:T(8,128)(2,1)}, bf16[3,64,512]{2,1,0:T(8,128)(2,1)S(1)}, u32[]{:S(2)}, u32[]{:S(2)}) collective-permute-start(bf16[3,64,512]{2,1,0:T(8,128)(2,1)} %pack.1), channel_id=1, source_target_pairs={{0,16},{1,17},{2,18},{3,19},{4,20},{5,21},{6,22},{7,23},{8,24},{9,... | collective-permute-start | bytes 589832 | tf_op jit(solution)/shard_map/ppermute | solution.py:591
  8.2 12.2 %collective-permute-start.11 = (bf16[1,64,512]{2,1,0:T(8,128)(2,1)S(1)}, bf16[1,64,512]{2,1,0:T(8,128)(2,1)S(1)}, u32[]{:S(2)}, u32[]{:S(2)}) collective-permute-start(bf16[1,64,512]{2,1,0:T(8,128)(2,1)S(1)} %get-tuple-element.90), channel_id=1, source_target_pairs={{0,4},{1,5},{2,6},{3,7},{4,0},{5,1},{6,2},{7,3},{8,12},{9,13},{10,... | collective-permute-start | bytes 196616 | tf_op jit(solution)/shard_map/ppermute | solution.py:591
  9.7 11.2 %collective-permute-start.6 = (bf16[1,64,512]{2,1,0:T(8,128)(2,1)S(1)}, bf16[1,64,512]{2,1,0:T(8,128)(2,1)S(1)}, u32[]{:S(2)}, u32[]{:S(2)}) collective-permute-start(bf16[1,64,512]{2,1,0:T(8,128)(2,1)S(1)} %get-tuple-element.91), channel_id=1, source_target_pairs={{0,2},{1,3},{2,0},{3,1},{4,6},{5,7},{6,4},{7,5},{8,10},{9,11},{10,... | collective-permute-start | bytes 196616 | tf_op jit(solution)/shard_map/ppermute | solution.py:591
  11.2 8.6 %collective-permute-start.1 = (bf16[1,64,512]{2,1,0:T(8,128)(2,1)S(1)}, bf16[1,64,512]{2,1,0:T(8,128)(2,1)S(1)}, u32[]{:S(2)}, u32[]{:S(2)}) collective-permute-start(bf16[1,64,512]{2,1,0:T(8,128)(2,1)S(1)} %get-tuple-element.92), channel_id=1, source_target_pairs={{0,8},{1,9},{2,10},{3,11},{4,12},{5,13},{6,14},{7,15},{8,0},{9,1},... | collective-permute-start | bytes 196616 | tf_op jit(solution)/shard_map/ppermute | solution.py:591
  19.8 5.0 %collective-permute-start.2 = (bf16[2,64,512]{2,1,0:T(8,128)(2,1)S(1)}, bf16[2,64,512]{2,1,0:T(8,128)(2,1)S(1)}, u32[]{:S(2)}, u32[]{:S(2)}) collective-permute-start(bf16[2,64,512]{2,1,0:T(8,128)(2,1)S(1)} %pad_maximum_fusion.8), channel_id=1, source_target_pairs={{0,4},{1,5},{2,6},{3,7},{4,0},{5,1},{6,2},{7,3},{8,12},{9,13},{10,... | collective-permute-start | bytes 393224 | tf_op jit(solution)/shard_map/ppermute | solution.py:591
  20.4 15.3 %collective-permute-start.12 = (bf16[2,64,512]{2,1,0:T(8,128)(2,1)S(1)}, bf16[2,64,512]{2,1,0:T(8,128)(2,1)S(1)}, u32[]{:S(2)}, u32[]{:S(2)}) collective-permute-start(bf16[2,64,512]{2,1,0:T(8,128)(2,1)S(1)} %pad_maximum_fusion.10), channel_id=1, source_target_pairs={{0,2},{1,3},{2,0},{3,1},{4,6},{5,7},{6,4},{7,5},{8,10},{9,11},{10,... | collective-permute-start | bytes 393224 | tf_op jit(solution)/shard_map/ppermute | solution.py:591
  21.0 5.1 %collective-permute-start.7 = (bf16[2,64,512]{2,1,0:T(8,128)(2,1)S(1)}, bf16[2,64,512]{2,1,0:T(8,128)(2,1)S(1)}, u32[]{:S(2)}, u32[]{:S(2)}) collective-permute-start(bf16[2,64,512]{2,1,0:T(8,128)(2,1)S(1)} %pad_maximum_fusion.9), channel_id=1, source_target_pairs={{0,8},{1,9},{2,10},{3,11},{4,12},{5,13},{6,14},{7,15},{8,0},{9,1},... | collective-permute-start | bytes 393224 | tf_op jit(solution)/shard_map/ppermute | solution.py:591
  24.8 20.1 %collective-permute-start.4 = (bf16[4,64,512]{2,1,0:T(8,128)(2,1)S(1)}, bf16[4,64,512]{2,1,0:T(8,128)(2,1)S(1)}, u32[]{:S(2)}, u32[]{:S(2)}) collective-permute-start(bf16[4,64,512]{2,1,0:T(8,128)(2,1)S(1)} %pad_maximum_fusion.refs_8_), channel_id=1, source_target_pairs={{0,1},{1,0},{2,3},{3,2},{4,5},{5,4},{6,7},{7,6},{8,9},{9,8},{10,11... | collective-permute-start | bytes 786440 | tf_op jit(solution)/shard_map/ppermute | solution.py:591
  24.9 20.6 %collective-permute-start.3 = (bf16[4,64,512]{2,1,0:T(8,128)(2,1)S(1)}, bf16[4,64,512]{2,1,0:T(8,128)(2,1)S(1)}, u32[]{:S(2)}, u32[]{:S(2)}) collective-permute-start(bf16[4,64,512]{2,1,0:T(8,128)(2,1)S(1)} %pad_maximum_fusion.refs_8_), channel_id=1, source_target_pairs={{0,2},{1,3},{2,0},{3,1},{4,6},{5,7},{6,4},{7,5},{8,10},{9,11},{10,... | collective-permute-start | bytes 786440 | tf_op jit(solution)/shard_map/ppermute | solution.py:591
  25.5 4.3 %collective-permute-start.16 = (bf16[1,64,512]{2,1,0:T(8,128)(2,1)S(1)}, bf16[1,64,512]{2,1,0:T(8,128)(2,1)S(1)}, u32[]{:S(2)}, u32[]{:S(2)}) collective-permute-start(bf16[1,64,512]{2,1,0:T(8,128)(2,1)S(1)} %get-tuple-element.89), channel_id=1, source_target_pairs={{0,8},{1,9},{2,10},{3,11},{4,12},{5,13},{6,14},{7,15},{8,0},{9,1},... | collective-permute-start | bytes 196616 | tf_op jit(solution)/shard_map/ppermute | solution.py:591
  26.2 9.4 %collective-permute-start.26 = (bf16[1,64,512]{2,1,0:T(8,128)(2,1)S(1)}, bf16[1,64,512]{2,1,0:T(8,128)(2,1)S(1)}, u32[]{:S(2)}, u32[]{:S(2)}) collective-permute-start(bf16[1,64,512]{2,1,0:T(8,128)(2,1)S(1)} %get-tuple-element.87), channel_id=1, source_target_pairs={{0,4},{1,5},{2,6},{3,7},{4,0},{5,1},{6,2},{7,3},{8,12},{9,13},{10,... | collective-permute-start | bytes 196616 | tf_op jit(solution)/shard_map/ppermute | solution.py:591
  29.8 5.2 %collective-permute-start.21 = (bf16[1,64,512]{2,1,0:T(8,128)(2,1)S(1)}, bf16[1,64,512]{2,1,0:T(8,128)(2,1)S(1)}, u32[]{:S(2)}, u32[]{:S(2)}) collective-permute-start(bf16[1,64,512]{2,1,0:T(8,128)(2,1)S(1)} %get-tuple-element.88), channel_id=1, source_target_pairs={{0,2},{1,3},{2,0},{3,1},{4,6},{5,7},{6,4},{7,5},{8,10},{9,11},{10,... | collective-permute-start | bytes 196616 | tf_op jit(solution)/shard_map/ppermute | solution.py:591
  35.0 5.0 %collective-permute-start.17 = (bf16[2,64,512]{2,1,0:T(8,128)(2,1)S(1)}, bf16[2,64,512]{2,1,0:T(8,128)(2,1)S(1)}, u32[]{:S(2)}, u32[]{:S(2)}) collective-permute-start(bf16[2,64,512]{2,1,0:T(8,128)(2,1)S(1)} %pad_maximum_fusion.11), channel_id=1, source_target_pairs={{0,4},{1,5},{2,6},{3,7},{4,0},{5,1},{6,2},{7,3},{8,12},{9,13},{10,... | collective-permute-start | bytes 393224 | tf_op jit(solution)/shard_map/ppermute | solution.py:591
  35.6 10.1 %collective-permute-start.9 = (bf16[4,64,512]{2,1,0:T(8,128)(2,1)S(1)}, bf16[4,64,512]{2,1,0:T(8,128)(2,1)S(1)}, u32[]{:S(2)}, u32[]{:S(2)}) collective-permute-start(bf16[4,64,512]{2,1,0:T(8,128)(2,1)S(1)} %pad_maximum_fusion.1.refs_12_), channel_id=1, source_target_pairs={{0,1},{1,0},{2,3},{3,2},{4,5},{5,4},{6,7},{7,6},{8,9},{9,8},{10,11... | collective-permute-start | bytes 786440 | tf_op jit(solution)/shard_map/ppermute | solution.py:591
  35.7 6.0 %collective-permute-start.27 = (bf16[2,64,512]{2,1,0:T(8,128)(2,1)S(1)}, bf16[2,64,512]{2,1,0:T(8,128)(2,1)S(1)}, u32[]{:S(2)}, u32[]{:S(2)}) collective-permute-start(bf16[2,64,512]{2,1,0:T(8,128)(2,1)S(1)} %pad_maximum_fusion.13), channel_id=1, source_target_pairs={{0,2},{1,3},{2,0},{3,1},{4,6},{5,7},{6,4},{7,5},{8,10},{9,11},{10,... | collective-permute-start | bytes 393224 | tf_op jit(solution)/shard_map/ppermute | solution.py:591
  40.0 5.0 %collective-permute-start.22 = (bf16[2,64,512]{2,1,0:T(8,128)(2,1)S(1)}, bf16[2,64,512]{2,1,0:T(8,128)(2,1)S(1)}, u32[]{:S(2)}, u32[]{:S(2)}) collective-permute-start(bf16[2,64,512]{2,1,0:T(8,128)(2,1)S(1)} %pad_maximum_fusion.12), channel_id=1, source_target_pairs={{0,8},{1,9},{2,10},{3,11},{4,12},{5,13},{6,14},{7,15},{8,0},{9,1},... | collective-permute-start | bytes 393224 | tf_op jit(solution)/shard_map/ppermute | solution.py:591
  41.7 7.8 %collective-permute-start.8 = (bf16[4,64,512]{2,1,0:T(8,128)(2,1)S(1)}, bf16[4,64,512]{2,1,0:T(8,128)(2,1)S(1)}, u32[]{:S(2)}, u32[]{:S(2)}) collective-permute-start(bf16[4,64,512]{2,1,0:T(8,128)(2,1)S(1)} %pad_maximum_fusion.1.refs_12_), channel_id=1, source_target_pairs={{0,4},{1,5},{2,6},{3,7},{4,0},{5,1},{6,2},{7,3},{8,12},{9,13},{10,... | collective-permute-start | bytes 786440 | tf_op jit(solution)/shard_map/ppermute | solution.py:591
  45.0 4.5 %collective-permute-start.14 = (bf16[4,64,512]{2,1,0:T(8,128)(2,1)S(1)}, bf16[4,64,512]{2,1,0:T(8,128)(2,1)S(1)}, u32[]{:S(2)}, u32[]{:S(2)}) collective-permute-start(bf16[4,64,512]{2,1,0:T(8,128)(2,1)S(1)} %pad_maximum_fusion.2.refs_16_), channel_id=1, source_target_pairs={{0,1},{1,0},{2,3},{3,2},{4,5},{5,4},{6,7},{7,6},{8,9},{9,8},{10,11... | collective-permute-start | bytes 786440 | tf_op jit(solution)/shard_map/ppermute | solution.py:591
  45.0 8.7 %collective-permute-start.13 = (bf16[4,64,512]{2,1,0:T(8,128)(2,1)S(1)}, bf16[4,64,512]{2,1,0:T(8,128)(2,1)S(1)}, u32[]{:S(2)}, u32[]{:S(2)}) collective-permute-start(bf16[4,64,512]{2,1,0:T(8,128)(2,1)S(1)} %pad_maximum_fusion.2.refs_16_), channel_id=1, source_target_pairs={{0,8},{1,9},{2,10},{3,11},{4,12},{5,13},{6,14},{7,15},{8,0},{9,1},... | collective-permute-start | bytes 786440 | tf_op jit(solution)/shard_map/ppermute | solution.py:591
  45.5 8.2 %collective-permute-start.19 = (bf16[4,64,512]{2,1,0:T(8,128)(2,1)S(1)}, bf16[4,64,512]{2,1,0:T(8,128)(2,1)S(1)}, u32[]{:S(2)}, u32[]{:S(2)}) collective-permute-start(bf16[4,64,512]{2,1,0:T(8,128)(2,1)S(1)} %pad_maximum_fusion.3.refs_20_), channel_id=1, source_target_pairs={{0,1},{1,0},{2,3},{3,2},{4,5},{5,4},{6,7},{7,6},{8,9},{9,8},{10,11... | collective-permute-start | bytes 786440 | tf_op jit(solution)/shard_map/ppermute | solution.py:591
  45.7 8.6 %collective-permute-start.18 = (bf16[4,64,512]{2,1,0:T(8,128)(2,1)S(1)}, bf16[4,64,512]{2,1,0:T(8,128)(2,1)S(1)}, u32[]{:S(2)}, u32[]{:S(2)}) collective-permute-start(bf16[4,64,512]{2,1,0:T(8,128)(2,1)S(1)} %pad_maximum_fusion.3.refs_20_), channel_id=1, source_target_pairs={{0,2},{1,3},{2,0},{3,1},{4,6},{5,7},{6,4},{7,5},{8,10},{9,11},{10,... | collective-permute-start | bytes 786440 | tf_op jit(solution)/shard_map/ppermute | solution.py:591
  49.5 4.9 %collective-permute-start.24 = (bf16[4,64,512]{2,1,0:T(8,128)(2,1)S(1)}, bf16[4,64,512]{2,1,0:T(8,128)(2,1)S(1)}, u32[]{:S(2)}, u32[]{:S(2)}) collective-permute-start(bf16[4,64,512]{2,1,0:T(8,128)(2,1)S(1)} %pad_maximum_fusion.4.refs_24_), channel_id=1, source_target_pairs={{0,1},{1,0},{2,3},{3,2},{4,5},{5,4},{6,7},{7,6},{8,9},{9,8},{10,11... | collective-permute-start | bytes 786440 | tf_op jit(solution)/shard_map/ppermute | solution.py:591
  49.5 8.7 %collective-permute-start.23 = (bf16[4,64,512]{2,1,0:T(8,128)(2,1)S(1)}, bf16[4,64,512]{2,1,0:T(8,128)(2,1)S(1)}, u32[]{:S(2)}, u32[]{:S(2)}) collective-permute-start(bf16[4,64,512]{2,1,0:T(8,128)(2,1)S(1)} %pad_maximum_fusion.4.refs_24_), channel_id=1, source_target_pairs={{0,4},{1,5},{2,6},{3,7},{4,0},{5,1},{6,2},{7,3},{8,12},{9,13},{10,... | collective-permute-start | bytes 786440 | tf_op jit(solution)/shard_map/ppermute | solution.py:591
  53.7 4.5 %collective-permute-start.29 = (bf16[4,64,512]{2,1,0:T(8,128)(2,1)S(1)}, bf16[4,64,512]{2,1,0:T(8,128)(2,1)S(1)}, u32[]{:S(2)}, u32[]{:S(2)}) collective-permute-start(bf16[4,64,512]{2,1,0:T(8,128)(2,1)S(1)} %pad_maximum_fusion.5.refs_28_), channel_id=1, source_target_pairs={{0,1},{1,0},{2,3},{3,2},{4,5},{5,4},{6,7},{7,6},{8,9},{9,8},{10,11... | collective-permute-start | bytes 786440 | tf_op jit(solution)/shard_map/ppermute | solution.py:591
  53.7 8.7 %collective-permute-start.28 = (bf16[4,64,512]{2,1,0:T(8,128)(2,1)S(1)}, bf16[4,64,512]{2,1,0:T(8,128)(2,1)S(1)}, u32[]{:S(2)}, u32[]{:S(2)}) collective-permute-start(bf16[4,64,512]{2,1,0:T(8,128)(2,1)S(1)} %pad_maximum_fusion.5.refs_28_), channel_id=1, source_target_pairs={{0,8},{1,9},{2,10},{3,11},{4,12},{5,13},{6,14},{7,15},{8,0},{9,1},... | collective-permute-start | bytes 786440 | tf_op jit(solution)/shard_map/ppermute | solution.py:591
  54.2 8.2 %collective-permute-start.5 = (bf16[4,64,512]{2,1,0:T(8,128)(2,1)S(1)}, bf16[4,64,512]{2,1,0:T(8,128)(2,1)S(1)}, u32[]{:S(2)}, u32[]{:S(2)}) collective-permute-start(bf16[4,64,512]{2,1,0:T(8,128)(2,1)S(1)} %collective-permute-done.3.refs_9_), channel_id=1, source_target_pairs={{0,1},{1,0},{2,3},{3,2},{4,5},{5,4},{6,7},{7,6},{8,9},{9,8},{10,11... | collective-permute-start | bytes 786440 | tf_op jit(solution)/shard_map/ppermute | solution.py:591
  54.4 8.6 %collective-permute-start.10 = (bf16[4,64,512]{2,1,0:T(8,128)(2,1)S(1)}, bf16[4,64,512]{2,1,0:T(8,128)(2,1)S(1)}, u32[]{:S(2)}, u32[]{:S(2)}) collective-permute-start(bf16[4,64,512]{2,1,0:T(8,128)(2,1)S(1)} %collective-permute-done.8.refs_13_), channel_id=1, source_target_pairs={{0,1},{1,0},{2,3},{3,2},{4,5},{5,4},{6,7},{7,6},{8,9},{9,8},{10,11... | collective-permute-start | bytes 786440 | tf_op jit(solution)/shard_map/ppermute | solution.py:591
  58.2 4.7 %collective-permute-start.15 = (bf16[4,64,512]{2,1,0:T(8,128)(2,1)S(1)}, bf16[4,64,512]{2,1,0:T(8,128)(2,1)S(1)}, u32[]{:S(2)}, u32[]{:S(2)}) collective-permute-start(bf16[4,64,512]{2,1,0:T(8,128)(2,1)S(1)} %collective-permute-done.13.refs_17_), channel_id=1, source_target_pairs={{0,1},{1,0},{2,3},{3,2},{4,5},{5,4},{6,7},{7,6},{8,9},{9,8},{10,11... | collective-permute-start | bytes 786440 | tf_op jit(solution)/shard_map/ppermute | solution.py:591
  58.2 4.7 %collective-permute-start.20 = (bf16[4,64,512]{2,1,0:T(8,128)(2,1)S(1)}, bf16[4,64,512]{2,1,0:T(8,128)(2,1)S(1)}, u32[]{:S(2)}, u32[]{:S(2)}) collective-permute-start(bf16[4,64,512]{2,1,0:T(8,128)(2,1)S(1)} %collective-permute-done.18.refs_21_), channel_id=1, source_target_pairs={{0,1},{1,0},{2,3},{3,2},{4,5},{5,4},{6,7},{7,6},{8,9},{9,8},{10,11... | collective-permute-start | bytes 786440 | tf_op jit(solution)/shard_map/ppermute | solution.py:591
  93.3 13.1 %collective-permute-start.31 = (bf16[8,64,512]{2,1,0:T(8,128)(2,1)}, bf16[8,64,512]{2,1,0:T(8,128)(2,1)S(1)}, u32[]{:S(2)}, u32[]{:S(2)}) collective-permute-start(bf16[8,64,512]{2,1,0:T(8,128)(2,1)} %get-tuple-element.45), channel_id=1, source_target_pairs={{0,1},{1,0},{2,3},{3,2},{4,5},{5,4},{6,7},{7,6},{8,9},{9,8},{10,11... | collective-permute-start | bytes 1572872 | tf_op jit(solution)/shard_map/ppermute | solution.py:591
  93.7 13.4 %collective-permute-start.32 = (bf16[8,64,512]{2,1,0:T(8,128)(2,1)}, bf16[8,64,512]{2,1,0:T(8,128)(2,1)S(1)}, u32[]{:S(2)}, u32[]{:S(2)}) collective-permute-start(bf16[8,64,512]{2,1,0:T(8,128)(2,1)} %get-tuple-element.47), channel_id=1, source_target_pairs={{0,1},{1,0},{2,3},{3,2},{4,5},{5,4},{6,7},{7,6},{8,9},{9,8},{10,11... | collective-permute-start | bytes 1572872 | tf_op jit(solution)/shard_map/ppermute | solution.py:591
  94.4 4.0 %collective-permute-start.48 = (f32[8848]{0:T(1024)S(1)}, f32[8848]{0:T(1024)S(1)}, u32[]{:S(2)}, u32[]{:S(2)}) collective-permute-start(f32[8848]{0:T(1024)S(1)} %fusion.24), channel_id=1, source_target_pairs={{0,2},{1,3},{2,0},{3,1},{4,6},{5,7},{6,4},{7,5},{8,10},{9,11},{10,... | collective-permute-start | bytes 106184 | tf_op jit(solution)/shard_map/ppermute | solution.py:591
  98.5 4.0 %collective-permute-start.49 = (f32[8848]{0:T(1024)S(1)}, f32[8848]{0:T(1024)S(1)}, u32[]{:S(2)}, u32[]{:S(2)}) collective-permute-start(f32[8848]{0:T(1024)S(1)} %add.159), channel_id=1, source_target_pairs={{0,4},{1,5},{2,6},{3,7},{4,0},{5,1},{6,2},{7,3},{8,12},{9,13},{10,... | collective-permute-start | bytes 106184 | tf_op jit(solution)/shard_map/ppermute | solution.py:591
  102.4 4.0 %collective-permute-start.50 = (f32[8848]{0:T(1024)S(1)}, f32[8848]{0:T(1024)S(1)}, u32[]{:S(2)}, u32[]{:S(2)}) collective-permute-start(f32[8848]{0:T(1024)S(1)} %add.160), channel_id=1, source_target_pairs={{0,8},{1,9},{2,10},{3,11},{4,12},{5,13},{6,14},{7,15},{8,0},{9,1},... | collective-permute-start | bytes 106184 | tf_op jit(solution)/shard_map/ppermute | solution.py:591
  102.9 6.9 %collective-permute-start.36 = (bf16[8,64,512]{2,1,0:T(8,128)(2,1)S(1)}, bf16[8,64,512]{2,1,0:T(8,128)(2,1)S(1)}, u32[]{:S(2)}, u32[]{:S(2)}) collective-permute-start(bf16[8,64,512]{2,1,0:T(8,128)(2,1)S(1)} %copy-done.40), channel_id=1, source_target_pairs={{0,1},{1,0},{2,3},{3,2},{4,5},{5,4},{6,7},{7,6},{8,9},{9,8},{10,11... | collective-permute-start | bytes 1572872 | tf_op jit(solution)/shard_map/ppermute | solution.py:591
  102.9 4.9 %collective-permute-start.37 = (bf16[8,64,512]{2,1,0:T(8,128)(2,1)S(1)}, bf16[8,64,512]{2,1,0:T(8,128)(2,1)S(1)}, u32[]{:S(2)}, u32[]{:S(2)}) collective-permute-start(bf16[8,64,512]{2,1,0:T(8,128)(2,1)S(1)} %copy-done.42), channel_id=1, source_target_pairs={{0,1},{1,0},{2,3},{3,2},{4,5},{5,4},{6,7},{7,6},{8,9},{9,8},{10,11... | collective-permute-start | bytes 1572872 | tf_op jit(solution)/shard_map/ppermute | solution.py:591
  106.4 4.1 %collective-permute-start.41 = (bf16[8,64,512]{2,1,0:T(8,128)(2,1)S(1)}, bf16[8,64,512]{2,1,0:T(8,128)(2,1)S(1)}, u32[]{:S(2)}, u32[]{:S(2)}) collective-permute-start(bf16[8,64,512]{2,1,0:T(8,128)(2,1)S(1)} %copy-done.39), channel_id=1, source_target_pairs={{0,1},{1,0},{2,3},{3,2},{4,5},{5,4},{6,7},{7,6},{8,9},{9,8},{10,11... | collective-permute-start | bytes 1572872 | tf_op jit(solution)/shard_map/ppermute | solution.py:591
  107.2 31.5 %collective-permute-start.51 = (f32[8848]{0:T(1024)S(1)}, f32[8848]{0:T(1024)S(1)}, u32[]{:S(2)}, u32[]{:S(2)}) collective-permute-start(f32[8848]{0:T(1024)S(1)} %add.161), channel_id=1, source_target_pairs={{0,16},{1,17},{2,18},{3,19},{4,20},{5,21},{6,22},{7,23},{8,24},{9,... | collective-permute-start | bytes 106184 | tf_op jit(solution)/shard_map/ppermute | solution.py:591
  107.8 13.6 %collective-permute-start.33 = (bf16[8,64,512]{2,1,0:T(8,128)(2,1)S(1)}, bf16[8,64,512]{2,1,0:T(8,128)(2,1)S(1)}, u32[]{:S(2)}, u32[]{:S(2)}) collective-permute-start(bf16[8,64,512]{2,1,0:T(8,128)(2,1)S(1)} %add_convert_fusion.4), channel_id=1, source_target_pairs={{0,2},{1,3},{2,0},{3,1},{4,6},{5,7},{6,4},{7,5},{8,10},{9,11},{10,... | collective-permute-start | bytes 1572872 | tf_op jit(solution)/shard_map/ppermute | solution.py:591
  109.1 14.0 %collective-permute-start.38 = (bf16[8,64,512]{2,1,0:T(8,128)(2,1)S(1)}, bf16[8,64,512]{2,1,0:T(8,128)(2,1)S(1)}, u32[]{:S(2)}, u32[]{:S(2)}) collective-permute-start(bf16[8,64,512]{2,1,0:T(8,128)(2,1)S(1)} %add_convert_fusion.2), channel_id=1, source_target_pairs={{0,4},{1,5},{2,6},{3,7},{4,0},{5,1},{6,2},{7,3},{8,12},{9,13},{10,... | collective-permute-start | bytes 1572872 | tf_op jit(solution)/shard_map/ppermute | solution.py:591
  109.8 13.9 %collective-permute-start.43 = (bf16[8,64,512]{2,1,0:T(8,128)(2,1)S(1)}, bf16[8,64,512]{2,1,0:T(8,128)(2,1)S(1)}, u32[]{:S(2)}, u32[]{:S(2)}) collective-permute-start(bf16[8,64,512]{2,1,0:T(8,128)(2,1)S(1)} %add_convert_fusion), channel_id=1, source_target_pairs={{0,8},{1,9},{2,10},{3,11},{4,12},{5,13},{6,14},{7,15},{8,0},{9,1},... | collective-permute-start | bytes 1572872 | tf_op jit(solution)/shard_map/ppermute | solution.py:591
  121.6 7.2 %collective-permute-start.34 = (bf16[4,64,512]{2,1,0:T(8,128)(2,1)S(1)}, bf16[4,64,512]{2,1,0:T(8,128)(2,1)S(1)}, u32[]{:S(2)}, u32[]{:S(2)}) collective-permute-start(bf16[4,64,512]{2,1,0:T(8,128)(2,1)S(1)} %get-tuple-element.67), channel_id=1, source_target_pairs={{0,4},{1,5},{2,6},{3,7},{4,0},{5,1},{6,2},{7,3},{8,12},{9,13},{10,... | collective-permute-start | bytes 786440 | tf_op jit(solution)/shard_map/ppermute | solution.py:591
  123.2 8.7 %collective-permute-start.39 = (bf16[4,64,512]{2,1,0:T(8,128)(2,1)S(1)}, bf16[4,64,512]{2,1,0:T(8,128)(2,1)S(1)}, u32[]{:S(2)}, u32[]{:S(2)}) collective-permute-start(bf16[4,64,512]{2,1,0:T(8,128)(2,1)S(1)} %get-tuple-element.69), channel_id=1, source_target_pairs={{0,8},{1,9},{2,10},{3,11},{4,12},{5,13},{6,14},{7,15},{8,0},{9,1},... | collective-permute-start | bytes 786440 | tf_op jit(solution)/shard_map/ppermute | solution.py:591
  123.8 8.2 %collective-permute-start.44 = (bf16[4,64,512]{2,1,0:T(8,128)(2,1)S(1)}, bf16[4,64,512]{2,1,0:T(8,128)(2,1)S(1)}, u32[]{:S(2)}, u32[]{:S(2)}) collective-permute-start(bf16[4,64,512]{2,1,0:T(8,128)(2,1)S(1)} %get-tuple-element.71), channel_id=1, source_target_pairs={{0,2},{1,3},{2,0},{3,1},{4,6},{5,7},{6,4},{7,5},{8,10},{9,11},{10,... | collective-permute-start | bytes 786440 | tf_op jit(solution)/shard_map/ppermute | solution.py:591
  128.8 5.0 %collective-permute-start.35 = (bf16[2,64,512]{2,1,0:T(8,128)(2,1)S(1)}, bf16[2,64,512]{2,1,0:T(8,128)(2,1)S(1)}, u32[]{:S(2)}, u32[]{:S(2)}) collective-permute-start(bf16[2,64,512]{2,1,0:T(8,128)(2,1)S(1)} %get-tuple-element.76), channel_id=1, source_target_pairs={{0,8},{1,9},{2,10},{3,11},{4,12},{5,13},{6,14},{7,15},{8,0},{9,1},... | collective-permute-start | bytes 393224 | tf_op jit(solution)/shard_map/ppermute | solution.py:591
  132.0 5.0 %collective-permute-start.40 = (bf16[2,64,512]{2,1,0:T(8,128)(2,1)S(1)}, bf16[2,64,512]{2,1,0:T(8,128)(2,1)S(1)}, u32[]{:S(2)}, u32[]{:S(2)}) collective-permute-start(bf16[2,64,512]{2,1,0:T(8,128)(2,1)S(1)} %get-tuple-element.78), channel_id=1, source_target_pairs={{0,2},{1,3},{2,0},{3,1},{4,6},{5,7},{6,4},{7,5},{8,10},{9,11},{10,... | collective-permute-start | bytes 393224 | tf_op jit(solution)/shard_map/ppermute | solution.py:591
  132.2 5.0 %collective-permute-start.45 = (bf16[2,64,512]{2,1,0:T(8,128)(2,1)S(1)}, bf16[2,64,512]{2,1,0:T(8,128)(2,1)S(1)}, u32[]{:S(2)}, u32[]{:S(2)}) collective-permute-start(bf16[2,64,512]{2,1,0:T(8,128)(2,1)S(1)} %get-tuple-element.80), channel_id=1, source_target_pairs={{0,4},{1,5},{2,6},{3,7},{4,0},{5,1},{6,2},{7,3},{8,12},{9,13},{10,... | collective-permute-start | bytes 393224 | tf_op jit(solution)/shard_map/ppermute | solution.py:591
  137.3 8.7 %collective-permute-start.46 = (bf16[3,64,512]{2,1,0:T(8,128)(2,1)S(1)}, bf16[3,64,512]{2,1,0:T(8,128)(2,1)S(1)}, u32[]{:S(2)}, u32[]{:S(2)}) collective-permute-start(bf16[3,64,512]{2,1,0:T(8,128)(2,1)S(1)} %pad_maximum_fusion.7), channel_id=1, source_target_pairs={{0,16},{1,17},{2,18},{3,19},{4,20},{5,21},{6,22},{7,23},{8,24},{9,... | collective-permute-start | bytes 589832 | tf_op jit(solution)/shard_map/ppermute | solution.py:591
  (48 other events, 509.3 us)

commit v2 on v1

--- a/solution.py
+++ b/solution.py
@@ -240,7 +240,7 @@
                 mixed[at, lanes] = join_heads(t_dot(low, qkv[2, at, lanes])).astype(bf16)
             return carry
 
-        lax.fori_loop(0, WINDOWS, attend, 0)
+        lax.fori_loop(0, WINDOWS, attend, 0, unroll=True)
 
         resid[...] = xw[...] + (dot(mixed[...], proj_block()) + bias_proj)
 
@@ -269,7 +269,7 @@
                 return total + col_sum(back)
 
             sums[pl.ds(8 + j, 1), :] = lax.fori_loop(
-                0, ROWS // 32, gelu_part, jnp.zeros((1, D), f32), unroll=2
+                0, ROWS // 32, gelu_part, jnp.zeros((1, D), f32), unroll=True
             )
             forward = dot(act[...], down_block(j))
             backward = dot_t(grow[...], up_block(j))
@@ -293,7 +293,7 @@
             )
             return carry
 
-        lax.fori_loop(0, FF // D, feed, 0)
+        lax.fori_loop(0, FF // D, feed, 0, unroll=True)
 
         def second_back(number, carry):
             gain_sum, shift_sum, resid_sum, cot_sum = carry
@@ -316,7 +316,7 @@
 
         zero_row = jnp.zeros((1, D), f32)
         sums[1:2, :], sums[6:7, :], sums[5:6, :], sums[7:8, :] = lax.fori_loop(
-            0, ROWS // 32, second_back, (zero_row,) * 4, unroll=4
+            0, ROWS // 32, second_back, (zero_row,) * 4, unroll=True
         )
         result = t_dot(perm[...], act[...]).astype(bf16)
         for row in range(SIDE):
@@ -351,7 +351,7 @@
                 dqkv[2, at, lanes] = value_grad.astype(bf16)
             return carry
 
-        lax.fori_loop(0, WINDOWS, attend_back, 0)
+        lax.fori_loop(0, WINDOWS, attend_back, 0, unroll=True)
 
         for part in range(3):
             part_grad = t_dot(in_one[...], dqkv[part]).astype(bf16)
@@ -384,7 +384,7 @@
             return gain_sum + col_sum(incoming * normed), shift_sum + col_sum(incoming)
 
         sums[0:1, :], sums[2:3, :] = lax.fori_loop(
-            0, ROWS // 32, first_back, (zero_row,) * 2, unroll=4
+            0, ROWS // 32, first_back, (zero_row,) * 2, unroll=True
         )
         result = t_dot(perm[...], act[...]).astype(bf16)
         for row in range(SIDE):
@@ -716,6 +716,7 @@
         parts = [jnp.concatenate(near), swap(jnp.concatenate(far), top)]
         for bit in bits:
             small_grad = small_grad + swap(small_grad, bit)
+        parts = [pltpu.with_memory_space_constraint(piece, pltpu.VMEM) for piece in parts]
         owned_grad, new_matrices, new_matrix_m, new_matrix_v = adam_shard(
             kinds, parts, matrices, matrix_m, matrix_v, grad_scale
         )

time: 150 us -> 142 us (0.947)
  Pallas kernels: 29.8 us -> 22.6 us
    pallas_call x1, Pallas kernels: 24.9 us -> 17.9 us  [run_layer(): pl.pallas_call(layer_kernel(counts, outs), in_specs=[smem, smem] + [vmem]...]
where the time goes in v2:
time: 142 us
  waiting for transfers between devices  68.4 us (48%)
  starting transfers between devices  34.2 us (24%)
  Pallas kernels  22.6 us (16%)
  local copies, waits for them, and re-layouts  7.13 us (5%)
  other arithmetic  4.74 us (3%)
  matrix products  3.36 us (2%)
  between operations  1.47 us (1%)
    ppermute x52, waiting for transfers between devices, swap(): return lax.ppermute(value, AXES, [(i, i ^ bit) for i in range(devices)])  68.4 us
    ppermute x52, starting transfers between devices, swap(): return lax.ppermute(value, AXES, [(i, i ^ bit) for i in range(devices)])  34.2 us
    pallas_call x1, Pallas kernels, run_layer(): pl.pallas_call(layer_kernel(counts, outs), in_specs=[smem, smem] + [vmem]...  17.9 us
    pallas_call x1, Pallas kernels, adam_shard(): pl.pallas_call(adam_kernel(grad_scale), in_specs=[pl.BlockSpec(memory_spa...  2.94 us
  transfers between devices with their start and end apart: 52, of which 24 were waited for; matrix products, arithmetic and copies ran while one was open for 7% of the time, Pallas kernels for 0%

profile of v2, /device:TPU:0, one launch (start us, length us, event | category | flops | bytes accessed | tf_op | source)
XLA Modules:
  0.0 141.9 jit_solution(5194794250673457791)
XLA Ops:
  1.2 1.8 %pack.1 = bf16[3,64,512]{2,1,0:T(8,128)(2,1)} custom-call(s32[3]{0:T(128)} %compare_select_fusion.kinds, f32[768,128]{1,0:T(8,128)} %bitcast.26), custom_call_target="tpu_custom_call" | custom-call | tf_op jit(solution)/shard_map/pack/pallas_call | solution.py:485
  3.1 4.2 %collective-permute-start = (bf16[3,64,512]{2,1,0:T(8,128)(2,1)}, bf16[3,64,512]{2,1,0:T(8,128)(2,1)S(1)}, u32[]{:S(2)}, u32[]{:S(2)}) collective-permute-start(bf16[3,64,512]{2,1,0:T(8,128)(2,1)} %pack.1), channel_id=1, source_target_pairs={{0,16},{1,17},{2,18},{3,19},{4,20},{5,21},{6,22},{7,23},{8,24},{9,... | collective-permute-start | bytes 589832 | tf_op jit(solution)/shard_map/ppermute | solution.py:591
  7.2 0.9 fusion.27
  8.1 1.6 %collective-permute-start.11 = (bf16[1,64,512]{2,1,0:T(8,128)(2,1)S(1)}, bf16[1,64,512]{2,1,0:T(8,128)(2,1)S(1)}, u32[]{:S(2)}, u32[]{:S(2)}) collective-permute-start(bf16[1,64,512]{2,1,0:T(8,128)(2,1)S(1)} %get-tuple-element.90), channel_id=1, source_target_pairs={{0,4},{1,5},{2,6},{3,7},{4,0},{5,1},{6,2},{7,3},{8,12},{9,13},{10,... | collective-permute-start | bytes 196616 | tf_op jit(solution)/shard_map/ppermute | solution.py:591
  9.7 1.4 %collective-permute-start.6 = (bf16[1,64,512]{2,1,0:T(8,128)(2,1)S(1)}, bf16[1,64,512]{2,1,0:T(8,128)(2,1)S(1)}, u32[]{:S(2)}, u32[]{:S(2)}) collective-permute-start(bf16[1,64,512]{2,1,0:T(8,128)(2,1)S(1)} %get-tuple-element.91), channel_id=1, source_target_pairs={{0,2},{1,3},{2,0},{3,1},{4,6},{5,7},{6,4},{7,5},{8,10},{9,11},{10,... | collective-permute-start | bytes 196616 | tf_op jit(solution)/shard_map/ppermute | solution.py:591
  11.1 1.6 %collective-permute-start.1 = (bf16[1,64,512]{2,1,0:T(8,128)(2,1)S(1)}, bf16[1,64,512]{2,1,0:T(8,128)(2,1)S(1)}, u32[]{:S(2)}, u32[]{:S(2)}) collective-permute-start(bf16[1,64,512]{2,1,0:T(8,128)(2,1)S(1)} %get-tuple-element.92), channel_id=1, source_target_pairs={{0,8},{1,9},{2,10},{3,11},{4,12},{5,13},{6,14},{7,15},{8,0},{9,1},... | collective-permute-start | bytes 196616 | tf_op jit(solution)/shard_map/ppermute | solution.py:591
  12.7 0.7 slice.153
  13.4 0.8 reshape.104
  14.5 1.0 reduce-precision_convert_fusion.3
  15.5 0.8 compare_convert_fusion.refs_7_
  16.3 1.2 fusion.1
  18.8 0.9 reshape.103.refs_6_
  21.5 3.2 %collective-permute-done.2 = bf16[2,64,512]{2,1,0:T(8,128)(2,1)S(1)} collective-permute-done((bf16[2,64,512]{2,1,0:T(8,128)(2,1)S(1)}, bf16[2,64,512]{2,1,0:T(8,128)(2,1)S(1)}, u32[]{:S(2)}, u32[]{:S(2)}) %collective-permute-start.2) | collective-permute-done | bytes 131104 | tf_op jit(solution)/shard_map/ppermute | solution.py:591
  26.1 1.4 %collective-permute-start.26 = (bf16[1,64,512]{2,1,0:T(8,128)(2,1)S(1)}, bf16[1,64,512]{2,1,0:T(8,128)(2,1)S(1)}, u32[]{:S(2)}, u32[]{:S(2)}) collective-permute-start(bf16[1,64,512]{2,1,0:T(8,128)(2,1)S(1)} %get-tuple-element.87), channel_id=1, source_target_pairs={{0,4},{1,5},{2,6},{3,7},{4,0},{5,1},{6,2},{7,3},{8,12},{9,13},{10,... | collective-permute-start | bytes 196616 | tf_op jit(solution)/shard_map/ppermute | solution.py:591
  27.6 2.2 %collective-permute-done.16 = bf16[1,64,512]{2,1,0:T(8,128)(2,1)S(1)} collective-permute-done((bf16[1,64,512]{2,1,0:T(8,128)(2,1)S(1)}, bf16[1,64,512]{2,1,0:T(8,128)(2,1)S(1)}, u32[]{:S(2)}, u32[]{:S(2)}) %collective-permute-start.16) | collective-permute-done | bytes 65568 | tf_op jit(solution)/shard_map/ppermute | solution.py:591
  29.8 1.5 %collective-permute-start.21 = (bf16[1,64,512]{2,1,0:T(8,128)(2,1)S(1)}, bf16[1,64,512]{2,1,0:T(8,128)(2,1)S(1)}, u32[]{:S(2)}, u32[]{:S(2)}) collective-permute-start(bf16[1,64,512]{2,1,0:T(8,128)(2,1)S(1)} %get-tuple-element.88), channel_id=1, source_target_pairs={{0,2},{1,3},{2,0},{3,1},{4,6},{5,7},{6,4},{7,5},{8,10},{9,11},{10,... | collective-permute-start | bytes 196616 | tf_op jit(solution)/shard_map/ppermute | solution.py:591
  31.3 3.7 %collective-permute-done.21 = bf16[1,64,512]{2,1,0:T(8,128)(2,1)S(1)} collective-permute-done((bf16[1,64,512]{2,1,0:T(8,128)(2,1)S(1)}, bf16[1,64,512]{2,1,0:T(8,128)(2,1)S(1)}, u32[]{:S(2)}, u32[]{:S(2)}) %collective-permute-start.21) | collective-permute-done | bytes 65568 | tf_op jit(solution)/shard_map/ppermute | solution.py:591
  36.3 3.6 %collective-permute-done.17 = bf16[2,64,512]{2,1,0:T(8,128)(2,1)S(1)} collective-permute-done((bf16[2,64,512]{2,1,0:T(8,128)(2,1)S(1)}, bf16[2,64,512]{2,1,0:T(8,128)(2,1)S(1)}, u32[]{:S(2)}, u32[]{:S(2)}) %collective-permute-start.17) | collective-permute-done | bytes 131104 | tf_op jit(solution)/shard_map/ppermute | solution.py:591
  40.5 1.1 collective-permute-done.27
  41.6 1.5 %collective-permute-start.8 = (bf16[4,64,512]{2,1,0:T(8,128)(2,1)S(1)}, bf16[4,64,512]{2,1,0:T(8,128)(2,1)S(1)}, u32[]{:S(2)}, u32[]{:S(2)}) collective-permute-start(bf16[4,64,512]{2,1,0:T(8,128)(2,1)S(1)} %pad_maximum_fusion.1.refs_12_), channel_id=1, source_target_pairs={{0,4},{1,5},{2,6},{3,7},{4,0},{5,1},{6,2},{7,3},{8,12},{9,13},{10,... | collective-permute-start | bytes 786440 | tf_op jit(solution)/shard_map/ppermute | solution.py:591
  43.1 1.8 %collective-permute-done.22 = bf16[2,64,512]{2,1,0:T(8,128)(2,1)S(1)} collective-permute-done((bf16[2,64,512]{2,1,0:T(8,128)(2,1)S(1)}, bf16[2,64,512]{2,1,0:T(8,128)(2,1)S(1)}, u32[]{:S(2)}, u32[]{:S(2)}) %collective-permute-start.22) | collective-permute-done | bytes 131104 | tf_op jit(solution)/shard_map/ppermute | solution.py:591
  46.3 3.1 %collective-permute-done.8.refs_13_ = bf16[4,64,512]{2,1,0:T(8,128)(2,1)S(1)} collective-permute-done((bf16[4,64,512]{2,1,0:T(8,128)(2,1)S(1)}, bf16[4,64,512]{2,1,0:T(8,128)(2,1)S(1)}, u32[]{:S(2)}, u32[]{:S(2)}) %collective-permute-start.8) | collective-permute-done | bytes 262176 | tf_op jit(solution)/shard_map/ppermute | solution.py:591
  49.5 1.6 %collective-permute-start.23 = (bf16[4,64,512]{2,1,0:T(8,128)(2,1)S(1)}, bf16[4,64,512]{2,1,0:T(8,128)(2,1)S(1)}, u32[]{:S(2)}, u32[]{:S(2)}) collective-permute-start(bf16[4,64,512]{2,1,0:T(8,128)(2,1)S(1)} %pad_maximum_fusion.4.refs_24_), channel_id=1, source_target_pairs={{0,4},{1,5},{2,6},{3,7},{4,0},{5,1},{6,2},{7,3},{8,12},{9,13},{10,... | collective-permute-start | bytes 786440 | tf_op jit(solution)/shard_map/ppermute | solution.py:591
  51.0 2.6 %collective-permute-done.13.refs_17_ = bf16[4,64,512]{2,1,0:T(8,128)(2,1)S(1)} collective-permute-done((bf16[4,64,512]{2,1,0:T(8,128)(2,1)S(1)}, bf16[4,64,512]{2,1,0:T(8,128)(2,1)S(1)}, u32[]{:S(2)}, u32[]{:S(2)}) %collective-permute-start.13) | collective-permute-done | bytes 262176 | tf_op jit(solution)/shard_map/ppermute | solution.py:591
  54.7 3.5 %collective-permute-done.23.refs_25_ = bf16[4,64,512]{2,1,0:T(8,128)(2,1)S(1)} collective-permute-done((bf16[4,64,512]{2,1,0:T(8,128)(2,1)S(1)}, bf16[4,64,512]{2,1,0:T(8,128)(2,1)S(1)}, u32[]{:S(2)}, u32[]{:S(2)}) %collective-permute-start.23) | collective-permute-done | bytes 262176 | tf_op jit(solution)/shard_map/ppermute | solution.py:591
  58.7 3.7 %collective-permute-done.28.refs_29_ = bf16[4,64,512]{2,1,0:T(8,128)(2,1)S(1)} collective-permute-done((bf16[4,64,512]{2,1,0:T(8,128)(2,1)S(1)}, bf16[4,64,512]{2,1,0:T(8,128)(2,1)S(1)}, u32[]{:S(2)}, u32[]{:S(2)}) %collective-permute-start.28) | collective-permute-done | bytes 262176 | tf_op jit(solution)/shard_map/ppermute | solution.py:591
  62.9 1.0 collective-permute-done.25.refs_27_
  64.0 0.7 copy-done.28
  64.8 17.9 %layer.1 = (bf16[1,14,14,512]{3,2,1,0:T(8,128)(2,1)}, bf16[1,14,14,512]{3,2,1,0:T(8,128)(2,1)}, f32[12,512]{1,0:T(8,128)}, f32[64,1024]{1,0:T(8,128)}, bf16[8,64...) custom-call(s32[96]{0:T(128)} %get-tuple-element.36.refs_0_, ...), custom_call_target="tpu_custom_call" | custom-call | tf_op jit(solution)/shard_map/layer/pallas_call | solution.py:404
  82.7 0.8 reshape.109
  83.4 1.1 reshape.110
  84.7 0.8 fusion
  88.1 3.4 %collective-permute-done.48 = f32[8848]{0:T(1024)S(1)} collective-permute-done((f32[8848]{0:T(1024)S(1)}, f32[8848]{0:T(1024)S(1)}, u32[]{:S(2)}, u32[]{:S(2)}) %collective-permute-start.48) | collective-permute-done | bytes 35424 | tf_op jit(solution)/shard_map/ppermute | solution.py:591
  92.0 3.4 %collective-permute-done.49 = f32[8848]{0:T(1024)S(1)} collective-permute-done((f32[8848]{0:T(1024)S(1)}, f32[8848]{0:T(1024)S(1)}, u32[]{:S(2)}, u32[]{:S(2)}) %collective-permute-start.49) | collective-permute-done | bytes 35424 | tf_op jit(solution)/shard_map/ppermute | solution.py:591
  96.4 3.0 %collective-permute-done.50 = f32[8848]{0:T(1024)S(1)} collective-permute-done((f32[8848]{0:T(1024)S(1)}, f32[8848]{0:T(1024)S(1)}, u32[]{:S(2)}, u32[]{:S(2)}) %collective-permute-start.50) | collective-permute-done | bytes 35424 | tf_op jit(solution)/shard_map/ppermute | solution.py:591
  103.8 10.7 %collective-permute-done.33 = bf16[8,64,512]{2,1,0:T(8,128)(2,1)S(1)} collective-permute-done((bf16[8,64,512]{2,1,0:T(8,128)(2,1)S(1)}, bf16[8,64,512]{2,1,0:T(8,128)(2,1)S(1)}, u32[]{:S(2)}, u32[]{:S(2)}) %collective-permute-start.33) | collective-permute-done | bytes 524320 | tf_op jit(solution)/shard_map/ppermute | solution.py:591
  115.1 0.9 collective-permute-done.38
  116.8 1.2 collective-permute-start.44
  118.0 3.7 %collective-permute-done.34 = bf16[4,64,512]{2,1,0:T(8,128)(2,1)S(1)} collective-permute-done((bf16[4,64,512]{2,1,0:T(8,128)(2,1)S(1)}, bf16[4,64,512]{2,1,0:T(8,128)(2,1)S(1)}, u32[]{:S(2)}, u32[]{:S(2)}) %collective-permute-start.34) | collective-permute-done | bytes 262176 | tf_op jit(solution)/shard_map/ppermute | solution.py:591
  121.8 1.3 collective-permute-start.35
  123.1 1.8 %collective-permute-done.39 = bf16[4,64,512]{2,1,0:T(8,128)(2,1)S(1)} collective-permute-done((bf16[4,64,512]{2,1,0:T(8,128)(2,1)S(1)}, bf16[4,64,512]{2,1,0:T(8,128)(2,1)S(1)}, u32[]{:S(2)}, u32[]{:S(2)}) %collective-permute-start.39) | collective-permute-done | bytes 262176 | tf_op jit(solution)/shard_map/ppermute | solution.py:591
  125.1 0.7 collective-permute-start.45
  125.8 1.0 collective-permute-done.35
  126.9 3.1 %collective-permute-done.40 = bf16[2,64,512]{2,1,0:T(8,128)(2,1)S(1)} collective-permute-done((bf16[2,64,512]{2,1,0:T(8,128)(2,1)S(1)}, bf16[2,64,512]{2,1,0:T(8,128)(2,1)S(1)}, u32[]{:S(2)}, u32[]{:S(2)}) %collective-permute-start.40) | collective-permute-done | bytes 131104 | tf_op jit(solution)/shard_map/ppermute | solution.py:591
  130.2 1.4 collective-permute-start.46
  131.7 0.7 multiply_subtract_fusion
  132.4 6.6 %collective-permute-done.46.refs_1_ = bf16[3,64,512]{2,1,0:T(8,128)(2,1)S(1)} collective-permute-done((bf16[3,64,512]{2,1,0:T(8,128)(2,1)S(1)}, bf16[3,64,512]{2,1,0:T(8,128)(2,1)S(1)}, u32[]{:S(2)}, u32[]{:S(2)}) %collective-permute-start.46) | collective-permute-done | bytes 196640 | tf_op jit(solution)/shard_map/ppermute | solution.py:591
  139.0 2.9 %adam.1 = (f32[768,128]{1,0:T(8,128)}, f32[768,128]{1,0:T(8,128)}, f32[768,128]{1,0:T(8,128)}, f32[768,128]{1,0:T(8,128)}) custom-call(s32[3]{0:T(128)} %compare_select_fusion.kinds, bf16[3,64,512]{2,1,0:T(8,128)(2,1)S(1)} %pad_maximum_fusion.6.refs_0_, bf16[3,64,512]{2,1,0:T(8,128)(2,1)S(1)} %collective-permute-done.46.refs_1_, f32[768,128]{1,0:T(8,128)} %bitcast.27, ...), custom_call_target="tpu_custom_call" | custom-call | tf_op jit(solution)/shard_map/adam/pallas_call | solution.py:536
  (205 shorter events, 21.1 us)
Async XLA Ops:
  3.1 22.4 %collective-permute-start = (bf16[3,64,512]{2,1,0:T(8,128)(2,1)}, bf16[3,64,512]{2,1,0:T(8,128)(2,1)S(1)}, u32[]{:S(2)}, u32[]{:S(2)}) collective-permute-start(bf16[3,64,512]{2,1,0:T(8,128)(2,1)} %pack.1), channel_id=1, source_target_pairs={{0,16},{1,17},{2,18},{3,19},{4,20},{5,21},{6,22},{7,23},{8,24},{9,... | collective-permute-start | bytes 589832 | tf_op jit(solution)/shard_map/ppermute | solution.py:591
  8.1 12.2 %collective-permute-start.11 = (bf16[1,64,512]{2,1,0:T(8,128)(2,1)S(1)}, bf16[1,64,512]{2,1,0:T(8,128)(2,1)S(1)}, u32[]{:S(2)}, u32[]{:S(2)}) collective-permute-start(bf16[1,64,512]{2,1,0:T(8,128)(2,1)S(1)} %get-tuple-element.90), channel_id=1, source_target_pairs={{0,4},{1,5},{2,6},{3,7},{4,0},{5,1},{6,2},{7,3},{8,12},{9,13},{10,... | collective-permute-start | bytes 196616 | tf_op jit(solution)/shard_map/ppermute | solution.py:591
  9.7 11.2 %collective-permute-start.6 = (bf16[1,64,512]{2,1,0:T(8,128)(2,1)S(1)}, bf16[1,64,512]{2,1,0:T(8,128)(2,1)S(1)}, u32[]{:S(2)}, u32[]{:S(2)}) collective-permute-start(bf16[1,64,512]{2,1,0:T(8,128)(2,1)S(1)} %get-tuple-element.91), channel_id=1, source_target_pairs={{0,2},{1,3},{2,0},{3,1},{4,6},{5,7},{6,4},{7,5},{8,10},{9,11},{10,... | collective-permute-start | bytes 196616 | tf_op jit(solution)/shard_map/ppermute | solution.py:591
  11.1 8.6 %collective-permute-start.1 = (bf16[1,64,512]{2,1,0:T(8,128)(2,1)S(1)}, bf16[1,64,512]{2,1,0:T(8,128)(2,1)S(1)}, u32[]{:S(2)}, u32[]{:S(2)}) collective-permute-start(bf16[1,64,512]{2,1,0:T(8,128)(2,1)S(1)} %get-tuple-element.92), channel_id=1, source_target_pairs={{0,8},{1,9},{2,10},{3,11},{4,12},{5,13},{6,14},{7,15},{8,0},{9,1},... | collective-permute-start | bytes 196616 | tf_op jit(solution)/shard_map/ppermute | solution.py:591
  19.7 5.0 %collective-permute-start.2 = (bf16[2,64,512]{2,1,0:T(8,128)(2,1)S(1)}, bf16[2,64,512]{2,1,0:T(8,128)(2,1)S(1)}, u32[]{:S(2)}, u32[]{:S(2)}) collective-permute-start(bf16[2,64,512]{2,1,0:T(8,128)(2,1)S(1)} %pad_maximum_fusion.8), channel_id=1, source_target_pairs={{0,4},{1,5},{2,6},{3,7},{4,0},{5,1},{6,2},{7,3},{8,12},{9,13},{10,... | collective-permute-start | bytes 393224 | tf_op jit(solution)/shard_map/ppermute | solution.py:591
  20.3 15.3 %collective-permute-start.12 = (bf16[2,64,512]{2,1,0:T(8,128)(2,1)S(1)}, bf16[2,64,512]{2,1,0:T(8,128)(2,1)S(1)}, u32[]{:S(2)}, u32[]{:S(2)}) collective-permute-start(bf16[2,64,512]{2,1,0:T(8,128)(2,1)S(1)} %pad_maximum_fusion.10), channel_id=1, source_target_pairs={{0,2},{1,3},{2,0},{3,1},{4,6},{5,7},{6,4},{7,5},{8,10},{9,11},{10,... | collective-permute-start | bytes 393224 | tf_op jit(solution)/shard_map/ppermute | solution.py:591
  20.9 5.1 %collective-permute-start.7 = (bf16[2,64,512]{2,1,0:T(8,128)(2,1)S(1)}, bf16[2,64,512]{2,1,0:T(8,128)(2,1)S(1)}, u32[]{:S(2)}, u32[]{:S(2)}) collective-permute-start(bf16[2,64,512]{2,1,0:T(8,128)(2,1)S(1)} %pad_maximum_fusion.9), channel_id=1, source_target_pairs={{0,8},{1,9},{2,10},{3,11},{4,12},{5,13},{6,14},{7,15},{8,0},{9,1},... | collective-permute-start | bytes 393224 | tf_op jit(solution)/shard_map/ppermute | solution.py:591
  24.8 20.1 %collective-permute-start.4 = (bf16[4,64,512]{2,1,0:T(8,128)(2,1)S(1)}, bf16[4,64,512]{2,1,0:T(8,128)(2,1)S(1)}, u32[]{:S(2)}, u32[]{:S(2)}) collective-permute-start(bf16[4,64,512]{2,1,0:T(8,128)(2,1)S(1)} %pad_maximum_fusion.refs_8_), channel_id=1, source_target_pairs={{0,1},{1,0},{2,3},{3,2},{4,5},{5,4},{6,7},{7,6},{8,9},{9,8},{10,11... | collective-permute-start | bytes 786440 | tf_op jit(solution)/shard_map/ppermute | solution.py:591
  24.9 20.6 %collective-permute-start.3 = (bf16[4,64,512]{2,1,0:T(8,128)(2,1)S(1)}, bf16[4,64,512]{2,1,0:T(8,128)(2,1)S(1)}, u32[]{:S(2)}, u32[]{:S(2)}) collective-permute-start(bf16[4,64,512]{2,1,0:T(8,128)(2,1)S(1)} %pad_maximum_fusion.refs_8_), channel_id=1, source_target_pairs={{0,2},{1,3},{2,0},{3,1},{4,6},{5,7},{6,4},{7,5},{8,10},{9,11},{10,... | collective-permute-start | bytes 786440 | tf_op jit(solution)/shard_map/ppermute | solution.py:591
  25.5 4.3 %collective-permute-start.16 = (bf16[1,64,512]{2,1,0:T(8,128)(2,1)S(1)}, bf16[1,64,512]{2,1,0:T(8,128)(2,1)S(1)}, u32[]{:S(2)}, u32[]{:S(2)}) collective-permute-start(bf16[1,64,512]{2,1,0:T(8,128)(2,1)S(1)} %get-tuple-element.89), channel_id=1, source_target_pairs={{0,8},{1,9},{2,10},{3,11},{4,12},{5,13},{6,14},{7,15},{8,0},{9,1},... | collective-permute-start | bytes 196616 | tf_op jit(solution)/shard_map/ppermute | solution.py:591
  26.1 9.4 %collective-permute-start.26 = (bf16[1,64,512]{2,1,0:T(8,128)(2,1)S(1)}, bf16[1,64,512]{2,1,0:T(8,128)(2,1)S(1)}, u32[]{:S(2)}, u32[]{:S(2)}) collective-permute-start(bf16[1,64,512]{2,1,0:T(8,128)(2,1)S(1)} %get-tuple-element.87), channel_id=1, source_target_pairs={{0,4},{1,5},{2,6},{3,7},{4,0},{5,1},{6,2},{7,3},{8,12},{9,13},{10,... | collective-permute-start | bytes 196616 | tf_op jit(solution)/shard_map/ppermute | solution.py:591
  29.8 5.2 %collective-permute-start.21 = (bf16[1,64,512]{2,1,0:T(8,128)(2,1)S(1)}, bf16[1,64,512]{2,1,0:T(8,128)(2,1)S(1)}, u32[]{:S(2)}, u32[]{:S(2)}) collective-permute-start(bf16[1,64,512]{2,1,0:T(8,128)(2,1)S(1)} %get-tuple-element.88), channel_id=1, source_target_pairs={{0,2},{1,3},{2,0},{3,1},{4,6},{5,7},{6,4},{7,5},{8,10},{9,11},{10,... | collective-permute-start | bytes 196616 | tf_op jit(solution)/shard_map/ppermute | solution.py:591
  35.0 5.0 %collective-permute-start.17 = (bf16[2,64,512]{2,1,0:T(8,128)(2,1)S(1)}, bf16[2,64,512]{2,1,0:T(8,128)(2,1)S(1)}, u32[]{:S(2)}, u32[]{:S(2)}) collective-permute-start(bf16[2,64,512]{2,1,0:T(8,128)(2,1)S(1)} %pad_maximum_fusion.11), channel_id=1, source_target_pairs={{0,4},{1,5},{2,6},{3,7},{4,0},{5,1},{6,2},{7,3},{8,12},{9,13},{10,... | collective-permute-start | bytes 393224 | tf_op jit(solution)/shard_map/ppermute | solution.py:591
  35.5 10.1 %collective-permute-start.9 = (bf16[4,64,512]{2,1,0:T(8,128)(2,1)S(1)}, bf16[4,64,512]{2,1,0:T(8,128)(2,1)S(1)}, u32[]{:S(2)}, u32[]{:S(2)}) collective-permute-start(bf16[4,64,512]{2,1,0:T(8,128)(2,1)S(1)} %pad_maximum_fusion.1.refs_12_), channel_id=1, source_target_pairs={{0,1},{1,0},{2,3},{3,2},{4,5},{5,4},{6,7},{7,6},{8,9},{9,8},{10,11... | collective-permute-start | bytes 786440 | tf_op jit(solution)/shard_map/ppermute | solution.py:591
  35.6 6.0 %collective-permute-start.27 = (bf16[2,64,512]{2,1,0:T(8,128)(2,1)S(1)}, bf16[2,64,512]{2,1,0:T(8,128)(2,1)S(1)}, u32[]{:S(2)}, u32[]{:S(2)}) collective-permute-start(bf16[2,64,512]{2,1,0:T(8,128)(2,1)S(1)} %pad_maximum_fusion.13), channel_id=1, source_target_pairs={{0,2},{1,3},{2,0},{3,1},{4,6},{5,7},{6,4},{7,5},{8,10},{9,11},{10,... | collective-permute-start | bytes 393224 | tf_op jit(solution)/shard_map/ppermute | solution.py:591
  39.9 5.0 %collective-permute-start.22 = (bf16[2,64,512]{2,1,0:T(8,128)(2,1)S(1)}, bf16[2,64,512]{2,1,0:T(8,128)(2,1)S(1)}, u32[]{:S(2)}, u32[]{:S(2)}) collective-permute-start(bf16[2,64,512]{2,1,0:T(8,128)(2,1)S(1)} %pad_maximum_fusion.12), channel_id=1, source_target_pairs={{0,8},{1,9},{2,10},{3,11},{4,12},{5,13},{6,14},{7,15},{8,0},{9,1},... | collective-permute-start | bytes 393224 | tf_op jit(solution)/shard_map/ppermute | solution.py:591
  41.6 7.8 %collective-permute-start.8 = (bf16[4,64,512]{2,1,0:T(8,128)(2,1)S(1)}, bf16[4,64,512]{2,1,0:T(8,128)(2,1)S(1)}, u32[]{:S(2)}, u32[]{:S(2)}) collective-permute-start(bf16[4,64,512]{2,1,0:T(8,128)(2,1)S(1)} %pad_maximum_fusion.1.refs_12_), channel_id=1, source_target_pairs={{0,4},{1,5},{2,6},{3,7},{4,0},{5,1},{6,2},{7,3},{8,12},{9,13},{10,... | collective-permute-start | bytes 786440 | tf_op jit(solution)/shard_map/ppermute | solution.py:591
  44.9 4.5 %collective-permute-start.14 = (bf16[4,64,512]{2,1,0:T(8,128)(2,1)S(1)}, bf16[4,64,512]{2,1,0:T(8,128)(2,1)S(1)}, u32[]{:S(2)}, u32[]{:S(2)}) collective-permute-start(bf16[4,64,512]{2,1,0:T(8,128)(2,1)S(1)} %pad_maximum_fusion.2.refs_16_), channel_id=1, source_target_pairs={{0,1},{1,0},{2,3},{3,2},{4,5},{5,4},{6,7},{7,6},{8,9},{9,8},{10,11... | collective-permute-start | bytes 786440 | tf_op jit(solution)/shard_map/ppermute | solution.py:591
  44.9 8.7 %collective-permute-start.13 = (bf16[4,64,512]{2,1,0:T(8,128)(2,1)S(1)}, bf16[4,64,512]{2,1,0:T(8,128)(2,1)S(1)}, u32[]{:S(2)}, u32[]{:S(2)}) collective-permute-start(bf16[4,64,512]{2,1,0:T(8,128)(2,1)S(1)} %pad_maximum_fusion.2.refs_16_), channel_id=1, source_target_pairs={{0,8},{1,9},{2,10},{3,11},{4,12},{5,13},{6,14},{7,15},{8,0},{9,1},... | collective-permute-start | bytes 786440 | tf_op jit(solution)/shard_map/ppermute | solution.py:591
  45.4 8.2 %collective-permute-start.19 = (bf16[4,64,512]{2,1,0:T(8,128)(2,1)S(1)}, bf16[4,64,512]{2,1,0:T(8,128)(2,1)S(1)}, u32[]{:S(2)}, u32[]{:S(2)}) collective-permute-start(bf16[4,64,512]{2,1,0:T(8,128)(2,1)S(1)} %pad_maximum_fusion.3.refs_20_), channel_id=1, source_target_pairs={{0,1},{1,0},{2,3},{3,2},{4,5},{5,4},{6,7},{7,6},{8,9},{9,8},{10,11... | collective-permute-start | bytes 786440 | tf_op jit(solution)/shard_map/ppermute | solution.py:591
  45.6 8.6 %collective-permute-start.18 = (bf16[4,64,512]{2,1,0:T(8,128)(2,1)S(1)}, bf16[4,64,512]{2,1,0:T(8,128)(2,1)S(1)}, u32[]{:S(2)}, u32[]{:S(2)}) collective-permute-start(bf16[4,64,512]{2,1,0:T(8,128)(2,1)S(1)} %pad_maximum_fusion.3.refs_20_), channel_id=1, source_target_pairs={{0,2},{1,3},{2,0},{3,1},{4,6},{5,7},{6,4},{7,5},{8,10},{9,11},{10,... | collective-permute-start | bytes 786440 | tf_op jit(solution)/shard_map/ppermute | solution.py:591
  49.5 4.9 %collective-permute-start.24 = (bf16[4,64,512]{2,1,0:T(8,128)(2,1)S(1)}, bf16[4,64,512]{2,1,0:T(8,128)(2,1)S(1)}, u32[]{:S(2)}, u32[]{:S(2)}) collective-permute-start(bf16[4,64,512]{2,1,0:T(8,128)(2,1)S(1)} %pad_maximum_fusion.4.refs_24_), channel_id=1, source_target_pairs={{0,1},{1,0},{2,3},{3,2},{4,5},{5,4},{6,7},{7,6},{8,9},{9,8},{10,11... | collective-permute-start | bytes 786440 | tf_op jit(solution)/shard_map/ppermute | solution.py:591
  49.5 8.7 %collective-permute-start.23 = (bf16[4,64,512]{2,1,0:T(8,128)(2,1)S(1)}, bf16[4,64,512]{2,1,0:T(8,128)(2,1)S(1)}, u32[]{:S(2)}, u32[]{:S(2)}) collective-permute-start(bf16[4,64,512]{2,1,0:T(8,128)(2,1)S(1)} %pad_maximum_fusion.4.refs_24_), channel_id=1, source_target_pairs={{0,4},{1,5},{2,6},{3,7},{4,0},{5,1},{6,2},{7,3},{8,12},{9,13},{10,... | collective-permute-start | bytes 786440 | tf_op jit(solution)/shard_map/ppermute | solution.py:591
  53.6 4.5 %collective-permute-start.29 = (bf16[4,64,512]{2,1,0:T(8,128)(2,1)S(1)}, bf16[4,64,512]{2,1,0:T(8,128)(2,1)S(1)}, u32[]{:S(2)}, u32[]{:S(2)}) collective-permute-start(bf16[4,64,512]{2,1,0:T(8,128)(2,1)S(1)} %pad_maximum_fusion.5.refs_28_), channel_id=1, source_target_pairs={{0,1},{1,0},{2,3},{3,2},{4,5},{5,4},{6,7},{7,6},{8,9},{9,8},{10,11... | collective-permute-start | bytes 786440 | tf_op jit(solution)/shard_map/ppermute | solution.py:591
  53.7 8.7 %collective-permute-start.28 = (bf16[4,64,512]{2,1,0:T(8,128)(2,1)S(1)}, bf16[4,64,512]{2,1,0:T(8,128)(2,1)S(1)}, u32[]{:S(2)}, u32[]{:S(2)}) collective-permute-start(bf16[4,64,512]{2,1,0:T(8,128)(2,1)S(1)} %pad_maximum_fusion.5.refs_28_), channel_id=1, source_target_pairs={{0,8},{1,9},{2,10},{3,11},{4,12},{5,13},{6,14},{7,15},{8,0},{9,1},... | collective-permute-start | bytes 786440 | tf_op jit(solution)/shard_map/ppermute | solution.py:591
  54.2 8.2 %collective-permute-start.5 = (bf16[4,64,512]{2,1,0:T(8,128)(2,1)S(1)}, bf16[4,64,512]{2,1,0:T(8,128)(2,1)S(1)}, u32[]{:S(2)}, u32[]{:S(2)}) collective-permute-start(bf16[4,64,512]{2,1,0:T(8,128)(2,1)S(1)} %collective-permute-done.3.refs_9_), channel_id=1, source_target_pairs={{0,1},{1,0},{2,3},{3,2},{4,5},{5,4},{6,7},{7,6},{8,9},{9,8},{10,11... | collective-permute-start | bytes 786440 | tf_op jit(solution)/shard_map/ppermute | solution.py:591
  54.3 8.6 %collective-permute-start.10 = (bf16[4,64,512]{2,1,0:T(8,128)(2,1)S(1)}, bf16[4,64,512]{2,1,0:T(8,128)(2,1)S(1)}, u32[]{:S(2)}, u32[]{:S(2)}) collective-permute-start(bf16[4,64,512]{2,1,0:T(8,128)(2,1)S(1)} %collective-permute-done.8.refs_13_), channel_id=1, source_target_pairs={{0,1},{1,0},{2,3},{3,2},{4,5},{5,4},{6,7},{7,6},{8,9},{9,8},{10,11... | collective-permute-start | bytes 786440 | tf_op jit(solution)/shard_map/ppermute | solution.py:591
  58.2 4.7 %collective-permute-start.15 = (bf16[4,64,512]{2,1,0:T(8,128)(2,1)S(1)}, bf16[4,64,512]{2,1,0:T(8,128)(2,1)S(1)}, u32[]{:S(2)}, u32[]{:S(2)}) collective-permute-start(bf16[4,64,512]{2,1,0:T(8,128)(2,1)S(1)} %collective-permute-done.13.refs_17_), channel_id=1, source_target_pairs={{0,1},{1,0},{2,3},{3,2},{4,5},{5,4},{6,7},{7,6},{8,9},{9,8},{10,11... | collective-permute-start | bytes 786440 | tf_op jit(solution)/shard_map/ppermute | solution.py:591
  58.2 4.7 %collective-permute-start.20 = (bf16[4,64,512]{2,1,0:T(8,128)(2,1)S(1)}, bf16[4,64,512]{2,1,0:T(8,128)(2,1)S(1)}, u32[]{:S(2)}, u32[]{:S(2)}) collective-permute-start(bf16[4,64,512]{2,1,0:T(8,128)(2,1)S(1)} %collective-permute-done.18.refs_21_), channel_id=1, source_target_pairs={{0,1},{1,0},{2,3},{3,2},{4,5},{5,4},{6,7},{7,6},{8,9},{9,8},{10,11... | collective-permute-start | bytes 786440 | tf_op jit(solution)/shard_map/ppermute | solution.py:591
  86.3 13.1 %collective-permute-start.31 = (bf16[8,64,512]{2,1,0:T(8,128)(2,1)}, bf16[8,64,512]{2,1,0:T(8,128)(2,1)S(1)}, u32[]{:S(2)}, u32[]{:S(2)}) collective-permute-start(bf16[8,64,512]{2,1,0:T(8,128)(2,1)} %get-tuple-element.45), channel_id=1, source_target_pairs={{0,1},{1,0},{2,3},{3,2},{4,5},{5,4},{6,7},{7,6},{8,9},{9,8},{10,11... | collective-permute-start | bytes 1572872 | tf_op jit(solution)/shard_map/ppermute | solution.py:591
  86.7 13.4 %collective-permute-start.32 = (bf16[8,64,512]{2,1,0:T(8,128)(2,1)}, bf16[8,64,512]{2,1,0:T(8,128)(2,1)S(1)}, u32[]{:S(2)}, u32[]{:S(2)}) collective-permute-start(bf16[8,64,512]{2,1,0:T(8,128)(2,1)} %get-tuple-element.47), channel_id=1, source_target_pairs={{0,1},{1,0},{2,3},{3,2},{4,5},{5,4},{6,7},{7,6},{8,9},{9,8},{10,11... | collective-permute-start | bytes 1572872 | tf_op jit(solution)/shard_map/ppermute | solution.py:591
  87.4 4.0 %collective-permute-start.48 = (f32[8848]{0:T(1024)S(1)}, f32[8848]{0:T(1024)S(1)}, u32[]{:S(2)}, u32[]{:S(2)}) collective-permute-start(f32[8848]{0:T(1024)S(1)} %fusion.24), channel_id=1, source_target_pairs={{0,2},{1,3},{2,0},{3,1},{4,6},{5,7},{6,4},{7,5},{8,10},{9,11},{10,... | collective-permute-start | bytes 106184 | tf_op jit(solution)/shard_map/ppermute | solution.py:591
  91.4 4.0 %collective-permute-start.49 = (f32[8848]{0:T(1024)S(1)}, f32[8848]{0:T(1024)S(1)}, u32[]{:S(2)}, u32[]{:S(2)}) collective-permute-start(f32[8848]{0:T(1024)S(1)} %add.159), channel_id=1, source_target_pairs={{0,4},{1,5},{2,6},{3,7},{4,0},{5,1},{6,2},{7,3},{8,12},{9,13},{10,... | collective-permute-start | bytes 106184 | tf_op jit(solution)/shard_map/ppermute | solution.py:591
  95.4 4.0 %collective-permute-start.50 = (f32[8848]{0:T(1024)S(1)}, f32[8848]{0:T(1024)S(1)}, u32[]{:S(2)}, u32[]{:S(2)}) collective-permute-start(f32[8848]{0:T(1024)S(1)} %add.160), channel_id=1, source_target_pairs={{0,8},{1,9},{2,10},{3,11},{4,12},{5,13},{6,14},{7,15},{8,0},{9,1},... | collective-permute-start | bytes 106184 | tf_op jit(solution)/shard_map/ppermute | solution.py:591
  95.9 6.9 %collective-permute-start.36 = (bf16[8,64,512]{2,1,0:T(8,128)(2,1)S(1)}, bf16[8,64,512]{2,1,0:T(8,128)(2,1)S(1)}, u32[]{:S(2)}, u32[]{:S(2)}) collective-permute-start(bf16[8,64,512]{2,1,0:T(8,128)(2,1)S(1)} %copy-done.39), channel_id=1, source_target_pairs={{0,1},{1,0},{2,3},{3,2},{4,5},{5,4},{6,7},{7,6},{8,9},{9,8},{10,11... | collective-permute-start | bytes 1572872 | tf_op jit(solution)/shard_map/ppermute | solution.py:591
  95.9 4.9 %collective-permute-start.37 = (bf16[8,64,512]{2,1,0:T(8,128)(2,1)S(1)}, bf16[8,64,512]{2,1,0:T(8,128)(2,1)S(1)}, u32[]{:S(2)}, u32[]{:S(2)}) collective-permute-start(bf16[8,64,512]{2,1,0:T(8,128)(2,1)S(1)} %copy-done.41), channel_id=1, source_target_pairs={{0,1},{1,0},{2,3},{3,2},{4,5},{5,4},{6,7},{7,6},{8,9},{9,8},{10,11... | collective-permute-start | bytes 1572872 | tf_op jit(solution)/shard_map/ppermute | solution.py:591
  99.4 4.1 %collective-permute-start.41 = (bf16[8,64,512]{2,1,0:T(8,128)(2,1)S(1)}, bf16[8,64,512]{2,1,0:T(8,128)(2,1)S(1)}, u32[]{:S(2)}, u32[]{:S(2)}) collective-permute-start(bf16[8,64,512]{2,1,0:T(8,128)(2,1)S(1)} %copy-done.38), channel_id=1, source_target_pairs={{0,1},{1,0},{2,3},{3,2},{4,5},{5,4},{6,7},{7,6},{8,9},{9,8},{10,11... | collective-permute-start | bytes 1572872 | tf_op jit(solution)/shard_map/ppermute | solution.py:591
  100.1 31.5 %collective-permute-start.51 = (f32[8848]{0:T(1024)S(1)}, f32[8848]{0:T(1024)S(1)}, u32[]{:S(2)}, u32[]{:S(2)}) collective-permute-start(f32[8848]{0:T(1024)S(1)} %add.161), channel_id=1, source_target_pairs={{0,16},{1,17},{2,18},{3,19},{4,20},{5,21},{6,22},{7,23},{8,24},{9,... | collective-permute-start | bytes 106184 | tf_op jit(solution)/shard_map/ppermute | solution.py:591
  100.8 13.6 %collective-permute-start.33 = (bf16[8,64,512]{2,1,0:T(8,128)(2,1)S(1)}, bf16[8,64,512]{2,1,0:T(8,128)(2,1)S(1)}, u32[]{:S(2)}, u32[]{:S(2)}) collective-permute-start(bf16[8,64,512]{2,1,0:T(8,128)(2,1)S(1)} %add_convert_fusion.4), channel_id=1, source_target_pairs={{0,2},{1,3},{2,0},{3,1},{4,6},{5,7},{6,4},{7,5},{8,10},{9,11},{10,... | collective-permute-start | bytes 1572872 | tf_op jit(solution)/shard_map/ppermute | solution.py:591
  102.0 14.0 %collective-permute-start.38 = (bf16[8,64,512]{2,1,0:T(8,128)(2,1)S(1)}, bf16[8,64,512]{2,1,0:T(8,128)(2,1)S(1)}, u32[]{:S(2)}, u32[]{:S(2)}) collective-permute-start(bf16[8,64,512]{2,1,0:T(8,128)(2,1)S(1)} %add_convert_fusion.2), channel_id=1, source_target_pairs={{0,4},{1,5},{2,6},{3,7},{4,0},{5,1},{6,2},{7,3},{8,12},{9,13},{10,... | collective-permute-start | bytes 1572872 | tf_op jit(solution)/shard_map/ppermute | solution.py:591
  102.7 13.9 %collective-permute-start.43 = (bf16[8,64,512]{2,1,0:T(8,128)(2,1)S(1)}, bf16[8,64,512]{2,1,0:T(8,128)(2,1)S(1)}, u32[]{:S(2)}, u32[]{:S(2)}) collective-permute-start(bf16[8,64,512]{2,1,0:T(8,128)(2,1)S(1)} %add_convert_fusion), channel_id=1, source_target_pairs={{0,8},{1,9},{2,10},{3,11},{4,12},{5,13},{6,14},{7,15},{8,0},{9,1},... | collective-permute-start | bytes 1572872 | tf_op jit(solution)/shard_map/ppermute | solution.py:591
  114.6 7.2 %collective-permute-start.34 = (bf16[4,64,512]{2,1,0:T(8,128)(2,1)S(1)}, bf16[4,64,512]{2,1,0:T(8,128)(2,1)S(1)}, u32[]{:S(2)}, u32[]{:S(2)}) collective-permute-start(bf16[4,64,512]{2,1,0:T(8,128)(2,1)S(1)} %get-tuple-element.67), channel_id=1, source_target_pairs={{0,4},{1,5},{2,6},{3,7},{4,0},{5,1},{6,2},{7,3},{8,12},{9,13},{10,... | collective-permute-start | bytes 786440 | tf_op jit(solution)/shard_map/ppermute | solution.py:591
  116.2 8.7 %collective-permute-start.39 = (bf16[4,64,512]{2,1,0:T(8,128)(2,1)S(1)}, bf16[4,64,512]{2,1,0:T(8,128)(2,1)S(1)}, u32[]{:S(2)}, u32[]{:S(2)}) collective-permute-start(bf16[4,64,512]{2,1,0:T(8,128)(2,1)S(1)} %get-tuple-element.69), channel_id=1, source_target_pairs={{0,8},{1,9},{2,10},{3,11},{4,12},{5,13},{6,14},{7,15},{8,0},{9,1},... | collective-permute-start | bytes 786440 | tf_op jit(solution)/shard_map/ppermute | solution.py:591
  116.8 8.2 %collective-permute-start.44 = (bf16[4,64,512]{2,1,0:T(8,128)(2,1)S(1)}, bf16[4,64,512]{2,1,0:T(8,128)(2,1)S(1)}, u32[]{:S(2)}, u32[]{:S(2)}) collective-permute-start(bf16[4,64,512]{2,1,0:T(8,128)(2,1)S(1)} %get-tuple-element.71), channel_id=1, source_target_pairs={{0,2},{1,3},{2,0},{3,1},{4,6},{5,7},{6,4},{7,5},{8,10},{9,11},{10,... | collective-permute-start | bytes 786440 | tf_op jit(solution)/shard_map/ppermute | solution.py:591
  121.8 5.0 %collective-permute-start.35 = (bf16[2,64,512]{2,1,0:T(8,128)(2,1)S(1)}, bf16[2,64,512]{2,1,0:T(8,128)(2,1)S(1)}, u32[]{:S(2)}, u32[]{:S(2)}) collective-permute-start(bf16[2,64,512]{2,1,0:T(8,128)(2,1)S(1)} %get-tuple-element.76), channel_id=1, source_target_pairs={{0,8},{1,9},{2,10},{3,11},{4,12},{5,13},{6,14},{7,15},{8,0},{9,1},... | collective-permute-start | bytes 393224 | tf_op jit(solution)/shard_map/ppermute | solution.py:591
  125.0 5.0 %collective-permute-start.40 = (bf16[2,64,512]{2,1,0:T(8,128)(2,1)S(1)}, bf16[2,64,512]{2,1,0:T(8,128)(2,1)S(1)}, u32[]{:S(2)}, u32[]{:S(2)}) collective-permute-start(bf16[2,64,512]{2,1,0:T(8,128)(2,1)S(1)} %get-tuple-element.78), channel_id=1, source_target_pairs={{0,2},{1,3},{2,0},{3,1},{4,6},{5,7},{6,4},{7,5},{8,10},{9,11},{10,... | collective-permute-start | bytes 393224 | tf_op jit(solution)/shard_map/ppermute | solution.py:591
  125.1 5.0 %collective-permute-start.45 = (bf16[2,64,512]{2,1,0:T(8,128)(2,1)S(1)}, bf16[2,64,512]{2,1,0:T(8,128)(2,1)S(1)}, u32[]{:S(2)}, u32[]{:S(2)}) collective-permute-start(bf16[2,64,512]{2,1,0:T(8,128)(2,1)S(1)} %get-tuple-element.80), channel_id=1, source_target_pairs={{0,4},{1,5},{2,6},{3,7},{4,0},{5,1},{6,2},{7,3},{8,12},{9,13},{10,... | collective-permute-start | bytes 393224 | tf_op jit(solution)/shard_map/ppermute | solution.py:591
  130.2 8.7 %collective-permute-start.46 = (bf16[3,64,512]{2,1,0:T(8,128)(2,1)S(1)}, bf16[3,64,512]{2,1,0:T(8,128)(2,1)S(1)}, u32[]{:S(2)}, u32[]{:S(2)}) collective-permute-start(bf16[3,64,512]{2,1,0:T(8,128)(2,1)S(1)} %pad_maximum_fusion.7), channel_id=1, source_target_pairs={{0,16},{1,17},{2,18},{3,19},{4,20},{5,21},{6,22},{7,23},{8,24},{9,... | collective-permute-start | bytes 589832 | tf_op jit(solution)/shard_map/ppermute | solution.py:591
  (47 other events, 508.6 us)

commit v3 on v2

--- a/solution.py
+++ b/solution.py
@@ -533,13 +533,17 @@
 def adam_shard(kinds, parts, weights, first, second, grad_scale):
     vmem = pl.BlockSpec(memory_space=pltpu.VMEM)
     size = weights.shape[0]
+    views = [
+        pltpu.with_memory_space_constraint(array.reshape(VIEW, 128), pltpu.VMEM)
+        for array in (weights, first, second)
+    ]
     results = pl.pallas_call(
         adam_kernel(grad_scale),
         in_specs=[pl.BlockSpec(memory_space=pltpu.SMEM)] + [vmem] * 5,
         out_specs=[vmem] * 4,
         out_shape=[jax.ShapeDtypeStruct((VIEW, 128), f32)] * 4,
         name="adam",
-    )(kinds, *parts, *(array.reshape(VIEW, 128) for array in (weights, first, second)))
+    )(kinds, *parts, *views)
     return [result.reshape(size) for result in results]
 
 

time: 142 us -> 142 us (level)
  no operation moved by 1% of the time
where the time goes in v3:
time: 142 us; the launch traced here: 141 us
  waiting for transfers between devices  68.3 us (48%)
  starting transfers between devices  34.3 us (24%)
  Pallas kernels  22.1 us (16%)
  local copies, waits for them, and re-layouts  7.13 us (5%)
  other arithmetic  4.75 us (3%)
  matrix products  3.36 us (2%)
  between operations  1.5 us (1%)
    ppermute x52, waiting for transfers between devices, swap(): return lax.ppermute(value, AXES, [(i, i ^ bit) for i in range(devices)])  68.3 us
    ppermute x52, starting transfers between devices, swap(): return lax.ppermute(value, AXES, [(i, i ^ bit) for i in range(devices)])  34.3 us
    pallas_call x1, Pallas kernels, run_layer(): pl.pallas_call(layer_kernel(counts, outs), in_specs=[smem, smem] + [vmem]...  17.9 us
  transfers between devices with their start and end apart: 52, of which 24 were waited for; matrix products, arithmetic and copies ran while one was open for 7% of the time, Pallas kernels for 0%

profile of v3, /device:TPU:0, one launch (start us, length us, event | category | flops | bytes accessed | tf_op | source)
XLA Modules:
  0.0 141.4 jit_solution(6132840510070313640)
XLA Ops:
  1.2 1.8 %pack.1 = bf16[3,64,512]{2,1,0:T(8,128)(2,1)} custom-call(s32[3]{0:T(128)} %compare_select_fusion.kinds, f32[768,128]{1,0:T(8,128)} %bitcast.25), custom_call_target="tpu_custom_call" | custom-call | tf_op jit(solution)/shard_map/pack/pallas_call | solution.py:485
  3.1 4.2 %collective-permute-start = (bf16[3,64,512]{2,1,0:T(8,128)(2,1)}, bf16[3,64,512]{2,1,0:T(8,128)(2,1)S(1)}, u32[]{:S(2)}, u32[]{:S(2)}) collective-permute-start(bf16[3,64,512]{2,1,0:T(8,128)(2,1)} %pack.1), channel_id=1, source_target_pairs={{0,16},{1,17},{2,18},{3,19},{4,20},{5,21},{6,22},{7,23},{8,24},{9,... | collective-permute-start | bytes 589832 | tf_op jit(solution)/shard_map/ppermute | solution.py:595
  7.2 0.9 fusion.27
  8.1 1.6 %collective-permute-start.11 = (bf16[1,64,512]{2,1,0:T(8,128)(2,1)S(1)}, bf16[1,64,512]{2,1,0:T(8,128)(2,1)S(1)}, u32[]{:S(2)}, u32[]{:S(2)}) collective-permute-start(bf16[1,64,512]{2,1,0:T(8,128)(2,1)S(1)} %get-tuple-element.90), channel_id=1, source_target_pairs={{0,4},{1,5},{2,6},{3,7},{4,0},{5,1},{6,2},{7,3},{8,12},{9,13},{10,... | collective-permute-start | bytes 196616 | tf_op jit(solution)/shard_map/ppermute | solution.py:595
  9.7 1.4 %collective-permute-start.6 = (bf16[1,64,512]{2,1,0:T(8,128)(2,1)S(1)}, bf16[1,64,512]{2,1,0:T(8,128)(2,1)S(1)}, u32[]{:S(2)}, u32[]{:S(2)}) collective-permute-start(bf16[1,64,512]{2,1,0:T(8,128)(2,1)S(1)} %get-tuple-element.91), channel_id=1, source_target_pairs={{0,2},{1,3},{2,0},{3,1},{4,6},{5,7},{6,4},{7,5},{8,10},{9,11},{10,... | collective-permute-start | bytes 196616 | tf_op jit(solution)/shard_map/ppermute | solution.py:595
  11.1 1.6 %collective-permute-start.1 = (bf16[1,64,512]{2,1,0:T(8,128)(2,1)S(1)}, bf16[1,64,512]{2,1,0:T(8,128)(2,1)S(1)}, u32[]{:S(2)}, u32[]{:S(2)}) collective-permute-start(bf16[1,64,512]{2,1,0:T(8,128)(2,1)S(1)} %get-tuple-element.92), channel_id=1, source_target_pairs={{0,8},{1,9},{2,10},{3,11},{4,12},{5,13},{6,14},{7,15},{8,0},{9,1},... | collective-permute-start | bytes 196616 | tf_op jit(solution)/shard_map/ppermute | solution.py:595
  12.7 0.7 slice.153
  13.4 0.8 reshape.104
  14.5 1.0 reduce-precision_convert_fusion.3
  15.4 0.8 compare_convert_fusion.refs_7_
  16.3 1.2 fusion.1
  18.8 0.9 reshape.103.refs_6_
  21.5 3.2 %collective-permute-done.2 = bf16[2,64,512]{2,1,0:T(8,128)(2,1)S(1)} collective-permute-done((bf16[2,64,512]{2,1,0:T(8,128)(2,1)S(1)}, bf16[2,64,512]{2,1,0:T(8,128)(2,1)S(1)}, u32[]{:S(2)}, u32[]{:S(2)}) %collective-permute-start.2) | collective-permute-done | bytes 131104 | tf_op jit(solution)/shard_map/ppermute | solution.py:595
  26.1 1.4 %collective-permute-start.26 = (bf16[1,64,512]{2,1,0:T(8,128)(2,1)S(1)}, bf16[1,64,512]{2,1,0:T(8,128)(2,1)S(1)}, u32[]{:S(2)}, u32[]{:S(2)}) collective-permute-start(bf16[1,64,512]{2,1,0:T(8,128)(2,1)S(1)} %get-tuple-element.87), channel_id=1, source_target_pairs={{0,4},{1,5},{2,6},{3,7},{4,0},{5,1},{6,2},{7,3},{8,12},{9,13},{10,... | collective-permute-start | bytes 196616 | tf_op jit(solution)/shard_map/ppermute | solution.py:595
  27.5 2.2 %collective-permute-done.16 = bf16[1,64,512]{2,1,0:T(8,128)(2,1)S(1)} collective-permute-done((bf16[1,64,512]{2,1,0:T(8,128)(2,1)S(1)}, bf16[1,64,512]{2,1,0:T(8,128)(2,1)S(1)}, u32[]{:S(2)}, u32[]{:S(2)}) %collective-permute-start.16) | collective-permute-done | bytes 65568 | tf_op jit(solution)/shard_map/ppermute | solution.py:595
  29.8 1.5 %collective-permute-start.21 = (bf16[1,64,512]{2,1,0:T(8,128)(2,1)S(1)}, bf16[1,64,512]{2,1,0:T(8,128)(2,1)S(1)}, u32[]{:S(2)}, u32[]{:S(2)}) collective-permute-start(bf16[1,64,512]{2,1,0:T(8,128)(2,1)S(1)} %get-tuple-element.88), channel_id=1, source_target_pairs={{0,2},{1,3},{2,0},{3,1},{4,6},{5,7},{6,4},{7,5},{8,10},{9,11},{10,... | collective-permute-start | bytes 196616 | tf_op jit(solution)/shard_map/ppermute | solution.py:595
  31.3 3.7 %collective-permute-done.21 = bf16[1,64,512]{2,1,0:T(8,128)(2,1)S(1)} collective-permute-done((bf16[1,64,512]{2,1,0:T(8,128)(2,1)S(1)}, bf16[1,64,512]{2,1,0:T(8,128)(2,1)S(1)}, u32[]{:S(2)}, u32[]{:S(2)}) %collective-permute-start.21) | collective-permute-done | bytes 65568 | tf_op jit(solution)/shard_map/ppermute | solution.py:595
  36.3 3.6 %collective-permute-done.17 = bf16[2,64,512]{2,1,0:T(8,128)(2,1)S(1)} collective-permute-done((bf16[2,64,512]{2,1,0:T(8,128)(2,1)S(1)}, bf16[2,64,512]{2,1,0:T(8,128)(2,1)S(1)}, u32[]{:S(2)}, u32[]{:S(2)}) %collective-permute-start.17) | collective-permute-done | bytes 131104 | tf_op jit(solution)/shard_map/ppermute | solution.py:595
  40.5 1.1 collective-permute-done.27
  41.6 1.5 %collective-permute-start.8 = (bf16[4,64,512]{2,1,0:T(8,128)(2,1)S(1)}, bf16[4,64,512]{2,1,0:T(8,128)(2,1)S(1)}, u32[]{:S(2)}, u32[]{:S(2)}) collective-permute-start(bf16[4,64,512]{2,1,0:T(8,128)(2,1)S(1)} %pad_maximum_fusion.1.refs_12_), channel_id=1, source_target_pairs={{0,4},{1,5},{2,6},{3,7},{4,0},{5,1},{6,2},{7,3},{8,12},{9,13},{10,... | collective-permute-start | bytes 786440 | tf_op jit(solution)/shard_map/ppermute | solution.py:595
  43.1 1.8 %collective-permute-done.22 = bf16[2,64,512]{2,1,0:T(8,128)(2,1)S(1)} collective-permute-done((bf16[2,64,512]{2,1,0:T(8,128)(2,1)S(1)}, bf16[2,64,512]{2,1,0:T(8,128)(2,1)S(1)}, u32[]{:S(2)}, u32[]{:S(2)}) %collective-permute-start.22) | collective-permute-done | bytes 131104 | tf_op jit(solution)/shard_map/ppermute | solution.py:595
  46.3 3.1 %collective-permute-done.8.refs_13_ = bf16[4,64,512]{2,1,0:T(8,128)(2,1)S(1)} collective-permute-done((bf16[4,64,512]{2,1,0:T(8,128)(2,1)S(1)}, bf16[4,64,512]{2,1,0:T(8,128)(2,1)S(1)}, u32[]{:S(2)}, u32[]{:S(2)}) %collective-permute-start.8) | collective-permute-done | bytes 262176 | tf_op jit(solution)/shard_map/ppermute | solution.py:595
  49.5 1.6 %collective-permute-start.23 = (bf16[4,64,512]{2,1,0:T(8,128)(2,1)S(1)}, bf16[4,64,512]{2,1,0:T(8,128)(2,1)S(1)}, u32[]{:S(2)}, u32[]{:S(2)}) collective-permute-start(bf16[4,64,512]{2,1,0:T(8,128)(2,1)S(1)} %pad_maximum_fusion.4.refs_24_), channel_id=1, source_target_pairs={{0,4},{1,5},{2,6},{3,7},{4,0},{5,1},{6,2},{7,3},{8,12},{9,13},{10,... | collective-permute-start | bytes 786440 | tf_op jit(solution)/shard_map/ppermute | solution.py:595
  51.0 2.6 %collective-permute-done.13.refs_17_ = bf16[4,64,512]{2,1,0:T(8,128)(2,1)S(1)} collective-permute-done((bf16[4,64,512]{2,1,0:T(8,128)(2,1)S(1)}, bf16[4,64,512]{2,1,0:T(8,128)(2,1)S(1)}, u32[]{:S(2)}, u32[]{:S(2)}) %collective-permute-start.13) | collective-permute-done | bytes 262176 | tf_op jit(solution)/shard_map/ppermute | solution.py:595
  54.7 3.5 %collective-permute-done.23.refs_25_ = bf16[4,64,512]{2,1,0:T(8,128)(2,1)S(1)} collective-permute-done((bf16[4,64,512]{2,1,0:T(8,128)(2,1)S(1)}, bf16[4,64,512]{2,1,0:T(8,128)(2,1)S(1)}, u32[]{:S(2)}, u32[]{:S(2)}) %collective-permute-start.23) | collective-permute-done | bytes 262176 | tf_op jit(solution)/shard_map/ppermute | solution.py:595
  58.7 3.7 %collective-permute-done.28.refs_29_ = bf16[4,64,512]{2,1,0:T(8,128)(2,1)S(1)} collective-permute-done((bf16[4,64,512]{2,1,0:T(8,128)(2,1)S(1)}, bf16[4,64,512]{2,1,0:T(8,128)(2,1)S(1)}, u32[]{:S(2)}, u32[]{:S(2)}) %collective-permute-start.28) | collective-permute-done | bytes 262176 | tf_op jit(solution)/shard_map/ppermute | solution.py:595
  62.9 1.0 collective-permute-done.25.refs_27_
  64.0 0.7 copy-done.31
  64.8 17.9 %layer.1 = (bf16[1,14,14,512]{3,2,1,0:T(8,128)(2,1)}, bf16[1,14,14,512]{3,2,1,0:T(8,128)(2,1)}, f32[12,512]{1,0:T(8,128)}, f32[64,1024]{1,0:T(8,128)}, bf16[8,64...) custom-call(s32[96]{0:T(128)} %get-tuple-element.36.refs_0_, ...), custom_call_target="tpu_custom_call" | custom-call | tf_op jit(solution)/shard_map/layer/pallas_call | solution.py:404
  82.7 0.8 reshape.109
  83.4 1.1 reshape.110
  84.7 0.8 fusion
  88.1 3.4 %collective-permute-done.48 = f32[8848]{0:T(1024)S(1)} collective-permute-done((f32[8848]{0:T(1024)S(1)}, f32[8848]{0:T(1024)S(1)}, u32[]{:S(2)}, u32[]{:S(2)}) %collective-permute-start.48) | collective-permute-done | bytes 35424 | tf_op jit(solution)/shard_map/ppermute | solution.py:595
  92.0 3.4 %collective-permute-done.49 = f32[8848]{0:T(1024)S(1)} collective-permute-done((f32[8848]{0:T(1024)S(1)}, f32[8848]{0:T(1024)S(1)}, u32[]{:S(2)}, u32[]{:S(2)}) %collective-permute-start.49) | collective-permute-done | bytes 35424 | tf_op jit(solution)/shard_map/ppermute | solution.py:595
  96.4 3.0 %collective-permute-done.50 = f32[8848]{0:T(1024)S(1)} collective-permute-done((f32[8848]{0:T(1024)S(1)}, f32[8848]{0:T(1024)S(1)}, u32[]{:S(2)}, u32[]{:S(2)}) %collective-permute-start.50) | collective-permute-done | bytes 35424 | tf_op jit(solution)/shard_map/ppermute | solution.py:595
  103.8 10.7 %collective-permute-done.33 = bf16[8,64,512]{2,1,0:T(8,128)(2,1)S(1)} collective-permute-done((bf16[8,64,512]{2,1,0:T(8,128)(2,1)S(1)}, bf16[8,64,512]{2,1,0:T(8,128)(2,1)S(1)}, u32[]{:S(2)}, u32[]{:S(2)}) %collective-permute-start.33) | collective-permute-done | bytes 524320 | tf_op jit(solution)/shard_map/ppermute | solution.py:595
  115.1 0.9 collective-permute-done.38
  116.8 1.3 collective-permute-start.44
  118.1 3.7 %collective-permute-done.34 = bf16[4,64,512]{2,1,0:T(8,128)(2,1)S(1)} collective-permute-done((bf16[4,64,512]{2,1,0:T(8,128)(2,1)S(1)}, bf16[4,64,512]{2,1,0:T(8,128)(2,1)S(1)}, u32[]{:S(2)}, u32[]{:S(2)}) %collective-permute-start.34) | collective-permute-done | bytes 262176 | tf_op jit(solution)/shard_map/ppermute | solution.py:595
  121.8 1.3 collective-permute-start.35
  123.1 1.8 %collective-permute-done.39 = bf16[4,64,512]{2,1,0:T(8,128)(2,1)S(1)} collective-permute-done((bf16[4,64,512]{2,1,0:T(8,128)(2,1)S(1)}, bf16[4,64,512]{2,1,0:T(8,128)(2,1)S(1)}, u32[]{:S(2)}, u32[]{:S(2)}) %collective-permute-start.39) | collective-permute-done | bytes 262176 | tf_op jit(solution)/shard_map/ppermute | solution.py:595
  125.2 0.7 collective-permute-start.45
  125.8 1.0 collective-permute-done.35
  126.9 3.1 %collective-permute-done.40 = bf16[2,64,512]{2,1,0:T(8,128)(2,1)S(1)} collective-permute-done((bf16[2,64,512]{2,1,0:T(8,128)(2,1)S(1)}, bf16[2,64,512]{2,1,0:T(8,128)(2,1)S(1)}, u32[]{:S(2)}, u32[]{:S(2)}) %collective-permute-start.40) | collective-permute-done | bytes 131104 | tf_op jit(solution)/shard_map/ppermute | solution.py:595
  130.3 1.4 %collective-permute-start.46 = (bf16[3,64,512]{2,1,0:T(8,128)(2,1)S(1)}, bf16[3,64,512]{2,1,0:T(8,128)(2,1)S(1)}, u32[]{:S(2)}, u32[]{:S(2)}) collective-permute-start(bf16[3,64,512]{2,1,0:T(8,128)(2,1)S(1)} %pad_maximum_fusion.7), channel_id=1, source_target_pairs={{0,16},{1,17},{2,18},{3,19},{4,20},{5,21},{6,22},{7,23},{8,24},{9,... | collective-permute-start | bytes 589832 | tf_op jit(solution)/shard_map/ppermute | solution.py:595
  131.7 0.7 multiply_subtract_fusion
  132.4 6.6 %collective-permute-done.46.refs_1_ = bf16[3,64,512]{2,1,0:T(8,128)(2,1)S(1)} collective-permute-done((bf16[3,64,512]{2,1,0:T(8,128)(2,1)S(1)}, bf16[3,64,512]{2,1,0:T(8,128)(2,1)S(1)}, u32[]{:S(2)}, u32[]{:S(2)}) %collective-permute-start.46) | collective-permute-done | bytes 196640 | tf_op jit(solution)/shard_map/ppermute | solution.py:595
  139.0 2.4 %adam.1 = (f32[768,128]{1,0:T(8,128)}, f32[768,128]{1,0:T(8,128)}, f32[768,128]{1,0:T(8,128)}, f32[768,128]{1,0:T(8,128)}) custom-call(s32[3]{0:T(128)} %compare_select_fusion.kinds, bf16[3,64,512]{2,1,0:T(8,128)(2,1)S(1)} %pad_maximum_fusion.6.refs_0_, bf16[3,64,512]{2,1,0:T(8,128)(2,1)S(1)} %collective-permute-done.46.refs_1_, f32[768,128]{1,0:T(8,128)S(1)} %bitcast.26, ...), custom_call_target="tpu_custom_call" | custom-call | tf_op jit(solution)/shard_map/adam/pallas_call | solution.py:540
  (211 shorter events, 21.1 us)
Async XLA Ops:
  3.1 22.4 %collective-permute-start = (bf16[3,64,512]{2,1,0:T(8,128)(2,1)}, bf16[3,64,512]{2,1,0:T(8,128)(2,1)S(1)}, u32[]{:S(2)}, u32[]{:S(2)}) collective-permute-start(bf16[3,64,512]{2,1,0:T(8,128)(2,1)} %pack.1), channel_id=1, source_target_pairs={{0,16},{1,17},{2,18},{3,19},{4,20},{5,21},{6,22},{7,23},{8,24},{9,... | collective-permute-start | bytes 589832 | tf_op jit(solution)/shard_map/ppermute | solution.py:595
  8.1 12.2 %collective-permute-start.11 = (bf16[1,64,512]{2,1,0:T(8,128)(2,1)S(1)}, bf16[1,64,512]{2,1,0:T(8,128)(2,1)S(1)}, u32[]{:S(2)}, u32[]{:S(2)}) collective-permute-start(bf16[1,64,512]{2,1,0:T(8,128)(2,1)S(1)} %get-tuple-element.90), channel_id=1, source_target_pairs={{0,4},{1,5},{2,6},{3,7},{4,0},{5,1},{6,2},{7,3},{8,12},{9,13},{10,... | collective-permute-start | bytes 196616 | tf_op jit(solution)/shard_map/ppermute | solution.py:595
  9.7 11.2 %collective-permute-start.6 = (bf16[1,64,512]{2,1,0:T(8,128)(2,1)S(1)}, bf16[1,64,512]{2,1,0:T(8,128)(2,1)S(1)}, u32[]{:S(2)}, u32[]{:S(2)}) collective-permute-start(bf16[1,64,512]{2,1,0:T(8,128)(2,1)S(1)} %get-tuple-element.91), channel_id=1, source_target_pairs={{0,2},{1,3},{2,0},{3,1},{4,6},{5,7},{6,4},{7,5},{8,10},{9,11},{10,... | collective-permute-start | bytes 196616 | tf_op jit(solution)/shard_map/ppermute | solution.py:595
  11.1 8.5 %collective-permute-start.1 = (bf16[1,64,512]{2,1,0:T(8,128)(2,1)S(1)}, bf16[1,64,512]{2,1,0:T(8,128)(2,1)S(1)}, u32[]{:S(2)}, u32[]{:S(2)}) collective-permute-start(bf16[1,64,512]{2,1,0:T(8,128)(2,1)S(1)} %get-tuple-element.92), channel_id=1, source_target_pairs={{0,8},{1,9},{2,10},{3,11},{4,12},{5,13},{6,14},{7,15},{8,0},{9,1},... | collective-permute-start | bytes 196616 | tf_op jit(solution)/shard_map/ppermute | solution.py:595
  19.7 5.0 %collective-permute-start.2 = (bf16[2,64,512]{2,1,0:T(8,128)(2,1)S(1)}, bf16[2,64,512]{2,1,0:T(8,128)(2,1)S(1)}, u32[]{:S(2)}, u32[]{:S(2)}) collective-permute-start(bf16[2,64,512]{2,1,0:T(8,128)(2,1)S(1)} %pad_maximum_fusion.8), channel_id=1, source_target_pairs={{0,4},{1,5},{2,6},{3,7},{4,0},{5,1},{6,2},{7,3},{8,12},{9,13},{10,... | collective-permute-start | bytes 393224 | tf_op jit(solution)/shard_map/ppermute | solution.py:595
  20.3 15.3 %collective-permute-start.12 = (bf16[2,64,512]{2,1,0:T(8,128)(2,1)S(1)}, bf16[2,64,512]{2,1,0:T(8,128)(2,1)S(1)}, u32[]{:S(2)}, u32[]{:S(2)}) collective-permute-start(bf16[2,64,512]{2,1,0:T(8,128)(2,1)S(1)} %pad_maximum_fusion.10), channel_id=1, source_target_pairs={{0,2},{1,3},{2,0},{3,1},{4,6},{5,7},{6,4},{7,5},{8,10},{9,11},{10,... | collective-permute-start | bytes 393224 | tf_op jit(solution)/shard_map/ppermute | solution.py:595
  20.9 5.1 %collective-permute-start.7 = (bf16[2,64,512]{2,1,0:T(8,128)(2,1)S(1)}, bf16[2,64,512]{2,1,0:T(8,128)(2,1)S(1)}, u32[]{:S(2)}, u32[]{:S(2)}) collective-permute-start(bf16[2,64,512]{2,1,0:T(8,128)(2,1)S(1)} %pad_maximum_fusion.9), channel_id=1, source_target_pairs={{0,8},{1,9},{2,10},{3,11},{4,12},{5,13},{6,14},{7,15},{8,0},{9,1},... | collective-permute-start | bytes 393224 | tf_op jit(solution)/shard_map/ppermute | solution.py:595
  24.8 20.1 %collective-permute-start.4 = (bf16[4,64,512]{2,1,0:T(8,128)(2,1)S(1)}, bf16[4,64,512]{2,1,0:T(8,128)(2,1)S(1)}, u32[]{:S(2)}, u32[]{:S(2)}) collective-permute-start(bf16[4,64,512]{2,1,0:T(8,128)(2,1)S(1)} %pad_maximum_fusion.refs_8_), channel_id=1, source_target_pairs={{0,1},{1,0},{2,3},{3,2},{4,5},{5,4},{6,7},{7,6},{8,9},{9,8},{10,11... | collective-permute-start | bytes 786440 | tf_op jit(solution)/shard_map/ppermute | solution.py:595
  24.9 20.6 %collective-permute-start.3 = (bf16[4,64,512]{2,1,0:T(8,128)(2,1)S(1)}, bf16[4,64,512]{2,1,0:T(8,128)(2,1)S(1)}, u32[]{:S(2)}, u32[]{:S(2)}) collective-permute-start(bf16[4,64,512]{2,1,0:T(8,128)(2,1)S(1)} %pad_maximum_fusion.refs_8_), channel_id=1, source_target_pairs={{0,2},{1,3},{2,0},{3,1},{4,6},{5,7},{6,4},{7,5},{8,10},{9,11},{10,... | collective-permute-start | bytes 786440 | tf_op jit(solution)/shard_map/ppermute | solution.py:595
  25.4 4.3 %collective-permute-start.16 = (bf16[1,64,512]{2,1,0:T(8,128)(2,1)S(1)}, bf16[1,64,512]{2,1,0:T(8,128)(2,1)S(1)}, u32[]{:S(2)}, u32[]{:S(2)}) collective-permute-start(bf16[1,64,512]{2,1,0:T(8,128)(2,1)S(1)} %get-tuple-element.89), channel_id=1, source_target_pairs={{0,8},{1,9},{2,10},{3,11},{4,12},{5,13},{6,14},{7,15},{8,0},{9,1},... | collective-permute-start | bytes 196616 | tf_op jit(solution)/shard_map/ppermute | solution.py:595
  26.1 9.4 %collective-permute-start.26 = (bf16[1,64,512]{2,1,0:T(8,128)(2,1)S(1)}, bf16[1,64,512]{2,1,0:T(8,128)(2,1)S(1)}, u32[]{:S(2)}, u32[]{:S(2)}) collective-permute-start(bf16[1,64,512]{2,1,0:T(8,128)(2,1)S(1)} %get-tuple-element.87), channel_id=1, source_target_pairs={{0,4},{1,5},{2,6},{3,7},{4,0},{5,1},{6,2},{7,3},{8,12},{9,13},{10,... | collective-permute-start | bytes 196616 | tf_op jit(solution)/shard_map/ppermute | solution.py:595
  29.8 5.2 %collective-permute-start.21 = (bf16[1,64,512]{2,1,0:T(8,128)(2,1)S(1)}, bf16[1,64,512]{2,1,0:T(8,128)(2,1)S(1)}, u32[]{:S(2)}, u32[]{:S(2)}) collective-permute-start(bf16[1,64,512]{2,1,0:T(8,128)(2,1)S(1)} %get-tuple-element.88), channel_id=1, source_target_pairs={{0,2},{1,3},{2,0},{3,1},{4,6},{5,7},{6,4},{7,5},{8,10},{9,11},{10,... | collective-permute-start | bytes 196616 | tf_op jit(solution)/shard_map/ppermute | solution.py:595
  35.0 5.0 %collective-permute-start.17 = (bf16[2,64,512]{2,1,0:T(8,128)(2,1)S(1)}, bf16[2,64,512]{2,1,0:T(8,128)(2,1)S(1)}, u32[]{:S(2)}, u32[]{:S(2)}) collective-permute-start(bf16[2,64,512]{2,1,0:T(8,128)(2,1)S(1)} %pad_maximum_fusion.11), channel_id=1, source_target_pairs={{0,4},{1,5},{2,6},{3,7},{4,0},{5,1},{6,2},{7,3},{8,12},{9,13},{10,... | collective-permute-start | bytes 393224 | tf_op jit(solution)/shard_map/ppermute | solution.py:595
  35.5 10.1 %collective-permute-start.9 = (bf16[4,64,512]{2,1,0:T(8,128)(2,1)S(1)}, bf16[4,64,512]{2,1,0:T(8,128)(2,1)S(1)}, u32[]{:S(2)}, u32[]{:S(2)}) collective-permute-start(bf16[4,64,512]{2,1,0:T(8,128)(2,1)S(1)} %pad_maximum_fusion.1.refs_12_), channel_id=1, source_target_pairs={{0,1},{1,0},{2,3},{3,2},{4,5},{5,4},{6,7},{7,6},{8,9},{9,8},{10,11... | collective-permute-start | bytes 786440 | tf_op jit(solution)/shard_map/ppermute | solution.py:595
  35.6 6.0 %collective-permute-start.27 = (bf16[2,64,512]{2,1,0:T(8,128)(2,1)S(1)}, bf16[2,64,512]{2,1,0:T(8,128)(2,1)S(1)}, u32[]{:S(2)}, u32[]{:S(2)}) collective-permute-start(bf16[2,64,512]{2,1,0:T(8,128)(2,1)S(1)} %pad_maximum_fusion.13), channel_id=1, source_target_pairs={{0,2},{1,3},{2,0},{3,1},{4,6},{5,7},{6,4},{7,5},{8,10},{9,11},{10,... | collective-permute-start | bytes 393224 | tf_op jit(solution)/shard_map/ppermute | solution.py:595
  39.9 5.0 %collective-permute-start.22 = (bf16[2,64,512]{2,1,0:T(8,128)(2,1)S(1)}, bf16[2,64,512]{2,1,0:T(8,128)(2,1)S(1)}, u32[]{:S(2)}, u32[]{:S(2)}) collective-permute-start(bf16[2,64,512]{2,1,0:T(8,128)(2,1)S(1)} %pad_maximum_fusion.12), channel_id=1, source_target_pairs={{0,8},{1,9},{2,10},{3,11},{4,12},{5,13},{6,14},{7,15},{8,0},{9,1},... | collective-permute-start | bytes 393224 | tf_op jit(solution)/shard_map/ppermute | solution.py:595
  41.6 7.8 %collective-permute-start.8 = (bf16[4,64,512]{2,1,0:T(8,128)(2,1)S(1)}, bf16[4,64,512]{2,1,0:T(8,128)(2,1)S(1)}, u32[]{:S(2)}, u32[]{:S(2)}) collective-permute-start(bf16[4,64,512]{2,1,0:T(8,128)(2,1)S(1)} %pad_maximum_fusion.1.refs_12_), channel_id=1, source_target_pairs={{0,4},{1,5},{2,6},{3,7},{4,0},{5,1},{6,2},{7,3},{8,12},{9,13},{10,... | collective-permute-start | bytes 786440 | tf_op jit(solution)/shard_map/ppermute | solution.py:595
  44.9 4.5 %collective-permute-start.14 = (bf16[4,64,512]{2,1,0:T(8,128)(2,1)S(1)}, bf16[4,64,512]{2,1,0:T(8,128)(2,1)S(1)}, u32[]{:S(2)}, u32[]{:S(2)}) collective-permute-start(bf16[4,64,512]{2,1,0:T(8,128)(2,1)S(1)} %pad_maximum_fusion.2.refs_16_), channel_id=1, source_target_pairs={{0,1},{1,0},{2,3},{3,2},{4,5},{5,4},{6,7},{7,6},{8,9},{9,8},{10,11... | collective-permute-start | bytes 786440 | tf_op jit(solution)/shard_map/ppermute | solution.py:595
  44.9 8.7 %collective-permute-start.13 = (bf16[4,64,512]{2,1,0:T(8,128)(2,1)S(1)}, bf16[4,64,512]{2,1,0:T(8,128)(2,1)S(1)}, u32[]{:S(2)}, u32[]{:S(2)}) collective-permute-start(bf16[4,64,512]{2,1,0:T(8,128)(2,1)S(1)} %pad_maximum_fusion.2.refs_16_), channel_id=1, source_target_pairs={{0,8},{1,9},{2,10},{3,11},{4,12},{5,13},{6,14},{7,15},{8,0},{9,1},... | collective-permute-start | bytes 786440 | tf_op jit(solution)/shard_map/ppermute | solution.py:595
  45.4 8.2 %collective-permute-start.19 = (bf16[4,64,512]{2,1,0:T(8,128)(2,1)S(1)}, bf16[4,64,512]{2,1,0:T(8,128)(2,1)S(1)}, u32[]{:S(2)}, u32[]{:S(2)}) collective-permute-start(bf16[4,64,512]{2,1,0:T(8,128)(2,1)S(1)} %pad_maximum_fusion.3.refs_20_), channel_id=1, source_target_pairs={{0,1},{1,0},{2,3},{3,2},{4,5},{5,4},{6,7},{7,6},{8,9},{9,8},{10,11... | collective-permute-start | bytes 786440 | tf_op jit(solution)/shard_map/ppermute | solution.py:595
  45.6 8.6 %collective-permute-start.18 = (bf16[4,64,512]{2,1,0:T(8,128)(2,1)S(1)}, bf16[4,64,512]{2,1,0:T(8,128)(2,1)S(1)}, u32[]{:S(2)}, u32[]{:S(2)}) collective-permute-start(bf16[4,64,512]{2,1,0:T(8,128)(2,1)S(1)} %pad_maximum_fusion.3.refs_20_), channel_id=1, source_target_pairs={{0,2},{1,3},{2,0},{3,1},{4,6},{5,7},{6,4},{7,5},{8,10},{9,11},{10,... | collective-permute-start | bytes 786440 | tf_op jit(solution)/shard_map/ppermute | solution.py:595
  49.4 4.9 %collective-permute-start.24 = (bf16[4,64,512]{2,1,0:T(8,128)(2,1)S(1)}, bf16[4,64,512]{2,1,0:T(8,128)(2,1)S(1)}, u32[]{:S(2)}, u32[]{:S(2)}) collective-permute-start(bf16[4,64,512]{2,1,0:T(8,128)(2,1)S(1)} %pad_maximum_fusion.4.refs_24_), channel_id=1, source_target_pairs={{0,1},{1,0},{2,3},{3,2},{4,5},{5,4},{6,7},{7,6},{8,9},{9,8},{10,11... | collective-permute-start | bytes 786440 | tf_op jit(solution)/shard_map/ppermute | solution.py:595
  49.5 8.7 %collective-permute-start.23 = (bf16[4,64,512]{2,1,0:T(8,128)(2,1)S(1)}, bf16[4,64,512]{2,1,0:T(8,128)(2,1)S(1)}, u32[]{:S(2)}, u32[]{:S(2)}) collective-permute-start(bf16[4,64,512]{2,1,0:T(8,128)(2,1)S(1)} %pad_maximum_fusion.4.refs_24_), channel_id=1, source_target_pairs={{0,4},{1,5},{2,6},{3,7},{4,0},{5,1},{6,2},{7,3},{8,12},{9,13},{10,... | collective-permute-start | bytes 786440 | tf_op jit(solution)/shard_map/ppermute | solution.py:595
  53.6 4.5 %collective-permute-start.29 = (bf16[4,64,512]{2,1,0:T(8,128)(2,1)S(1)}, bf16[4,64,512]{2,1,0:T(8,128)(2,1)S(1)}, u32[]{:S(2)}, u32[]{:S(2)}) collective-permute-start(bf16[4,64,512]{2,1,0:T(8,128)(2,1)S(1)} %pad_maximum_fusion.5.refs_28_), channel_id=1, source_target_pairs={{0,1},{1,0},{2,3},{3,2},{4,5},{5,4},{6,7},{7,6},{8,9},{9,8},{10,11... | collective-permute-start | bytes 786440 | tf_op jit(solution)/shard_map/ppermute | solution.py:595
  53.7 8.7 %collective-permute-start.28 = (bf16[4,64,512]{2,1,0:T(8,128)(2,1)S(1)}, bf16[4,64,512]{2,1,0:T(8,128)(2,1)S(1)}, u32[]{:S(2)}, u32[]{:S(2)}) collective-permute-start(bf16[4,64,512]{2,1,0:T(8,128)(2,1)S(1)} %pad_maximum_fusion.5.refs_28_), channel_id=1, source_target_pairs={{0,8},{1,9},{2,10},{3,11},{4,12},{5,13},{6,14},{7,15},{8,0},{9,1},... | collective-permute-start | bytes 786440 | tf_op jit(solution)/shard_map/ppermute | solution.py:595
  54.2 8.2 %collective-permute-start.5 = (bf16[4,64,512]{2,1,0:T(8,128)(2,1)S(1)}, bf16[4,64,512]{2,1,0:T(8,128)(2,1)S(1)}, u32[]{:S(2)}, u32[]{:S(2)}) collective-permute-start(bf16[4,64,512]{2,1,0:T(8,128)(2,1)S(1)} %collective-permute-done.3.refs_9_), channel_id=1, source_target_pairs={{0,1},{1,0},{2,3},{3,2},{4,5},{5,4},{6,7},{7,6},{8,9},{9,8},{10,11... | collective-permute-start | bytes 786440 | tf_op jit(solution)/shard_map/ppermute | solution.py:595
  54.3 8.6 %collective-permute-start.10 = (bf16[4,64,512]{2,1,0:T(8,128)(2,1)S(1)}, bf16[4,64,512]{2,1,0:T(8,128)(2,1)S(1)}, u32[]{:S(2)}, u32[]{:S(2)}) collective-permute-start(bf16[4,64,512]{2,1,0:T(8,128)(2,1)S(1)} %collective-permute-done.8.refs_13_), channel_id=1, source_target_pairs={{0,1},{1,0},{2,3},{3,2},{4,5},{5,4},{6,7},{7,6},{8,9},{9,8},{10,11... | collective-permute-start | bytes 786440 | tf_op jit(solution)/shard_map/ppermute | solution.py:595
  58.2 4.7 %collective-permute-start.15 = (bf16[4,64,512]{2,1,0:T(8,128)(2,1)S(1)}, bf16[4,64,512]{2,1,0:T(8,128)(2,1)S(1)}, u32[]{:S(2)}, u32[]{:S(2)}) collective-permute-start(bf16[4,64,512]{2,1,0:T(8,128)(2,1)S(1)} %collective-permute-done.13.refs_17_), channel_id=1, source_target_pairs={{0,1},{1,0},{2,3},{3,2},{4,5},{5,4},{6,7},{7,6},{8,9},{9,8},{10,11... | collective-permute-start | bytes 786440 | tf_op jit(solution)/shard_map/ppermute | solution.py:595
  58.2 4.7 %collective-permute-start.20 = (bf16[4,64,512]{2,1,0:T(8,128)(2,1)S(1)}, bf16[4,64,512]{2,1,0:T(8,128)(2,1)S(1)}, u32[]{:S(2)}, u32[]{:S(2)}) collective-permute-start(bf16[4,64,512]{2,1,0:T(8,128)(2,1)S(1)} %collective-permute-done.18.refs_21_), channel_id=1, source_target_pairs={{0,1},{1,0},{2,3},{3,2},{4,5},{5,4},{6,7},{7,6},{8,9},{9,8},{10,11... | collective-permute-start | bytes 786440 | tf_op jit(solution)/shard_map/ppermute | solution.py:595
  86.3 13.1 %collective-permute-start.31 = (bf16[8,64,512]{2,1,0:T(8,128)(2,1)}, bf16[8,64,512]{2,1,0:T(8,128)(2,1)S(1)}, u32[]{:S(2)}, u32[]{:S(2)}) collective-permute-start(bf16[8,64,512]{2,1,0:T(8,128)(2,1)} %get-tuple-element.45), channel_id=1, source_target_pairs={{0,1},{1,0},{2,3},{3,2},{4,5},{5,4},{6,7},{7,6},{8,9},{9,8},{10,11... | collective-permute-start | bytes 1572872 | tf_op jit(solution)/shard_map/ppermute | solution.py:595
  86.7 13.4 %collective-permute-start.32 = (bf16[8,64,512]{2,1,0:T(8,128)(2,1)}, bf16[8,64,512]{2,1,0:T(8,128)(2,1)S(1)}, u32[]{:S(2)}, u32[]{:S(2)}) collective-permute-start(bf16[8,64,512]{2,1,0:T(8,128)(2,1)} %get-tuple-element.47), channel_id=1, source_target_pairs={{0,1},{1,0},{2,3},{3,2},{4,5},{5,4},{6,7},{7,6},{8,9},{9,8},{10,11... | collective-permute-start | bytes 1572872 | tf_op jit(solution)/shard_map/ppermute | solution.py:595
  87.4 4.0 %collective-permute-start.48 = (f32[8848]{0:T(1024)S(1)}, f32[8848]{0:T(1024)S(1)}, u32[]{:S(2)}, u32[]{:S(2)}) collective-permute-start(f32[8848]{0:T(1024)S(1)} %fusion.24), channel_id=1, source_target_pairs={{0,2},{1,3},{2,0},{3,1},{4,6},{5,7},{6,4},{7,5},{8,10},{9,11},{10,... | collective-permute-start | bytes 106184 | tf_op jit(solution)/shard_map/ppermute | solution.py:595
  91.4 4.0 %collective-permute-start.49 = (f32[8848]{0:T(1024)S(1)}, f32[8848]{0:T(1024)S(1)}, u32[]{:S(2)}, u32[]{:S(2)}) collective-permute-start(f32[8848]{0:T(1024)S(1)} %add.159), channel_id=1, source_target_pairs={{0,4},{1,5},{2,6},{3,7},{4,0},{5,1},{6,2},{7,3},{8,12},{9,13},{10,... | collective-permute-start | bytes 106184 | tf_op jit(solution)/shard_map/ppermute | solution.py:595
  95.4 4.0 %collective-permute-start.50 = (f32[8848]{0:T(1024)S(1)}, f32[8848]{0:T(1024)S(1)}, u32[]{:S(2)}, u32[]{:S(2)}) collective-permute-start(f32[8848]{0:T(1024)S(1)} %add.160), channel_id=1, source_target_pairs={{0,8},{1,9},{2,10},{3,11},{4,12},{5,13},{6,14},{7,15},{8,0},{9,1},... | collective-permute-start | bytes 106184 | tf_op jit(solution)/shard_map/ppermute | solution.py:595
  95.9 6.9 %collective-permute-start.36 = (bf16[8,64,512]{2,1,0:T(8,128)(2,1)S(1)}, bf16[8,64,512]{2,1,0:T(8,128)(2,1)S(1)}, u32[]{:S(2)}, u32[]{:S(2)}) collective-permute-start(bf16[8,64,512]{2,1,0:T(8,128)(2,1)S(1)} %copy-done.42), channel_id=1, source_target_pairs={{0,1},{1,0},{2,3},{3,2},{4,5},{5,4},{6,7},{7,6},{8,9},{9,8},{10,11... | collective-permute-start | bytes 1572872 | tf_op jit(solution)/shard_map/ppermute | solution.py:595
  95.9 4.9 %collective-permute-start.37 = (bf16[8,64,512]{2,1,0:T(8,128)(2,1)S(1)}, bf16[8,64,512]{2,1,0:T(8,128)(2,1)S(1)}, u32[]{:S(2)}, u32[]{:S(2)}) collective-permute-start(bf16[8,64,512]{2,1,0:T(8,128)(2,1)S(1)} %copy-done.44), channel_id=1, source_target_pairs={{0,1},{1,0},{2,3},{3,2},{4,5},{5,4},{6,7},{7,6},{8,9},{9,8},{10,11... | collective-permute-start | bytes 1572872 | tf_op jit(solution)/shard_map/ppermute | solution.py:595
  99.4 4.1 %collective-permute-start.41 = (bf16[8,64,512]{2,1,0:T(8,128)(2,1)S(1)}, bf16[8,64,512]{2,1,0:T(8,128)(2,1)S(1)}, u32[]{:S(2)}, u32[]{:S(2)}) collective-permute-start(bf16[8,64,512]{2,1,0:T(8,128)(2,1)S(1)} %copy-done.41), channel_id=1, source_target_pairs={{0,1},{1,0},{2,3},{3,2},{4,5},{5,4},{6,7},{7,6},{8,9},{9,8},{10,11... | collective-permute-start | bytes 1572872 | tf_op jit(solution)/shard_map/ppermute | solution.py:595
  100.1 31.6 %collective-permute-start.51 = (f32[8848]{0:T(1024)S(1)}, f32[8848]{0:T(1024)S(1)}, u32[]{:S(2)}, u32[]{:S(2)}) collective-permute-start(f32[8848]{0:T(1024)S(1)} %add.161), channel_id=1, source_target_pairs={{0,16},{1,17},{2,18},{3,19},{4,20},{5,21},{6,22},{7,23},{8,24},{9,... | collective-permute-start | bytes 106184 | tf_op jit(solution)/shard_map/ppermute | solution.py:595
  100.8 13.6 %collective-permute-start.33 = (bf16[8,64,512]{2,1,0:T(8,128)(2,1)S(1)}, bf16[8,64,512]{2,1,0:T(8,128)(2,1)S(1)}, u32[]{:S(2)}, u32[]{:S(2)}) collective-permute-start(bf16[8,64,512]{2,1,0:T(8,128)(2,1)S(1)} %add_convert_fusion.4), channel_id=1, source_target_pairs={{0,2},{1,3},{2,0},{3,1},{4,6},{5,7},{6,4},{7,5},{8,10},{9,11},{10,... | collective-permute-start | bytes 1572872 | tf_op jit(solution)/shard_map/ppermute | solution.py:595
  102.0 14.0 %collective-permute-start.38 = (bf16[8,64,512]{2,1,0:T(8,128)(2,1)S(1)}, bf16[8,64,512]{2,1,0:T(8,128)(2,1)S(1)}, u32[]{:S(2)}, u32[]{:S(2)}) collective-permute-start(bf16[8,64,512]{2,1,0:T(8,128)(2,1)S(1)} %add_convert_fusion.2), channel_id=1, source_target_pairs={{0,4},{1,5},{2,6},{3,7},{4,0},{5,1},{6,2},{7,3},{8,12},{9,13},{10,... | collective-permute-start | bytes 1572872 | tf_op jit(solution)/shard_map/ppermute | solution.py:595
  102.7 13.9 %collective-permute-start.43 = (bf16[8,64,512]{2,1,0:T(8,128)(2,1)S(1)}, bf16[8,64,512]{2,1,0:T(8,128)(2,1)S(1)}, u32[]{:S(2)}, u32[]{:S(2)}) collective-permute-start(bf16[8,64,512]{2,1,0:T(8,128)(2,1)S(1)} %add_convert_fusion), channel_id=1, source_target_pairs={{0,8},{1,9},{2,10},{3,11},{4,12},{5,13},{6,14},{7,15},{8,0},{9,1},... | collective-permute-start | bytes 1572872 | tf_op jit(solution)/shard_map/ppermute | solution.py:595
  114.6 7.2 %collective-permute-start.34 = (bf16[4,64,512]{2,1,0:T(8,128)(2,1)S(1)}, bf16[4,64,512]{2,1,0:T(8,128)(2,1)S(1)}, u32[]{:S(2)}, u32[]{:S(2)}) collective-permute-start(bf16[4,64,512]{2,1,0:T(8,128)(2,1)S(1)} %get-tuple-element.67), channel_id=1, source_target_pairs={{0,4},{1,5},{2,6},{3,7},{4,0},{5,1},{6,2},{7,3},{8,12},{9,13},{10,... | collective-permute-start | bytes 786440 | tf_op jit(solution)/shard_map/ppermute | solution.py:595
  116.1 8.7 %collective-permute-start.39 = (bf16[4,64,512]{2,1,0:T(8,128)(2,1)S(1)}, bf16[4,64,512]{2,1,0:T(8,128)(2,1)S(1)}, u32[]{:S(2)}, u32[]{:S(2)}) collective-permute-start(bf16[4,64,512]{2,1,0:T(8,128)(2,1)S(1)} %get-tuple-element.69), channel_id=1, source_target_pairs={{0,8},{1,9},{2,10},{3,11},{4,12},{5,13},{6,14},{7,15},{8,0},{9,1},... | collective-permute-start | bytes 786440 | tf_op jit(solution)/shard_map/ppermute | solution.py:595
  116.8 8.3 %collective-permute-start.44 = (bf16[4,64,512]{2,1,0:T(8,128)(2,1)S(1)}, bf16[4,64,512]{2,1,0:T(8,128)(2,1)S(1)}, u32[]{:S(2)}, u32[]{:S(2)}) collective-permute-start(bf16[4,64,512]{2,1,0:T(8,128)(2,1)S(1)} %get-tuple-element.71), channel_id=1, source_target_pairs={{0,2},{1,3},{2,0},{3,1},{4,6},{5,7},{6,4},{7,5},{8,10},{9,11},{10,... | collective-permute-start | bytes 786440 | tf_op jit(solution)/shard_map/ppermute | solution.py:595
  121.8 5.0 %collective-permute-start.35 = (bf16[2,64,512]{2,1,0:T(8,128)(2,1)S(1)}, bf16[2,64,512]{2,1,0:T(8,128)(2,1)S(1)}, u32[]{:S(2)}, u32[]{:S(2)}) collective-permute-start(bf16[2,64,512]{2,1,0:T(8,128)(2,1)S(1)} %get-tuple-element.76), channel_id=1, source_target_pairs={{0,8},{1,9},{2,10},{3,11},{4,12},{5,13},{6,14},{7,15},{8,0},{9,1},... | collective-permute-start | bytes 393224 | tf_op jit(solution)/shard_map/ppermute | solution.py:595
  125.0 5.0 %collective-permute-start.40 = (bf16[2,64,512]{2,1,0:T(8,128)(2,1)S(1)}, bf16[2,64,512]{2,1,0:T(8,128)(2,1)S(1)}, u32[]{:S(2)}, u32[]{:S(2)}) collective-permute-start(bf16[2,64,512]{2,1,0:T(8,128)(2,1)S(1)} %get-tuple-element.78), channel_id=1, source_target_pairs={{0,2},{1,3},{2,0},{3,1},{4,6},{5,7},{6,4},{7,5},{8,10},{9,11},{10,... | collective-permute-start | bytes 393224 | tf_op jit(solution)/shard_map/ppermute | solution.py:595
  125.2 5.0 %collective-permute-start.45 = (bf16[2,64,512]{2,1,0:T(8,128)(2,1)S(1)}, bf16[2,64,512]{2,1,0:T(8,128)(2,1)S(1)}, u32[]{:S(2)}, u32[]{:S(2)}) collective-permute-start(bf16[2,64,512]{2,1,0:T(8,128)(2,1)S(1)} %get-tuple-element.80), channel_id=1, source_target_pairs={{0,4},{1,5},{2,6},{3,7},{4,0},{5,1},{6,2},{7,3},{8,12},{9,13},{10,... | collective-permute-start | bytes 393224 | tf_op jit(solution)/shard_map/ppermute | solution.py:595
  130.3 8.7 %collective-permute-start.46 = (bf16[3,64,512]{2,1,0:T(8,128)(2,1)S(1)}, bf16[3,64,512]{2,1,0:T(8,128)(2,1)S(1)}, u32[]{:S(2)}, u32[]{:S(2)}) collective-permute-start(bf16[3,64,512]{2,1,0:T(8,128)(2,1)S(1)} %pad_maximum_fusion.7), channel_id=1, source_target_pairs={{0,16},{1,17},{2,18},{3,19},{4,20},{5,21},{6,22},{7,23},{8,24},{9,... | collective-permute-start | bytes 589832 | tf_op jit(solution)/shard_map/ppermute | solution.py:595
  (50 other events, 550.8 us)
